TPU v7x, 256 devices: a whole 4x4x8 slice. The times are simulated.
256 devices in a mesh: guide: 2 (over core), row: 32 (over x, z), col: 4 (over y).
Axes of the slice: x: 4, y: 4, z: 8, core: 2. Of those that a mesh axis runs over, the one named last changes fastest.
Arguments:
- hidden: bfloat16 [2, 16, 2048], P('guide', None, 'row')
- lengths: int32 [2, 16], P('guide'), may hold values from 2 to 4096, as said below
- kv_cache: bfloat16 [2, 16, 2, 4096, 512], P('guide', None, None, 'row', 'col'), as said below
- attn_gain: bfloat16 [2048], P('row'), may hold values from 0.5 to 1.5
- w_query: bfloat16 [2048, 2048], P('row', 'col'), may hold values from -0.125 to 0.125
- w_key_value: bfloat16 [2048, 2, 512], P('row', None, 'col'), may hold values from -0.125 to 0.125
- w_out: bfloat16 [2048, 2048], P('col', 'row'), may hold values from -0.125 to 0.125
- mlp_gain: bfloat16 [2048], P('row'), may hold values from 0.5 to 1.5
- w_gate_up: bfloat16 [2048, 2, 8192], P('row', None, 'col'), may hold values from -0.125 to 0.125
- w_down: bfloat16 [8192, 2048], P('col', 'row'), may hold values from -0.0625 to 0.0625
- final_gain: bfloat16 [2048], P('row'), may hold values from 0.5 to 1.5
- w_head: bfloat16 [2048, 128256], P('row', 'col'), may hold values from -0.25 to 0.25
- next_gain: bfloat16 [2048], P('row'), may hold values from 0.5 to 1.5
- w_next_query: bfloat16 [2048, 2048], P('row', 'col'), may hold values from -0.125 to 0.125
- w_next_kv: bfloat16 [2048, 2, 512], P('row', None, 'col'), may hold values from -0.125 to 0.125
- tenant: int32 [16], replicated, may hold values from 0 to 3
- guide_scale: float32 [4], replicated, may hold values from 1.5 to 6
Outputs:
- guided_logits: float32 [16, 128256], P('guide', ('col', 'row'))
- next_query: bfloat16 [2, 16, 2048], P('guide', None, 'col')
- next_key_value: bfloat16 [2, 16, 2, 512], P('guide', None, None, 'col')
Inputs may be any that keep to these rules, and one draw needn't show every extreme that they name: `lengths`: in each group one request has exactly 4096 cached positions. `kv_cache`: keys (index 0 of the third dimension) are stored with the rotary embedding of their positions; values at index 1.
All inputs are finite; a program needn't handle non-finite values.
Results may differ from a plain program's by a relative error of at most 0.013.
Values may be sent and summed in bfloat16 or wider, within the bound.
No kernel may reach another device: no remote copies, remote signals or barrier semaphores. Data moves between devices by JAX's collectives and lax.ppermute only.
A program may use at most 64 MiB of HBM per device.

v0:
```python
import jax
import jax.numpy as jnp
from jax import lax
from jax.sharding import PartitionSpec as P

D = 2048
HEADS = 32
KVH = 8
HD = 64
TENANTS = 4


EPSILON = 1e-05
ROPE_BASE = 500000.0
NEGATIVE = -1e30


def joined(x, axis, combine):
    everything = jax.tree.map(lambda part: lax.all_gather(part, axis), x)
    first = jax.tree.map(lambda part: part[0], everything)

    def turn(k, so_far):
        return combine(so_far, jax.tree.map(lambda part: part[k], everything))

    return lax.fori_loop(1, lax.axis_size(axis), turn, first)


def partner_2(x, axis, apart):
    return lax.ppermute(x, axis, [(i, i ^ 1 << apart) for i in range(lax.axis_size(axis))])


def rotate(vectors, position):
    half_width = vectors.shape[-1] // 2
    frequency = ROPE_BASE ** (-2.0 * jnp.arange(half_width, dtype=jnp.float32) / vectors.shape[-1])
    angles = position.astype(jnp.float32)[:, None] * frequency[None, :]
    angles = angles.reshape((angles.shape[0],) + (1,) * (vectors.ndim - 2) + (half_width,))
    cosine = jnp.cos(angles)
    sines = jnp.sin(angles)
    first_half = vectors[..., :half_width]
    second_half = vectors[..., half_width:]
    return jnp.concatenate(
        [first_half * cosine - second_half * sines, second_half * cosine + first_half * sines],
        axis=-1,
    )


def squares(values):
    return jnp.sum(values * values, axis=1)


def join_parts(first, second):
    best_a, norm_a, weighted_a = first
    best_b, norm_b, weighted_b = second
    best = jnp.maximum(best_a, best_b)
    factor_a = jnp.exp(best_a - best)
    factor_b = jnp.exp(best_b - best)
    return (
        best,
        norm_a * factor_a + norm_b * factor_b,
        weighted_a * factor_a[..., None] + weighted_b * factor_b[..., None],
    )


def local(
    hidden,
    lengths,
    kv_cache,
    attn_gain,
    w_query,
    w_key_value,
    w_out,
    mlp_gain,
    w_gate_up,
    w_down,
    final_gain,
    w_head,
    next_gain,
    w_next_query,
    w_next_kv,
    tenant,
    guide_scale,
):
    x_rows = hidden[0]
    length = lengths[0]
    cache_block = kv_cache[0]
    requests = x_rows.shape[0]
    local_width = x_rows.shape[1]
    group_size = HEADS // KVH
    heads_here = w_key_value.shape[2] // HD
    x_float = x_rows.astype(jnp.float32)
    normed = (x_float * attn_gain.astype(jnp.float32)).astype(jnp.bfloat16)
    query_part = jnp.dot(normed, w_query, preferred_element_type=jnp.float32)
    pair_part = jnp.dot(
        normed, w_key_value.reshape(local_width, -1), preferred_element_type=jnp.float32
    )
    query_sum, pair_sum, first_squares = lax.psum((query_part, pair_part, squares(x_float)), "row")
    scaling = lax.rsqrt(first_squares / D + EPSILON)[:, None]
    query = rotate(
        (scaling * query_sum).reshape(requests, heads_here, group_size, HD), length
    ).astype(jnp.bfloat16)
    key_value = (scaling * pair_sum).reshape(requests, 2, heads_here, HD)
    new_key = rotate(key_value[:, 0], length).astype(jnp.bfloat16)
    new_value = key_value[:, 1].astype(jnp.bfloat16)
    cache_span = cache_block.shape[2]
    cache_keys = cache_block[:, 0].reshape(requests, cache_span, heads_here, HD)
    cache_values = cache_block[:, 1].reshape(requests, cache_span, heads_here, HD)
    inv_scale = HD ** (-0.5)
    scores = (
        jnp.einsum("bhgd,bshd->bhgs", query, cache_keys, preferred_element_type=jnp.float32)
        * inv_scale
    )
    positions = lax.axis_index("row") * cache_span + jnp.arange(cache_span, dtype=jnp.int32)
    usable = (positions[None, :] < length[:, None])[:, None, None, :]
    masked = jnp.where(usable, scores, NEGATIVE)
    local_best = jnp.max(masked, axis=-1)
    exp_terms = jnp.where(usable, jnp.exp(masked - local_best[..., None]), 0.0)
    local_norm = jnp.sum(exp_terms, axis=-1)
    local_weighted = jnp.einsum(
        "bhgs,bshd->bhgd",
        exp_terms.astype(jnp.bfloat16),
        cache_values,
        preferred_element_type=jnp.float32,
    )
    best, norm_sum, weighted = joined((local_best, local_norm, local_weighted), "row", join_parts)
    own_score = (
        jnp.einsum("bhgd,bhd->bhg", query, new_key, preferred_element_type=jnp.float32) * inv_scale
    )
    final_best = jnp.maximum(best, own_score)
    rescale = jnp.exp(best - final_best)
    own_exp = jnp.exp(own_score - final_best)
    norm_sum = norm_sum * rescale + own_exp
    weighted = weighted * rescale[..., None] + jnp.einsum(
        "bhg,bhd->bhgd", own_exp.astype(jnp.bfloat16), new_value, preferred_element_type=jnp.float32
    )
    attended = (weighted / norm_sum[..., None]).reshape(requests, -1).astype(jnp.bfloat16)
    out_part = jnp.dot(attended, w_out, preferred_element_type=jnp.float32)
    residual_one = (x_float + lax.psum(out_part, "col")).astype(jnp.bfloat16)
    one_float = residual_one.astype(jnp.float32)
    mlp_input = (one_float * mlp_gain.astype(jnp.float32)).astype(jnp.bfloat16)
    gate_part = jnp.dot(
        mlp_input, w_gate_up.reshape(local_width, -1), preferred_element_type=jnp.float32
    ).reshape(requests, 2, -1)
    gate_up, second_squares = lax.psum((gate_part, squares(one_float)), "row")
    mlp_scale = lax.rsqrt(second_squares / D + EPSILON)[:, None]
    activation = (jax.nn.silu(mlp_scale * gate_up[:, 0]) * (mlp_scale * gate_up[:, 1])).astype(
        jnp.bfloat16
    )
    down_part = jnp.dot(activation, w_down, preferred_element_type=jnp.float32)
    residual_two = (one_float + lax.psum(down_part, "col")).astype(jnp.bfloat16)
    two_float = residual_two.astype(jnp.float32)
    head_input = (two_float * final_gain.astype(jnp.float32)).astype(jnp.bfloat16)
    next_input = (two_float * next_gain.astype(jnp.float32)).astype(jnp.bfloat16)
    next_query_part = jnp.dot(next_input, w_next_query, preferred_element_type=jnp.float32)
    next_pair_part = jnp.dot(
        next_input, w_next_kv.reshape(local_width, -1), preferred_element_type=jnp.float32
    )
    next_query_sum, next_pair_sum, third_squares = lax.psum(
        (next_query_part, next_pair_part, squares(two_float)), "row"
    )
    out_scale = lax.rsqrt(third_squares / D + EPSILON)[:, None]
    next_query = (out_scale * next_query_sum).astype(jnp.bfloat16)[None]
    next_key_value = (out_scale * next_pair_sum).astype(jnp.bfloat16).reshape(1, requests, 2, -1)
    head_part = jnp.dot(head_input, w_head, preferred_element_type=jnp.float32)
    guidance = jnp.sum(
        jnp.where(
            tenant[:, None] == jnp.arange(TENANTS, dtype=jnp.int32)[None, :],
            guide_scale[None, :],
            0.0,
        ),
        axis=1,
    )
    guide_side = lax.axis_index("guide")
    half_rows = requests // 2
    own_logits = out_scale * lax.psum_scatter(head_part, "row", scatter_dimension=1, tiled=True)
    mine = lax.dynamic_slice_in_dim(own_logits, guide_side * half_rows, half_rows, 0)
    outgoing = lax.dynamic_slice_in_dim(own_logits, (1 - guide_side) * half_rows, half_rows, 0)
    partner = partner_2(outgoing, "guide", 0)
    conditional = jnp.where(guide_side == 0, mine, partner)
    unconditional = jnp.where(guide_side == 0, partner, mine)
    my_guidance = lax.dynamic_slice_in_dim(guidance, guide_side * half_rows, half_rows, 0)
    guided = unconditional + my_guidance[:, None] * (conditional - unconditional)
    return (guided, next_query, next_key_value)


def solution(mesh):
    placed = (
        P("guide", None, "row"),
        P("guide", None),
        P("guide", None, None, "row", "col"),
        P("row"),
        P("row", "col"),
        P("row", None, "col"),
        P("col", "row"),
        P("row"),
        P("row", None, "col"),
        P("col", "row"),
        P("row"),
        P("row", "col"),
        P("row"),
        P("row", "col"),
        P("row", None, "col"),
        P(),
        P(),
    )
    return jax.shard_map(
        local,
        mesh=mesh,
        in_specs=placed,
        out_specs=(
            P("guide", ("col", "row")),
            P("guide", None, "col"),
            P("guide", None, None, "col"),
        ),
        check_vma=False,
    )
```

profile of v0, /device:TPU:32, one launch (start us, length us, event | category | flops | bytes accessed | tf_op | source)
XLA Modules:
  0.0 620.4 jit_solution(462884868962780255)
XLA Ops:
  7.3 1.3 fusion.67
  9.4 140.2 %all-reduce.2 = (f32[16,512]{1,0:T(8,128)S(1)}, f32[16]{0:T(128)S(1)}, f32[16,256]{1,0:T(8,128)S(1)}) all-reduce(f32[16,512]{1,0:T(8,128)S(1)} %fusion.53, f32[16]{0:T(128)S(1)} %fusion.33, f32[16,256]{1,0:T(8,128)S(1)} %fusion.21), channel_id=1, replica_groups=mesh['guide'=2,'row'=32,'col'=4] {'row'}, use_global_device_ids=true, to_apply=%region_2.0 | all-reduce | flops 12304 | bytes 98432 | tf_op jit(solution)/shard_map/psum | solution.py:96
  152.0 51.8 %all-gather = f32[512,2,4]{2,1,0:T(2,128)S(1)} all-gather(f32[16,2,4]{2,1,0:T(2,128)S(1)} %get-tuple-element.244), channel_id=2, replica_groups=mesh['guide'=2,'row'=32,'col'=4] {'row'}, dimensions={0}, use_global_device_ids=true | all-gather | bytes 16896 | tf_op jit(solution)/shard_map/all_gather | solution.py:19
  204.1 46.2 %all-gather.1 = f32[512,2,4]{2,1,0:T(2,128)S(1)} all-gather(f32[16,2,4]{2,1,0:T(2,128)S(1)} %fusion.15), channel_id=3, replica_groups=mesh['guide'=2,'row'=32,'col'=4] {'row'}, dimensions={0}, use_global_device_ids=true | all-gather | bytes 16896 | tf_op jit(solution)/shard_map/all_gather | solution.py:19
  253.0 40.6 %while.19 = (s32[]{:T(128)}, f32[16,2,4]{0,2,1:T(4,128)S(1)}, f32[16,2,4]{0,2,1:T(4,128)S(1)}, f32[16,2,4,64]{3,2,1,0:T(4,128)S(1)}, f32[32,16,2,4]{1,3,2,0:T(4,...) while((s32[]{:T(128)}, f32[16,2,4]{0,2,1:T(4,128)S(1)}, ...), condition=%wide.region_6.7_spmd, body=%wide.region_5.6_spmd.sunk | while | flops 25349 | bytes 105623 | solution.py:25
  253.2 1.1 fusion.81
  255.8 1.1 fusion.81
  257.1 1.1 fusion.81
  259.8 1.1 fusion.81
  261.1 1.1 fusion.81
  263.7 1.1 fusion.81
  266.3 1.1 fusion.81
  267.6 1.1 fusion.81
  270.2 1.1 fusion.81
  271.5 1.1 fusion.81
  274.2 1.1 fusion.81
  275.5 1.1 fusion.81
  278.1 1.1 fusion.81
  280.7 1.1 fusion.81
  282.0 1.1 fusion.81
  284.6 1.1 fusion.81
  285.9 1.1 fusion.81
  288.6 1.1 fusion.81
  294.3 10.9 %psum.73 = f32[16,64]{1,0:T(8,128)S(1)} all-reduce(f32[16,64]{1,0:T(8,128)S(1)} %fusion.69), channel_id=1, replica_groups=mesh['guide'=2,'row'=32,'col'=4] {'col'}, use_global_device_ids=true, to_apply=%region_8.9 | all-reduce | flops 1024 | bytes 8192 | tf_op jit(solution)/shard_map/psum | solution.py:137
  305.3 1.1 fusion.4
  306.5 72.8 %psum.74 = f32[16]{0:T(128)S(1)} all-reduce(f32[16]{0:T(128)S(1)} %get-tuple-element.231), channel_id=1, replica_groups=mesh['guide'=2,'row'=32,'col'=4] {'row'}, use_global_device_ids=true, to_apply=%region_10.11 | all-reduce | flops 16 | bytes 128 | tf_op jit(solution)/shard_map/psum | solution.py:143
  379.3 66.7 %all-reduce.6.cloned.1.call-done = f32[16,2,2048]{2,0,1:T(8,128)} async-done(((f32[16,2,2048]{2,0,1:T(8,128)}), f32[16,2,2048]{2,0,1:T(8,128)}) %all-reduce.6.cloned.1.call-update) | async-done | bytes 262160 | tf_op jit(solution)/shard_map/psum | solution.py:143
  446.1 1.2 fusion.12
  447.3 10.6 %psum.76 = f32[16,64]{1,0:T(8,128)S(1)} all-reduce(f32[16,64]{1,0:T(8,128)S(1)} %fusion.12), channel_id=1, replica_groups=mesh['guide'=2,'row'=32,'col'=4] {'col'}, use_global_device_ids=true, to_apply=%region_12.13 | all-reduce | flops 1024 | bytes 8192 | tf_op jit(solution)/shard_map/psum | solution.py:149
  458.0 4.1 fusion.47
  464.4 136.7 %all-reduce.1 = (f32[16]{0:T(128)S(1)}, f32[16,512]{1,0:T(8,128)S(1)}, f32[16,256]{1,0:T(8,128)S(1)}) all-reduce(f32[16]{0:T(128)S(1)} %get-tuple-element.229, f32[16,512]{1,0:T(8,128)S(1)} %fusion.60, f32[16,256]{1,0:T(8,128)S(1)} %fusion.18), channel_id=1, replica_groups=mesh['guide'=2,'row'=32,'col'=4] {'row'}, use_global_device_ids=true, to_apply=%region_14.15 | all-reduce | flops 12304 | bytes 98432 | tf_op jit(solution)/shard_map/psum | solution.py:157
  601.8 9.1 %all-reduce.8.cloned.1.call-done = f32[16,32064]{1,0:T(8,128)} async-done(((f32[16,32064]{1,0:T(8,128)}), f32[16,32064]{1,0:T(8,128)}) %all-reduce.8.cloned.1.call-update) | async-done | bytes 2052112
  (205 shorter events, 32.9 us)
Async XLA Ops:
  7.2 438.9 %copy-start = (bf16[2048,64]{0,1:T(8,128)(2,1)S(1)}, bf16[2048,64]{0,1:T(8,128)(2,1)}, u32[]{:S(2)}) copy-start(bf16[2048,64]{0,1:T(8,128)(2,1)} %param.28) | copy-start | bytes 786436
  7.2 1.8 copy-start.9
  7.2 1.8 copy-start.5
  7.2 1.9 copy-start.2
  7.2 2.0 copy-start.6
  7.2 142.6 %copy-start.8 = (s32[1,16]{1,0:T(1,128)S(1)}, s32[1,16]{1,0:T(1,128)}, u32[]{:S(2)}) copy-start(s32[1,16]{1,0:T(1,128)} %param.20) | copy-start | bytes 196
  7.2 244.9 %all-gather.5.cloned.1.call-start = ((), (), s32[]{:S(2)}) async-start(), calls=%async_computation.1 | async-start | bytes 2162688 | tf_op jit(solution)/shard_map/all_gather | solution.py:19
  150.9 101.2 %copy-start.10 = (bf16[64]{0:T(256)(128)(2,1)S(1)}, bf16[64]{0:T(256)(128)(2,1)}, u32[]{:S(2)}) copy-start(bf16[64]{0:T(256)(128)(2,1)} %param.26) | copy-start | bytes 388
  152.0 294.1 %all-reduce.6.cloned.1.call-start = ((), (), s32[]{:S(2)}) async-start(), calls=%async_computation | async-start | bytes 524288 | tf_op jit(solution)/shard_map/psum | solution.py:143
  250.3 43.8 %copy-start.3 = (bf16[512,64]{0,1:T(8,128)(2,1)S(1)}, bf16[512,64]{0,1:T(8,128)(2,1)}, u32[]{:S(2)}) copy-start(bf16[512,64]{0,1:T(8,128)(2,1)} %param.25) | copy-start | bytes 196612
  250.3 54.9 %copy-start.1 = (bf16[64,2,2048]{2,1,0:T(2,128)(2,1)S(1)}, bf16[64,2,2048]{2,1,0:T(2,128)(2,1)}, u32[]{:S(2)}) copy-start(bf16[64,2,2048]{2,1,0:T(2,128)(2,1)} %param.27) | copy-start | bytes 1572868
  250.9 55.5 %copy-start.11 = (bf16[64]{0:T(256)(128)(2,1)S(1)}, bf16[64]{0:T(256)(128)(2,1)}, u32[]{:S(2)}) copy-start(bf16[64]{0:T(256)(128)(2,1)} %param.29) | copy-start | bytes 388
  306.4 304.5 %all-reduce.8.cloned.1.call-start = ((), (), s32[]{:S(2)}) async-start(), calls=%async_computation.2 | async-start | bytes 4112384
  458.0 4.2 copy-start.12
  462.1 0.7 copy-start.15
  462.1 1.9 copy-start.13
  462.1 1.9 copy-start.14
  462.1 2.1 copy-start.7
  462.1 2.2 copy-start.4
  611.9 1.3 collective-permute-start
Sparse Core Ops, SparseCore 0:
  152.1 76.1 all-gather.4
  306.5 139.4 all-reduce.5
  462.2 148.6 all-reduce.7
where the time goes:
time: 624 us; the launch traced here: 620 us
  blocking collectives  469 us (75%)
  waiting for transfers between devices  76.4 us (12%)
  other arithmetic  38 us (6%)
  between operations  14.8 us (2%)
  local copies, waits for them, and re-layouts  12.4 us (2%)
  matrix products  8.74 us (1%)
    psum x1, blocking collectives, local(): lax.psum((query_part, pair_part, squares(x_float)), 'row')  140 us
    psum x1, blocking collectives, local(): lax.psum((next_query_part, next_pair_part, squares(two_float)), 'row')  137 us
    all_gather x2, blocking collectives, joined(): everything = jax.tree.map(lambda part: lax.all_gather(part, axis), x)  98 us
    psum x1, blocking collectives, local(): gate_up, second_squares = lax.psum((gate_part, squares(one_float)), 'row')  72.8 us
    psum x1, waiting for transfers between devices, local(): gate_up, second_squares = lax.psum((gate_part, squares(one_float)), 'row')  66.7 us
    add x31, other arithmetic, join_parts(): weighted_a * factor_a[..., None] + weighted_b * factor_b[..., None]  33.2 us
  transfers between devices with their start and end apart: 4, of which 3 were waited for; matrix products, arithmetic and copies ran while one was open for 1% of the time, Pallas kernels for 0%

commit v1 on v0

v1 whole, which is shorter than its diff:
```python
import jax
import jax.numpy as jnp
from jax import lax
from jax.sharding import PartitionSpec as P

D = 2048
HEADS = 32
KVH = 8
HD = 64
TENANTS = 4
LANES = 128

EPSILON = 1e-05
ROPE_BASE = 500000.0
NEGATIVE = -1e30

F32 = jnp.float32
BF16 = jnp.bfloat16


def exchange(x, axis):
    return lax.all_to_all(x, axis, 0, 0, tiled=True)


def partner_2(x, axis, apart):
    return lax.ppermute(x, axis, [(i, i ^ 1 << apart) for i in range(lax.axis_size(axis))])


def rotate(vectors, position):
    half_width = vectors.shape[-1] // 2
    frequency = ROPE_BASE ** (-2.0 * jnp.arange(half_width, dtype=F32) / vectors.shape[-1])
    angles = position.astype(F32)[:, None] * frequency[None, :]
    angles = angles.reshape((angles.shape[0],) + (1,) * (vectors.ndim - 2) + (half_width,))
    cosine = jnp.cos(angles)
    sines = jnp.sin(angles)
    first_half = vectors[..., :half_width]
    second_half = vectors[..., half_width:]
    return jnp.concatenate(
        [first_half * cosine - second_half * sines, second_half * cosine + first_half * sines],
        axis=-1,
    )


def squares(values):
    return jnp.sum(values * values, axis=1)


def split(values, pieces):
    out = []
    rest = values
    for _ in range(pieces):
        piece = rest.astype(BF16)
        out.append(piece)
        rest = rest - piece.astype(F32)
    return out


def as_row(values):
    return jnp.pad(values, (0, LANES - values.shape[0]))[None, :]


def tiles(x):
    rows, width = x.shape
    return x.reshape(rows, width // LANES, LANES).transpose(1, 0, 2).reshape(-1, LANES)


def untiles(x, rows):
    return x.reshape(-1, rows, LANES).transpose(1, 0, 2).reshape(rows, -1)


def local(
    hidden,
    lengths,
    kv_cache,
    attn_gain,
    w_query,
    w_key_value,
    w_out,
    mlp_gain,
    w_gate_up,
    w_down,
    final_gain,
    w_head,
    next_gain,
    w_next_query,
    w_next_kv,
    tenant,
    guide_scale,
):
    x_rows = hidden[0]
    length = lengths[0]
    cache_block = kv_cache[0]
    requests = x_rows.shape[0]
    local_width = x_rows.shape[1]
    group_size = HEADS // KVH
    heads_here = w_key_value.shape[2] // HD
    peers = lax.axis_size("row")
    me = lax.axis_index("row")
    x_float = x_rows.astype(F32)
    normed = (x_float * attn_gain.astype(F32)).astype(BF16)
    query_part = jnp.dot(normed, w_query, preferred_element_type=F32)
    pair_part = jnp.dot(normed, w_key_value.reshape(local_width, -1), preferred_element_type=F32)
    own_part = (
        pair_part.astype(BF16)
        .reshape(requests, 2, heads_here, HD)
        .transpose(0, 2, 1, 3)
        .reshape(peers, 1, 2 * HD)
    )
    query_rows = tiles(query_part.astype(BF16))
    side = [as_row(piece) for piece in split(squares(x_float), 2)]
    shared = jnp.concatenate(side + [jnp.zeros((5, LANES), BF16)], axis=0)
    payload = jnp.concatenate(
        [
            jnp.broadcast_to(query_rows[None], (peers,) + query_rows.shape),
            own_part,
            jnp.broadcast_to(shared[None], (peers,) + shared.shape),
        ],
        axis=1,
    )
    total = jnp.sum(exchange(payload, "row").astype(F32), axis=0)
    depth = query_rows.shape[0]
    first_squares = total[depth + 1, :requests] + total[depth + 2, :requests]
    scaling = lax.rsqrt(first_squares / D + EPSILON)
    query = rotate(
        (scaling[:, None] * untiles(total[:depth], requests)).reshape(
            requests, heads_here, group_size, HD
        ),
        length,
    ).astype(BF16)
    own_request = me // heads_here
    own_head = me % heads_here
    own_pair = total[depth] * lax.dynamic_index_in_dim(scaling, own_request, 0, False)
    own_length = lax.dynamic_index_in_dim(length, own_request, 0, True)
    new_key = rotate(own_pair[None, :HD], own_length).astype(BF16)[0]
    new_value = own_pair[HD:].astype(BF16)
    cache_span = cache_block.shape[2]
    cache_keys = cache_block[:, 0].reshape(requests, cache_span, heads_here, HD)
    cache_values = cache_block[:, 1].reshape(requests, cache_span, heads_here, HD)
    inv_scale = HD ** (-0.5)
    scores = jnp.einsum("bhgd,bshd->bhgs", query, cache_keys, preferred_element_type=F32) * inv_scale
    positions = me * cache_span + jnp.arange(cache_span, dtype=jnp.int32)
    usable = (positions[None, :] < length[:, None])[:, None, None, :]
    mine_here = (
        (jnp.arange(requests) == own_request)[:, None] & (jnp.arange(heads_here) == own_head)[None, :]
    )[:, :, None]
    own_score = (
        jnp.sum(query.astype(F32) * new_key.astype(F32)[None, None, None, :], axis=-1) * inv_scale
    )
    masked = jnp.where(usable, scores, NEGATIVE)
    own_masked = jnp.where(mine_here, own_score, NEGATIVE)
    best = jnp.maximum(jnp.max(masked, axis=-1), own_masked)
    exp_terms = jnp.where(usable, jnp.exp(masked - best[..., None]), 0.0)
    own_exp = jnp.where(mine_here, jnp.exp(own_masked - best), 0.0)
    norm = jnp.sum(exp_terms, axis=-1) + own_exp
    weighted = jnp.einsum(
        "bhgs,bshd->bhgd", exp_terms.astype(BF16), cache_values, preferred_element_type=F32
    )
    weighted = weighted + own_exp.astype(BF16).astype(F32)[..., None] * new_value.astype(F32)
    average = weighted / jnp.where(norm > 0.0, norm, 1.0)[..., None]
    average_rows = tiles(average.reshape(requests, -1).astype(BF16))
    flat_heads = requests * heads_here * group_size
    side = [piece[None, :] for piece in split(best.reshape(flat_heads), 3)]
    side += [piece[None, :] for piece in split(norm.reshape(flat_heads), 2)]
    partial = jnp.concatenate([average_rows] + side + [jnp.zeros((3, LANES), BF16)], axis=0)
    parts = exchange(jnp.broadcast_to(partial[None], (peers,) + partial.shape), "row").astype(F32)
    bests = parts[:, depth] + (parts[:, depth + 1] + parts[:, depth + 2])
    norms = parts[:, depth + 3] + parts[:, depth + 4]
    factor = norms * jnp.exp(bests - jnp.max(bests, axis=0))
    factor = factor / jnp.sum(factor, axis=0)
    factor = jnp.repeat(factor.reshape(peers, requests, -1), HD, axis=2)
    factor = factor.reshape(peers, requests, -1, LANES).transpose(0, 2, 1, 3).reshape(peers, depth, LANES)
    attended = untiles(jnp.sum(parts[:, :depth] * factor, axis=0), requests).astype(BF16)
    out_part = jnp.dot(attended, w_out, preferred_element_type=F32)
    sides = lax.axis_size("col")
    out_sum = jnp.sum(
        exchange(jnp.broadcast_to(out_part[None], (sides,) + out_part.shape), "col"), axis=0
    )
    residual_one = (x_float + out_sum).astype(BF16)
    one_float = residual_one.astype(F32)
    mlp_input = (one_float * mlp_gain.astype(F32)).astype(BF16)
    gate_part = jnp.dot(
        mlp_input, w_gate_up.reshape(local_width, -1), preferred_element_type=F32
    ).astype(BF16)
    unit = w_gate_up.shape[2] // peers
    gate_rows = (
        gate_part.reshape(requests, 2, peers, unit)
        .transpose(2, 0, 1, 3)
        .reshape(peers, requests, 2 * unit)
    )
    side = jnp.concatenate(
        [as_row(piece) for piece in split(squares(one_float), 2)] + [jnp.zeros((6, LANES), BF16)],
        axis=0,
    )
    payload = jnp.concatenate(
        [gate_rows, jnp.broadcast_to(side[None], (peers,) + side.shape)], axis=1
    )
    total = jnp.sum(exchange(payload, "row").astype(F32), axis=0)
    second_squares = total[requests, :requests] + total[requests + 1, :requests]
    mlp_scale = lax.rsqrt(second_squares / D + EPSILON)[:, None]
    activation = (
        jax.nn.silu(mlp_scale * total[:requests, :unit]) * (mlp_scale * total[:requests, unit:])
    ).astype(BF16)
    units = exchange(jnp.broadcast_to(activation[None], (peers,) + activation.shape), "row")
    down_part = jnp.dot(
        units.transpose(1, 0, 2).reshape(requests, -1), w_down, preferred_element_type=F32
    )
    down_sum = jnp.sum(
        exchange(jnp.broadcast_to(down_part[None], (sides,) + down_part.shape), "col"), axis=0
    )
    residual_two = (one_float + down_sum).astype(BF16)
    guide_side = lax.axis_index("guide")
    other_two = partner_2(residual_two, "guide", 0)
    two_float = residual_two.astype(F32)
    groups = jnp.stack(
        [
            jnp.where(guide_side == 0, residual_two, other_two),
            jnp.where(guide_side == 0, other_two, residual_two),
        ]
    ).astype(F32)
    half_rows = requests // 2
    mine = lax.dynamic_slice_in_dim(groups, guide_side * half_rows, half_rows, 1)
    head_input = (mine * final_gain.astype(F32)).astype(BF16).reshape(requests, local_width)
    next_input = (two_float * next_gain.astype(F32)).astype(BF16)
    next_query_part = jnp.dot(next_input, w_next_query, preferred_element_type=F32)
    next_pair_part = jnp.dot(
        next_input, w_next_kv.reshape(local_width, -1), preferred_element_type=F32
    )
    query_width = next_query_part.shape[1]
    next_rows = tiles(
        jnp.concatenate([next_query_part, next_pair_part], axis=1).astype(BF16)
    ).reshape(peers, -1, LANES)
    chunk = next_rows.shape[1]
    both_squares = jnp.sum(groups * groups, axis=2).reshape(-1)
    side = jnp.concatenate(
        [as_row(piece) for piece in split(both_squares, 2)] + [jnp.zeros((6 - chunk, LANES), BF16)],
        axis=0,
    )
    payload = jnp.concatenate([next_rows, jnp.broadcast_to(side[None], (peers,) + side.shape)], axis=1)
    total = jnp.sum(exchange(payload, "row").astype(F32), axis=0)
    third_squares = (total[chunk] + total[chunk + 1])[: 2 * requests].reshape(2, requests)
    out_scale = lax.rsqrt(third_squares / D + EPSILON)
    guidance = jnp.sum(
        jnp.where(
            tenant[:, None] == jnp.arange(TENANTS, dtype=jnp.int32)[None, :],
            guide_scale[None, :],
            0.0,
        ),
        axis=1,
    )
    weights = jnp.stack([guidance, 1.0 - guidance]) * out_scale
    weights = lax.dynamic_slice_in_dim(weights, guide_side * half_rows, half_rows, 1)
    head_part = jnp.dot(head_input, w_head, preferred_element_type=F32)
    guided_part = (
        weights[0][:, None] * head_part[:half_rows] + weights[1][:, None] * head_part[half_rows:]
    ).astype(BF16)
    vocabulary = guided_part.shape[1]
    share = vocabulary // peers
    window = (share + 2 * LANES - 2) // LANES * LANES
    starts = [share * k // LANES * LANES for k in range(peers)]
    guided_part = jnp.pad(guided_part, ((0, 0), (0, max(0, starts[-1] + window - vocabulary))))
    pieces = jnp.stack([guided_part[:, start : start + window] for start in starts])
    next_piece = jnp.pad(total[:chunk].astype(BF16), ((0, half_rows - chunk), (0, 0)))
    payload = jnp.concatenate(
        [pieces, jnp.broadcast_to(next_piece[None], (peers,) + next_piece.shape)], axis=2
    )
    arrived = exchange(payload, "row")
    guided = jnp.sum(arrived[:, :, :window].astype(F32), axis=0)
    guided = lax.dynamic_slice_in_dim(guided, share * me % LANES, share, 1)
    next_all = untiles(arrived[:, :chunk, window:].reshape(-1, LANES), requests).astype(F32)
    own_scale = jnp.where(guide_side == 0, out_scale[0], out_scale[1])[:, None]
    next_all = (own_scale * next_all).astype(BF16)
    next_query = next_all[:, :query_width][None]
    next_key_value = next_all[:, query_width:].reshape(1, requests, 2, -1)
    return (guided, next_query, next_key_value)


def solution(mesh):
    placed = (
        P("guide", None, "row"),
        P("guide", None),
        P("guide", None, None, "row", "col"),
        P("row"),
        P("row", "col"),
        P("row", None, "col"),
        P("col", "row"),
        P("row"),
        P("row", None, "col"),
        P("col", "row"),
        P("row"),
        P("row", "col"),
        P("row"),
        P("row", "col"),
        P("row", None, "col"),
        P(),
        P(),
    )
    return jax.shard_map(
        local,
        mesh=mesh,
        in_specs=placed,
        out_specs=(
            P("guide", ("col", "row")),
            P("guide", None, "col"),
            P("guide", None, None, "col"),
        ),
        check_vma=False,
    )
```

time: 624 us -> 178 us (0.29)
  blocking collectives: 469 us -> 38.2 us
  starting transfers between devices: 0.21 us -> 32.5 us
  other arithmetic: 38 us -> 18 us
  between operations: 14.8 us -> 1.52 us
  waiting for transfers between devices: 76.4 us -> 63.5 us
    psum x5 -> x0, blocking collectives: 371 us -> none  [the longest x1 140 us: local(): lax.psum((query_part, pair_part, squares(x_float)), 'row')]
    all_gather x2 -> x0, blocking collectives: 98 us -> none  [joined(): everything = jax.tree.map(lambda part: lax.all_gather(part, axis), x)]
    psum x1 -> x0, waiting for transfers between devices: 66.7 us -> none  [local(): gate_up, second_squares = lax.psum((gate_part, squares(one_float)), 'row')]
    all_to_all x0 -> x6, waiting for transfers between devices: none -> 62.7 us  [exchange(): return lax.all_to_all(x, axis, 0, 0, tiled=True)]
    all_to_all x0 -> x2, blocking collectives: none -> 38.2 us  [exchange(): return lax.all_to_all(x, axis, 0, 0, tiled=True)]
    add x64 -> x2, other arithmetic: 34.7 us -> 0.01 us  [the longest x1 0.01 us: local(): total[chunk] + total[chunk + 1]]
    all_to_all x0 -> x6, starting transfers between devices: none -> 32.4 us  [exchange(): return lax.all_to_all(x, axis, 0, 0, tiled=True)]
    unnamed x4 -> x0, waiting for transfers between devices: 9.16 us -> none
  transfers between devices with their start and end apart: 4 -> 7, of which waited for: 3 -> 7; matrix products, arithmetic and copies ran while one was open for 1% -> 3% of each run, Pallas kernels for 0% -> 0%
where the time goes in v1:
time: 178 us; the launch traced here: 177 us
  waiting for transfers between devices  63.5 us (36%)
  blocking collectives  38.2 us (21%)
  starting transfers between devices  32.5 us (18%)
  other arithmetic  18 us (10%)
  local copies, waits for them, and re-layouts  17.5 us (10%)
  matrix products  6.27 us (4%)
    all_to_all x6, waiting for transfers between devices, exchange(): return lax.all_to_all(x, axis, 0, 0, tiled=True)  62.7 us
    all_to_all x2, blocking collectives, exchange(): return lax.all_to_all(x, axis, 0, 0, tiled=True)  38.2 us
    all_to_all x6, starting transfers between devices, exchange(): return lax.all_to_all(x, axis, 0, 0, tiled=True)  32.4 us
    unnamed x68, local copies, waits for them, and re-layouts  5.13 us
    reduce_sum x1, other arithmetic, local(): jnp.sum(parts[:, :depth] * factor, axis=0)  4.67 us
  transfers between devices with their start and end apart: 7, of which 7 were waited for; matrix products, arithmetic and copies ran while one was open for 3% of the time, Pallas kernels for 0%

profile of v1, /device:TPU:32, one launch (start us, length us, event | category | flops | bytes accessed | tf_op | source)
XLA Modules:
  0.0 177.5 jit_solution(17763787285954960845)
XLA Ops:
  0.7 0.9 fusion.38
  2.2 1.0 fusion.4
  3.2 0.9 convolution_convert_fusion.4
  4.6 0.9 pad_maximum_fusion.1
  5.5 11.2 %all-to-all-start = ((bf16[32,72,128]{2,1,0:T(8,128)(2,1)}), bf16[32,72,128]{2,1,0:T(8,128)(2,1)S(1)}, u32[]{:S(2)}, u32[]{:S(2)}) async-start(bf16[32,72,128]{2,1,0:T(8,128)(2,1)} %pad_maximum_fusion.1), calls=%async_computation | async-start | bytes 1179648 | tf_op jit(solution)/shard_map/all_to_all | solution.py:22
  18.6 17.1 %all-to-all-done = bf16[32,72,128]{2,1,0:T(8,128)(2,1)S(1)} async-done(((bf16[32,72,128]{2,1,0:T(8,128)(2,1)}), bf16[32,72,128]{2,1,0:T(8,128)(2,1)S(1)}, u32[]{:S(2)}, u32[]{:S(2)}) %all-to-all-start) | async-done | bytes 589856 | tf_op jit(solution)/shard_map/all_to_all | solution.py:22
  37.2 0.7 convert_bitcast_fusion.2
  40.3 22.9 %all_to_all.40 = bf16[32,72,128]{2,1,0:T(8,128)(2,1)S(1)} all-to-all(bf16[32,72,128]{2,1,0:T(8,128)(2,1)S(1)} %broadcast_in_dim.193), channel_id=1, replica_groups=mesh['guide'=2,'row'=32,'col'=4] {'row'}, dimensions={0} | all-to-all | bytes 1179648 | tf_op jit(solution)/shard_map/all_to_all | solution.py:22
  63.2 1.3 copy.73
  65.1 2.1 %copy-done.1 = f32[32,72,128]{0,2,1:T(8,128)} copy-done((f32[32,72,128]{0,2,1:T(8,128)}, f32[32,72,128]{0,2,1:T(8,128)S(1)}, u32[]{:S(2)}) %copy-start.1) | copy-done | bytes 1179672
  67.4 1.1 fusion.10
  68.6 1.0 fusion.13
  70.9 2.8 %copy.75 = f32[32,4,16,128]{0,3,2,1:T(8,128)} copy(f32[32,4,16,128]{3,1,2,0:T(4,128)S(1)} %bitcast.298) | data formatting | bytes 2097152 | tf_op jit(solution)/shard_map/transpose | solution.py:171
  73.7 4.7 %fusion = bf16[64,128]{1,0:T(8,128)(2,1)S(1)} fusion(f32[32,72,128]{0,2,1:T(8,128)} %copy-done.1, f32[32,4,16,128]{0,3,2,1:T(8,128)} %copy.75), kind=kLoop, calls=%fused_computation.2 | loop fusion | flops 516096 | bytes 2113536 | tf_op jit(solution)/shard_map/reduce_sum | solution.py:172
  78.5 0.7 reshape.614
  79.2 4.5 %all-to-all-start.2 = ((f32[4,1,1024]{2,1,0:T(1,128)}), f32[4,1,1024]{2,1,0:T(1,128)S(1)}, u32[]{:S(2)}, u32[]{:S(2)}) async-start(f32[4,1,1024]{2,1,0:T(1,128)} %reshape.614), calls=%async_computation.2 | async-start | bytes 32768 | tf_op jit(solution)/shard_map/all_to_all | solution.py:22
  84.0 5.1 %all-to-all-done.2 = f32[4,1,1024]{2,1,0:T(1,128)S(1)} async-done(((f32[4,1,1024]{2,1,0:T(1,128)}), f32[4,1,1024]{2,1,0:T(1,128)S(1)}, u32[]{:S(2)}, u32[]{:S(2)}) %all-to-all-start.2) | async-done | bytes 16416 | tf_op jit(solution)/shard_map/all_to_all | solution.py:22
  91.5 15.3 %all_to_all.41 = bf16[32,24,128]{2,1,0:T(8,128)(2,1)S(1)} all-to-all(bf16[32,24,128]{2,1,0:T(8,128)(2,1)S(1)} %pad_maximum_fusion.2), channel_id=1, replica_groups=mesh['guide'=2,'row'=32,'col'=4] {'row'}, dimensions={0} | all-to-all | bytes 393216 | tf_op jit(solution)/shard_map/all_to_all | solution.py:22
  106.9 0.8 reshape.616
  107.6 4.3 %all-to-all-start.4 = ((bf16[32,2,512]{2,1,0:T(2,128)(2,1)}), bf16[32,2,512]{2,1,0:T(2,128)(2,1)S(1)}, u32[]{:S(2)}, u32[]{:S(2)}) async-start(bf16[32,2,512]{2,1,0:T(2,128)(2,1)} %reshape.616), calls=%async_computation.4 | async-start | bytes 131072 | tf_op jit(solution)/shard_map/all_to_all | solution.py:22
  112.0 9.0 %all-to-all-done.4 = bf16[32,2,512]{2,1,0:T(2,128)(2,1)S(1)} async-done(((bf16[32,2,512]{2,1,0:T(2,128)(2,1)}), bf16[32,2,512]{2,1,0:T(2,128)(2,1)S(1)}, u32[]{:S(2)}, u32[]{:S(2)}) %all-to-all-start.4) | async-done | bytes 65568 | tf_op jit(solution)/shard_map/all_to_all | solution.py:22
  121.6 0.7 reshape.618
  122.3 3.3 %all-to-all-start.5 = ((f32[4,1,1024]{2,1,0:T(1,128)}), f32[4,1,1024]{2,1,0:T(1,128)S(1)}, u32[]{:S(2)}, u32[]{:S(2)}) async-start(f32[4,1,1024]{2,1,0:T(1,128)} %reshape.618), calls=%async_computation.5 | async-start | bytes 32768 | tf_op jit(solution)/shard_map/all_to_all | solution.py:22
  125.6 5.3 %all-to-all-done.5 = f32[4,1,1024]{2,1,0:T(1,128)S(1)} async-done(((f32[4,1,1024]{2,1,0:T(1,128)}), f32[4,1,1024]{2,1,0:T(1,128)S(1)}, u32[]{:S(2)}, u32[]{:S(2)}) %all-to-all-start.5) | async-done | bytes 16416 | tf_op jit(solution)/shard_map/all_to_all | solution.py:22
  132.2 0.8 collective-permute-done
  133.9 4.7 %all-to-all-start.6 = ((bf16[32,8,128]{2,1,0:T(8,128)(2,1)}), bf16[32,8,128]{2,1,0:T(8,128)(2,1)S(1)}, u32[]{:S(2)}, u32[]{:S(2)}) async-start(bf16[32,8,128]{2,1,0:T(8,128)(2,1)} %pad_maximum_fusion.3), calls=%async_computation.6 | async-start | bytes 131072 | tf_op jit(solution)/shard_map/all_to_all | solution.py:22
  138.5 2.8 %fusion.47 = f32[16,32064]{1,0:T(8,128)S(1)} fusion(bf16[64,32064]{1,0:T(8,128)(2,1)} %param.28, f32[2,16,64]{2,1,0:T(8,128)S(1)} %maximum_convert_fusion, s32[]{:T(128)S(6)} %select_n.153, f32[64]{0:T(128)S(1)} %convert_element_type.405), kind=kOutput, calls=%fused_computation.166 | convolution fusion | flops 65669120 | bytes 6164996 | tf_op jit(solution)/shard_map/dot_general | solution.py:252
  141.3 6.5 %all-to-all-done.6 = bf16[32,8,128]{2,1,0:T(8,128)(2,1)S(1)} async-done(((bf16[32,8,128]{2,1,0:T(8,128)(2,1)}), bf16[32,8,128]{2,1,0:T(8,128)(2,1)S(1)}, u32[]{:S(2)}, u32[]{:S(2)}) %all-to-all-start.6) | async-done | bytes 65568 | tf_op jit(solution)/shard_map/all_to_all | solution.py:22
  149.9 0.9 pad_maximum_fusion
  150.8 4.6 %all-to-all-start.7 = ((bf16[32,8,1280]{2,1,0:T(8,128)(2,1)}), bf16[32,8,1280]{2,1,0:T(8,128)(2,1)S(1)}, u32[]{:S(2)}, u32[]{:S(2)}) async-start(bf16[32,8,1280]{2,1,0:T(8,128)(2,1)} %pad_maximum_fusion), calls=%async_computation.7 | async-start | bytes 1310720 | tf_op jit(solution)/shard_map/all_to_all | solution.py:22
  155.5 19.8 %all-to-all-done.7 = bf16[32,8,1280]{2,1,0:T(8,128)(2,1)S(1)} async-done(((bf16[32,8,1280]{2,1,0:T(8,128)(2,1)}), bf16[32,8,1280]{2,1,0:T(8,128)(2,1)S(1)}, u32[]{:S(2)}, u32[]{:S(2)}) %all-to-all-start.7) | async-done | bytes 655392 | tf_op jit(solution)/shard_map/all_to_all | solution.py:22
  176.8 0.7 constant_dynamic-slice_fusion
  (196 shorter events, 18.0 us)
Async XLA Ops:
  0.6 120.8 %copy-start = (bf16[2048,64]{0,1:T(8,128)(2,1)S(1)}, bf16[2048,64]{0,1:T(8,128)(2,1)}, u32[]{:S(2)}) copy-start(bf16[2048,64]{0,1:T(8,128)(2,1)} %param.26) | copy-start | bytes 786436
  0.6 16.1 %copy-start.2 = (bf16[1,16,2,128,128]{4,3,2,1,0:T(8,128)(2,1)S(1)}, bf16[1,16,2,128,128]{4,3,2,1,0:T(8,128)(2,1)}, u32[]{:S(2)}) copy-start(bf16[1,16,2,128,128]{4,3,2,1,0:T(8,128)(2,1)} %param.19) | copy-start | bytes 3145732
  5.5 30.2 %all-to-all-start = ((bf16[32,72,128]{2,1,0:T(8,128)(2,1)}), bf16[32,72,128]{2,1,0:T(8,128)(2,1)S(1)}, u32[]{:S(2)}, u32[]{:S(2)}) async-start(bf16[32,72,128]{2,1,0:T(8,128)(2,1)} %pad_maximum_fusion.1), calls=%async_computation | async-start | bytes 1179648 | tf_op jit(solution)/shard_map/all_to_all | solution.py:22
  16.7 1.1 copy-start.8
  65.1 2.1 %copy-start.1 = (f32[32,72,128]{0,2,1:T(8,128)}, f32[32,72,128]{0,2,1:T(8,128)S(1)}, u32[]{:S(2)}) copy-start(f32[32,72,128]{0,2,1:T(8,128)S(1)} %convert_element_type.373) | copy-start | bytes 3538948
  73.7 4.7 %copy-start.5 = (bf16[512,64]{0,1:T(8,128)(2,1)S(1)}, bf16[512,64]{0,1:T(8,128)(2,1)}, u32[]{:S(2)}) copy-start(bf16[512,64]{0,1:T(8,128)(2,1)} %param.23) | copy-start | bytes 196612
  73.7 10.0 %copy-start.3 = (bf16[64,2,2048]{2,1,0:T(2,128)(2,1)S(1)}, bf16[64,2,2048]{2,1,0:T(2,128)(2,1)}, u32[]{:S(2)}) copy-start(bf16[64,2,2048]{2,1,0:T(2,128)(2,1)} %param.25) | copy-start | bytes 1572868
  73.7 10.2 %copy-start.10 = (bf16[64]{0:T(256)(128)(2,1)S(1)}, bf16[64]{0:T(256)(128)(2,1)}, u32[]{:S(2)}) copy-start(bf16[64]{0:T(256)(128)(2,1)} %param.24) | copy-start | bytes 388
  73.7 16.7 %copy-start.4 = (bf16[1,16,64]{2,1,0:T(8,128)(2,1)S(1)}, bf16[1,16,64]{2,1,0:T(8,128)(2,1)}, u32[]{:S(2)}) copy-start(bf16[1,16,64]{2,1,0:T(8,128)(2,1)} %param.17) | copy-start | bytes 6148
  79.2 9.8 %all-to-all-start.2 = ((f32[4,1,1024]{2,1,0:T(1,128)}), f32[4,1,1024]{2,1,0:T(1,128)S(1)}, u32[]{:S(2)}, u32[]{:S(2)}) async-start(f32[4,1,1024]{2,1,0:T(1,128)} %reshape.614), calls=%async_computation.2 | async-start | bytes 32768 | tf_op jit(solution)/shard_map/all_to_all | solution.py:22
  83.7 28.2 %copy-start.11 = (f32[4]{0:T(128)S(1)}, f32[4]{0:T(128)}, u32[]{:S(2)}) copy-start(f32[4]{0:T(128)} %param.33) | copy-start | bytes 52
  83.7 28.3 %copy-start.12 = (s32[16]{0:T(128)S(1)}, s32[16]{0:T(128)}, u32[]{:S(2)}) copy-start(s32[16]{0:T(128)} %param.32) | copy-start | bytes 196
  90.3 35.2 %copy-start.13 = (bf16[64]{0:T(256)(128)(2,1)S(1)}, bf16[64]{0:T(256)(128)(2,1)}, u32[]{:S(2)}) copy-start(bf16[64]{0:T(256)(128)(2,1)} %param.27) | copy-start | bytes 388
  90.3 35.3 %copy-start.14 = (bf16[64]{0:T(256)(128)(2,1)S(1)}, bf16[64]{0:T(256)(128)(2,1)}, u32[]{:S(2)}) copy-start(bf16[64]{0:T(256)(128)(2,1)} %param.29) | copy-start | bytes 388
  90.5 41.3 %copy-start.7 = (bf16[64,2,128]{2,1,0:T(2,128)(2,1)S(1)}, bf16[64,2,128]{2,1,0:T(2,128)(2,1)}, u32[]{:S(2)}) copy-start(bf16[64,2,128]{2,1,0:T(2,128)(2,1)} %param.31) | copy-start | bytes 98308
  90.5 41.4 %copy-start.6 = (bf16[64,512]{1,0:T(8,128)(2,1)S(1)}, bf16[64,512]{1,0:T(8,128)(2,1)}, u32[]{:S(2)}) copy-start(bf16[64,512]{1,0:T(8,128)(2,1)} %param.30) | copy-start | bytes 196612
  107.6 13.4 %all-to-all-start.4 = ((bf16[32,2,512]{2,1,0:T(2,128)(2,1)}), bf16[32,2,512]{2,1,0:T(2,128)(2,1)S(1)}, u32[]{:S(2)}, u32[]{:S(2)}) async-start(bf16[32,2,512]{2,1,0:T(2,128)(2,1)} %reshape.616), calls=%async_computation.4 | async-start | bytes 131072 | tf_op jit(solution)/shard_map/all_to_all | solution.py:22
  122.3 8.6 %all-to-all-start.5 = ((f32[4,1,1024]{2,1,0:T(1,128)}), f32[4,1,1024]{2,1,0:T(1,128)S(1)}, u32[]{:S(2)}, u32[]{:S(2)}) async-start(f32[4,1,1024]{2,1,0:T(1,128)} %reshape.618), calls=%async_computation.5 | async-start | bytes 32768 | tf_op jit(solution)/shard_map/all_to_all | solution.py:22
  131.7 1.3 collective-permute-start
  133.9 14.0 %all-to-all-start.6 = ((bf16[32,8,128]{2,1,0:T(8,128)(2,1)}), bf16[32,8,128]{2,1,0:T(8,128)(2,1)S(1)}, u32[]{:S(2)}, u32[]{:S(2)}) async-start(bf16[32,8,128]{2,1,0:T(8,128)(2,1)} %pad_maximum_fusion.3), calls=%async_computation.6 | async-start | bytes 131072 | tf_op jit(solution)/shard_map/all_to_all | solution.py:22
  141.3 8.5 %copy-start.9 = (pred[8]{0:T(512)(128)(4,1)S(1)}, pred[8]{0:T(512)(128)(4,1)}, u32[]{:S(2)}) copy-start(pred[8]{0:T(512)(128)(4,1)} %constant.101.clone.1) | copy-start | bytes 28
  150.8 24.5 %all-to-all-start.7 = ((bf16[32,8,1280]{2,1,0:T(8,128)(2,1)}), bf16[32,8,1280]{2,1,0:T(8,128)(2,1)S(1)}, u32[]{:S(2)}, u32[]{:S(2)}) async-start(bf16[32,8,1280]{2,1,0:T(8,128)(2,1)} %pad_maximum_fusion), calls=%async_computation.7 | async-start | bytes 1310720 | tf_op jit(solution)/shard_map/all_to_all | solution.py:22

commit v2 on v0

v2 whole, which is shorter than its diff:
```python
import functools

import jax
import jax.numpy as jnp
from jax import lax
from jax.experimental import pallas as pl
from jax.experimental.pallas import tpu as pltpu
from jax.sharding import PartitionSpec as P

D = 2048
HEADS = 32
KVH = 8
HD = 64
TENANTS = 4
LANES = 128
SUBLANES = 8

EPSILON = 1e-05
ROPE_BASE = 500000.0
NEGATIVE = -1e30

F32 = jnp.float32
BF16 = jnp.bfloat16
LANE_CONTRACT = (((1,), (1,)), ((), ()))


def exchange(x, axis):
    return lax.all_to_all(x, axis, 0, 0, tiled=True)


def partner_2(x, axis, apart):
    return lax.ppermute(x, axis, [(i, i ^ 1 << apart) for i in range(lax.axis_size(axis))])


def call(body, outs, *operands, scratch=(), scalars=0):
    specs = [pl.BlockSpec(memory_space=pltpu.SMEM)] * scalars
    specs += [pl.BlockSpec(memory_space=pltpu.VMEM)] * (len(operands) - scalars)
    out_specs = jax.tree.map(lambda _: pl.BlockSpec(memory_space=pltpu.VMEM), outs)
    return pl.pallas_call(
        body,
        out_shape=outs,
        in_specs=specs,
        out_specs=out_specs,
        scratch_shapes=list(scratch),
        compiler_params=pltpu.CompilerParams(vmem_limit_bytes=24 << 20),
    )(*operands)


def shape(dims, dtype):
    return jax.ShapeDtypeStruct(dims, dtype)


def index(dims, dim):
    return lax.broadcasted_iota(jnp.int32, dims, dim)


def low_lanes(rows):
    return index((rows, LANES), 1) < LANES // 2


def turned(x):
    return pltpu.roll(x, LANES // 2, 1)


def to_row(column, offset=0):
    n = column.shape[0]
    hit = index((n, LANES), 1) == index((n, LANES), 0) + offset
    return jnp.sum(jnp.where(hit, column, 0.0), axis=0, keepdims=True)


def to_column(row, n, offset=0):
    hit = index((n, LANES), 1) == index((n, LANES), 0) + offset
    return jnp.sum(jnp.where(hit, row, 0.0), axis=1, keepdims=True)


def halves(value):
    high = value.astype(BF16).astype(F32)
    return high, value - high


def block_of(rows):
    at = index((SUBLANES, LANES), 0)
    block = jnp.zeros((SUBLANES, LANES), F32)
    for k, row in enumerate(rows):
        block = jnp.where(at == k, row, block)
    return block


def summed(ref):
    total = ref[0].astype(F32)
    for k in range(1, ref.shape[0]):
        total = total + ref[k].astype(F32)
    return total


def norm_scale(total):
    return lax.rsqrt(total / D + EPSILON)


def spread(normed, which):
    width = normed.shape[1]
    dims = (width, 2 * width)
    pick = (index(dims, 1) == 2 * index(dims, 0) + which).astype(F32).astype(BF16)
    return jnp.dot(normed, pick, preferred_element_type=F32).astype(BF16)


def pair_dots(normed, pair_ref):
    weights = pair_ref[...]
    return [jnp.dot(spread(normed, w), weights, preferred_element_type=F32) for w in range(2)]


def start_kernel(x_ref, gain_ref, query_ref, pair_ref, out_ref):
    x = x_ref[...].astype(F32)
    requests = x.shape[0]
    normed = (x * gain_ref[...].astype(F32)).astype(BF16)
    query = jnp.dot(normed, query_ref[...], preferred_element_type=F32)
    tiles = query.shape[1] // LANES
    rows = jnp.concatenate(
        [query[:, j * LANES : (j + 1) * LANES] for j in range(tiles)], axis=0
    ).astype(BF16)
    keys, values = pair_dots(normed, pair_ref)
    low = low_lanes(requests)
    own = (jnp.where(low, keys, turned(values)), jnp.where(low, turned(keys), values))
    high_part, low_part = halves(to_row(jnp.sum(x * x, axis=1, keepdims=True)))
    depth = rows.shape[0]
    for peer in range(out_ref.shape[0]):
        request, head = divmod(peer, 2)
        side = block_of([own[head][request : request + 1], high_part, low_part])
        out_ref[peer, 0:depth] = rows
        out_ref[peer, depth : depth + SUBLANES] = side.astype(BF16)


def turn_pairs(x, cosine, sine):
    quarter = LANES // 4
    first = index(x.shape, 1) % (2 * quarter) < quarter
    other = jnp.where(first, pltpu.roll(x, 3 * quarter, 1), pltpu.roll(x, quarter, 1))
    return x * cosine + other * sine


def attention_kernel(me_ref, in_ref, cos_ref, sin_ref, length_ref, cache_ref, out_ref, q_ref, o_ref):
    me = me_ref[0]
    requests, _, span, _ = cache_ref.shape
    heads = SUBLANES
    total = summed(in_ref)
    depth = total.shape[0] - SUBLANES
    tiles = depth // requests
    scale_row = norm_scale(total[depth + 1 : depth + 2] + total[depth + 2 : depth + 3])
    scale = to_column(scale_row, requests)
    cosine = cos_ref[...]
    sine = sin_ref[...]
    low = low_lanes(requests)
    for j in range(tiles):
        tile = total[j * requests : (j + 1) * requests] * scale
        tile = turn_pairs(tile, cosine, sine).astype(BF16).astype(F32)
        if j < tiles // 2:
            pair = (jnp.where(low, tile, 0.0), jnp.where(low, turned(tile), 0.0))
        else:
            pair = (jnp.where(low, 0.0, turned(tile)), jnp.where(low, 0.0, tile))
        q_ref[pl.ds(2 * j, requests, stride=heads), :] = pair[0]
        q_ref[pl.ds(2 * j + 1, requests, stride=heads), :] = pair[1]
    own_request = me // 2
    own_head = me % 2
    pick = index((requests, LANES), 0) == own_request
    one_low = low_lanes(1)
    own_scale = jnp.sum(
        jnp.where(index((1, LANES), 1) == own_request, scale_row, 0.0), axis=1, keepdims=True
    )
    own_pair = total[depth : depth + 1] * own_scale
    own_cos = jnp.sum(jnp.where(pick, cosine, 0.0), axis=0, keepdims=True)
    own_sin = jnp.sum(jnp.where(pick, sine, 0.0), axis=0, keepdims=True)
    new_key = jnp.where(one_low, turn_pairs(own_pair, own_cos, own_sin), 0.0)
    new_value = jnp.where(one_low, 0.0, own_pair)
    new_key = jnp.where(own_head == 0, new_key, turned(new_key)).astype(BF16).astype(F32)
    new_value = jnp.where(own_head == 0, turned(new_value), new_value).astype(BF16).astype(F32)
    inv_scale = HD ** (-0.5)
    flat = requests * heads
    row = index((flat, 1), 0)
    mine = (row // heads == own_request) & (row % heads // (heads // 2) == own_head)
    own_score = jnp.sum(q_ref[...] * new_key, axis=1, keepdims=True) * inv_scale
    own_score = jnp.where(mine, own_score, NEGATIVE)
    scores = jnp.concatenate(
        [
            lax.dot_general(
                q_ref[b * heads : (b + 1) * heads, :].astype(BF16),
                cache_ref[b, 0],
                LANE_CONTRACT,
                preferred_element_type=F32,
            )
            for b in range(requests)
        ],
        axis=0,
    )
    usable = me * span + index((flat, span), 1) < length_ref[...]
    scores = jnp.where(usable, scores * inv_scale, NEGATIVE)
    best = jnp.maximum(jnp.max(scores, axis=1, keepdims=True), own_score)
    terms = jnp.where(usable, jnp.exp(scores - best), 0.0)
    own_term = jnp.where(mine, jnp.exp(own_score - best), 0.0)
    norm = jnp.sum(terms, axis=1, keepdims=True) + own_term
    weighted = jnp.concatenate(
        [
            jnp.dot(
                terms[b * heads : (b + 1) * heads].astype(BF16),
                cache_ref[b, 1],
                preferred_element_type=F32,
            )
            for b in range(requests)
        ],
        axis=0,
    )
    weighted = weighted + own_term.astype(BF16).astype(F32) * new_value
    o_ref[...] = weighted / jnp.where(norm > 0.0, norm, 1.0)
    average = []
    for i in range(heads // 2):
        first = o_ref[pl.ds(i, requests, stride=heads), :]
        second = o_ref[pl.ds(i + heads // 2, requests, stride=heads), :]
        average.append(jnp.where(low, first, second))
    lane = index((requests, LANES), 1)
    wide = []
    for value in (best, norm):
        o_ref[...] = jnp.broadcast_to(value, (flat, LANES))
        tile = jnp.zeros((requests, LANES), F32)
        for h in range(heads):
            tile = jnp.where(lane % heads == h, o_ref[pl.ds(h, requests, stride=heads), :], tile)
        wide.append(tile)
    best_high, rest = halves(wide[0])
    best_mid, best_low = halves(rest)
    norm_high, norm_low = halves(wide[1])
    side = jnp.zeros((requests, LANES), F32)
    for k, piece in enumerate((best_high, best_mid, best_low, norm_high, norm_low)):
        side = jnp.where(lane // heads == k, piece, side)
    block = jnp.concatenate(average + [side], axis=0).astype(BF16)
    for peer in range(out_ref.shape[0]):
        out_ref[peer] = block


def combine_kernel(in_ref, weight_ref, out_ref):
    peers, rows, _ = in_ref.shape
    heads = SUBLANES
    tiles = heads // 2
    requests = rows // (tiles + 1)
    depth = tiles * requests
    side = in_ref[:, depth:rows, :].astype(F32).reshape(peers * requests, LANES)

    def piece(k):
        return pltpu.roll(side, LANES - heads * k, 1) if k else side

    best = ((piece(0) + piece(1)) + piece(2)).reshape(peers, requests, LANES)
    norm = (piece(3) + piece(4)).reshape(peers, requests, LANES)
    factor = norm * jnp.exp(best - jnp.max(best, axis=0, keepdims=True))
    factor = factor / jnp.sum(factor, axis=0, keepdims=True)
    factor = factor.reshape(peers * requests, LANES)
    factor = jnp.where(index((peers * requests, LANES), 1) < heads, factor, 0.0)
    dims = (LANES, tiles * LANES)
    column = index(dims, 1)
    owner = column // LANES + tiles * (column % LANES // (LANES // 2))
    pick = (index(dims, 0) == owner).astype(F32).astype(BF16)
    high, low = halves(factor)
    factor = jnp.dot(high.astype(BF16), pick, preferred_element_type=F32) + jnp.dot(
        low.astype(BF16), pick, preferred_element_type=F32
    )
    sums = [jnp.zeros((requests, LANES), F32) for _ in range(tiles)]
    for peer in range(peers):
        for i in range(tiles):
            sums[i] = sums[i] + in_ref[peer, i * requests : (i + 1) * requests, :].astype(
                F32
            ) * factor[peer * requests : (peer + 1) * requests, i * LANES : (i + 1) * LANES]
    weights = weight_ref[...].astype(F32)
    take = low_lanes(weights.shape[0])
    total = jnp.zeros((requests, LANES), F32)
    for i in range(tiles):
        first = weights[:, i // 2 * LANES : (i // 2 + 1) * LANES]
        second = weights[:, (i // 2 + 2) * LANES : (i // 2 + 3) * LANES]
        if i % 2 == 0:
            tile = jnp.where(take, first, turned(second))
        else:
            tile = jnp.where(take, turned(first), second)
        tile = jnp.concatenate([tile, tile], axis=0).astype(BF16)
        total = total + lax.dot_general(
            sums[i].astype(BF16), tile, LANE_CONTRACT, preferred_element_type=F32
        )
    half = requests // 2
    packed = jnp.where(low_lanes(half), total[:half], total[half:])
    for side_at in range(out_ref.shape[0]):
        out_ref[side_at] = packed


def unpacked(packed):
    width = LANES // 2
    return jnp.concatenate([packed[:, :width], turned(packed)[:, :width]], axis=0)


def packed_squares(packed, offset=0):
    half = packed.shape[0]
    low = low_lanes(half)
    square = packed * packed
    first = jnp.sum(jnp.where(low, square, 0.0), axis=1, keepdims=True)
    second = jnp.sum(jnp.where(low, 0.0, square), axis=1, keepdims=True)
    return to_row(first, offset) + to_row(second, offset + half)


def gate_kernel(in_ref, x_ref, gain_ref, weight_ref, out_ref, one_ref):
    one = (x_ref[...] + summed(in_ref)).astype(BF16).astype(F32)
    one_ref[...] = one
    normed = unpacked(one * gain_ref[...]).astype(BF16)
    requests = normed.shape[0]
    both = jnp.dot(normed, weight_ref[...], preferred_element_type=F32)
    width = both.shape[1] // 2
    high_part, low_part = halves(packed_squares(one))
    side = block_of([high_part, low_part]).astype(BF16)
    low = low_lanes(requests)
    for t in range(width // LANES):
        gate = both[:, t * LANES : (t + 1) * LANES]
        up = both[:, width + t * LANES : width + (t + 1) * LANES]
        out_ref[2 * t, 0:requests] = jnp.where(low, gate, turned(up)).astype(BF16)
        out_ref[2 * t + 1, 0:requests] = jnp.where(low, turned(gate), up).astype(BF16)
        out_ref[2 * t, requests : requests + SUBLANES] = side
        out_ref[2 * t + 1, requests : requests + SUBLANES] = side


def activation_kernel(in_ref, out_ref):
    total = summed(in_ref)
    requests = total.shape[0] - SUBLANES
    scale_row = norm_scale(total[requests : requests + 1] + total[requests + 1 : requests + 2])
    both = total[:requests] * to_column(scale_row, requests)
    active = both / (1.0 + jnp.exp(-both)) * turned(both)
    half = requests // 2
    packed = jnp.where(low_lanes(half), active[:half], turned(active)[half:]).astype(BF16)
    for peer in range(out_ref.shape[0]):
        out_ref[peer] = packed


def down_kernel(in_ref, weight_ref, out_ref):
    peers, half, _ = in_ref.shape
    low = low_lanes(half)
    total = jnp.zeros((2 * half, LANES), F32)
    for t in range(peers // 2):
        first = in_ref[2 * t].astype(F32)
        second = in_ref[2 * t + 1].astype(F32)
        units = jnp.concatenate(
            [jnp.where(low, first, turned(second)), jnp.where(low, turned(first), second)], axis=0
        )
        tile = weight_ref[:, t * LANES : (t + 1) * LANES]
        tile = jnp.concatenate([tile, tile], axis=0)
        total = total + lax.dot_general(
            units.astype(BF16), tile, LANE_CONTRACT, preferred_element_type=F32
        )
    packed = jnp.where(low, total[:half], total[half:])
    for side_at in range(out_ref.shape[0]):
        out_ref[side_at] = packed


def next_kernel(
    guide_ref,
    own_ref,
    other_ref,
    final_ref,
    gain_ref,
    query_ref,
    pair_ref,
    out_ref,
    head_ref,
):
    guide = guide_ref[0]
    own = own_ref[...].astype(F32)
    other = other_ref[...].astype(F32)
    half = own.shape[0]
    normed = unpacked(own * gain_ref[...]).astype(BF16)
    query = jnp.dot(normed, query_ref[...], preferred_element_type=F32)
    tiles = [query[:, j * LANES : (j + 1) * LANES] for j in range(query.shape[1] // LANES)]
    tiles += pair_dots(normed, pair_ref)
    first = jnp.where(guide == 0, own, other)
    second = jnp.where(guide == 0, other, own)
    high_part, low_part = halves(packed_squares(first) + packed_squares(second, 2 * half))
    side = block_of([high_part, low_part])
    zero = jnp.zeros((half, LANES), F32)
    for peer in range(out_ref.shape[0]):
        j, part = divmod(peer, 2)
        piece = tiles[j][part * half : (part + 1) * half] if j < len(tiles) else zero
        out_ref[peer] = jnp.concatenate([piece, side], axis=0).astype(BF16)
    width = LANES // 2
    both = []
    for group in (first, second):
        group = group * final_ref[...]
        both.append(jnp.where(guide == 0, group, turned(group))[:, :width])
    head_ref[...] = jnp.concatenate(both, axis=0).astype(BF16)


def guided_kernel(spot_ref, in_ref, guidance_ref, head_ref, out_ref, *, starts, window):
    me = spot_ref[0]
    guide = spot_ref[1]
    total = summed(in_ref)
    half = SUBLANES
    scale_row = norm_scale(total[half : half + 1] + total[half + 1 : half + 2])

    def scales(offset):
        hit = index((half, LANES), 1) == index((half, LANES), 0) + offset
        return jnp.sum(jnp.where(hit, scale_row, 0.0), axis=1, keepdims=True)

    guidance = guidance_ref[...]
    first = guidance * scales(guide * half)
    second = (1.0 - guidance) * scales(2 * half + guide * half)
    piece = (total[:half] * scales(2 * half * guide + me % 2 * half)).astype(BF16)
    vocabulary = head_ref.shape[1]
    for peer, start in enumerate(starts):
        stop = min(start + window, vocabulary)
        part = first * head_ref[0:half, start:stop] + second * head_ref[half : 2 * half, start:stop]
        if stop - start < window:
            out_ref[peer, :, window - LANES : window] = jnp.zeros((half, LANES), BF16)
        out_ref[peer, :, 0 : stop - start] = part.astype(BF16)
        out_ref[peer, :, window : window + LANES] = piece


def finish_kernel(spot_ref, in_ref, guided_ref, query_ref, pair_ref, total_ref, pairs_ref, *, window):
    shift = spot_ref[0]
    total = in_ref[0, :, 0:window].astype(F32)
    for peer in range(1, in_ref.shape[0]):
        total = total + in_ref[peer, :, 0:window].astype(F32)
    total = pltpu.roll(total, shift, 1)
    guided_ref[...] = total[:, : guided_ref.shape[1]]
    tiles = query_ref.shape[1] // LANES
    half = in_ref.shape[1]

    def tile(j):
        return jnp.concatenate(
            [in_ref[2 * j, :, window : window + LANES], in_ref[2 * j + 1, :, window : window + LANES]],
            axis=0,
        )

    for j in range(tiles):
        query_ref[:, j * LANES : (j + 1) * LANES] = tile(j)
    for which in range(2):
        pairs_ref[pl.ds(which, 2 * half, stride=2), :] = tile(tiles + which).astype(F32)
    pair_ref[...] = pairs_ref[...].astype(BF16)


def local(
    hidden,
    lengths,
    kv_cache,
    attn_gain,
    w_query,
    w_key_value,
    w_out,
    mlp_gain,
    w_gate_up,
    w_down,
    final_gain,
    w_head,
    next_gain,
    w_next_query,
    w_next_kv,
    tenant,
    guide_scale,
):
    x_rows = hidden[0]
    length = lengths[0]
    cache_block = kv_cache[0]
    requests, local_width = x_rows.shape
    half = requests // 2
    heads = (HEADS // KVH) * (w_key_value.shape[2] // HD)
    peers = lax.axis_size("row")
    sides = lax.axis_size("col")
    me = lax.axis_index("row").astype(jnp.int32)
    guide = lax.axis_index("guide").astype(jnp.int32)

    def doubled(gain):
        gain = gain.astype(F32)
        return jnp.concatenate([gain, gain])[None, :]

    query_width = w_query.shape[1]
    depth = query_width // LANES * requests
    payload = call(
        start_kernel,
        shape((peers, depth + SUBLANES, LANES), BF16),
        x_rows,
        attn_gain[None, :],
        w_query,
        w_key_value.reshape(2 * local_width, -1),
    )
    arrived = exchange(payload, "row")
    quarter = LANES // 4
    lane = jnp.arange(LANES)
    frequency = ROPE_BASE ** (-2.0 * (lane % quarter).astype(F32) / HD)
    angles = length.astype(F32)[:, None] * frequency[None, :]
    cosine = jnp.cos(angles)
    sine = jnp.where(lane % (2 * quarter) < quarter, -1.0, 1.0)[None, :] * jnp.sin(angles)
    flat = requests * heads
    partial = call(
        attention_kernel,
        shape((peers, depth + requests, LANES), BF16),
        me[None],
        arrived,
        cosine,
        sine,
        jnp.repeat(length, heads)[:, None],
        cache_block,
        scratch=[pltpu.VMEM((flat, LANES), F32), pltpu.VMEM((flat, LANES), F32)],
        scalars=1,
    )
    arrived = exchange(partial, "row")
    packed_sums = call(
        combine_kernel, shape((sides, half, LANES), F32), arrived, w_out.T
    )
    arrived = exchange(packed_sums, "col")
    x_packed = jnp.concatenate([x_rows[:half], x_rows[half:]], axis=1).astype(F32)
    payload, one_packed = call(
        gate_kernel,
        (shape((peers, requests + SUBLANES, LANES), BF16), shape((half, LANES), F32)),
        arrived,
        x_packed,
        doubled(mlp_gain),
        w_gate_up.reshape(local_width, -1),
    )
    arrived = exchange(payload, "row")
    active = call(activation_kernel, shape((peers, half, LANES), BF16), arrived)
    arrived = exchange(active, "row")
    packed_sums = call(down_kernel, shape((sides, half, LANES), F32), arrived, w_down.T)
    arrived = exchange(packed_sums, "col")
    residual_two = (one_packed + jnp.sum(arrived, axis=0)).astype(BF16)
    other_two = partner_2(residual_two, "guide", 0)
    payload, head_input = call(
        next_kernel,
        (shape((peers, 2 * SUBLANES, LANES), BF16), shape((requests, local_width), BF16)),
        guide[None],
        residual_two,
        other_two,
        doubled(final_gain),
        doubled(next_gain),
        w_next_query,
        w_next_kv.reshape(2 * local_width, -1),
        scalars=1,
    )
    arrived = exchange(payload, "row")
    head_part = jnp.dot(head_input, w_head, preferred_element_type=F32)
    guidance = jnp.sum(
        jnp.where(
            tenant[:, None] == jnp.arange(TENANTS, dtype=jnp.int32)[None, :],
            guide_scale[None, :],
            0.0,
        ),
        axis=1,
    )
    my_guidance = lax.dynamic_slice_in_dim(guidance, guide * half, half, 0)[:, None]
    vocabulary = w_head.shape[1]
    share = vocabulary // peers
    window = (share + 2 * LANES - 2) // LANES * LANES
    starts = [share * k // LANES * LANES for k in range(peers)]
    payload = call(
        functools.partial(guided_kernel, starts=starts, window=window),
        shape((peers, half, window + LANES), BF16),
        jnp.stack([me, guide]),
        arrived,
        my_guidance,
        head_part,
        scalars=1,
    )
    arrived = exchange(payload, "row")
    shift = (window - share * me % LANES) % window
    guided, next_query, next_pairs = call(
        functools.partial(finish_kernel, window=window),
        (
            shape((half, share), F32),
            shape((requests, query_width), BF16),
            shape((2 * requests, LANES), BF16),
        ),
        shift[None],
        arrived,
        scratch=[pltpu.VMEM((half, window), F32), pltpu.VMEM((2 * requests, LANES), F32)],
        scalars=1,
    )
    return (guided, next_query[None], next_pairs.reshape(1, requests, 2, LANES))


def solution(mesh):
    placed = (
        P("guide", None, "row"),
        P("guide", None),
        P("guide", None, None, "row", "col"),
        P("row"),
        P("row", "col"),
        P("row", None, "col"),
        P("col", "row"),
        P("row"),
        P("row", None, "col"),
        P("col", "row"),
        P("row"),
        P("row", "col"),
        P("row"),
        P("row", "col"),
        P("row", None, "col"),
        P(),
        P(),
    )
    return jax.shard_map(
        local,
        mesh=mesh,
        in_specs=placed,
        out_specs=(
            P("guide", ("col", "row")),
            P("guide", None, "col"),
            P("guide", None, None, "col"),
        ),
        check_vma=False,
    )
```

time: 624 us -> 158 us (0.25)
  blocking collectives: 469 us -> 15.3 us
  starting transfers between devices: 0.21 us -> 37.3 us
  other arithmetic: 38 us -> 1.19 us
  between operations: 14.8 us -> 0.86 us
  Pallas kernels: 0 us -> 10.1 us
  waiting for transfers between devices: 76.4 us -> 84.6 us
  local copies, waits for them, and re-layouts: 12.4 us -> 5.35 us
    psum x5 -> x0, blocking collectives: 371 us -> none  [the longest x1 140 us: local(): lax.psum((query_part, pair_part, squares(x_float)), 'row')]
    all_gather x2 -> x0, blocking collectives: 98 us -> none  [joined(): everything = jax.tree.map(lambda part: lax.all_gather(part, axis), x)]
    all_to_all x0 -> x7, waiting for transfers between devices: none -> 83.7 us  [exchange(): return lax.all_to_all(x, axis, 0, 0, tiled=True)]
    psum x1 -> x0, waiting for transfers between devices: 66.7 us -> none  [local(): gate_up, second_squares = lax.psum((gate_part, squares(one_float)), 'row')]
    all_to_all x0 -> x7, starting transfers between devices: none -> 37.2 us  [exchange(): return lax.all_to_all(x, axis, 0, 0, tiled=True)]
    add x64 -> x0, other arithmetic: 34.7 us -> none  [the longest x31 33.2 us: join_parts(): weighted_a * factor_a[..., None] + weighted_b * factor_b[..., None]]
    all_to_all x0 -> x1, blocking collectives: none -> 15.3 us  [exchange(): return lax.all_to_all(x, axis, 0, 0, tiled=True)]
    pallas_call x0 -> x9, Pallas kernels: none -> 10.1 us  [call(): pl.pallas_call(body, out_shape=outs, in_specs=specs, out_specs=out_specs,...]
  transfers between devices with their start and end apart: 4 -> 8, of which waited for: 3 -> 8; matrix products, arithmetic and copies ran while one was open for 1% -> 3% of each run, Pallas kernels for 0% -> 0%
where the time goes in v2:
time: 158 us
  waiting for transfers between devices  84.6 us (54%)
  starting transfers between devices  37.3 us (24%)
  blocking collectives  15.3 us (10%)
  Pallas kernels  10.1 us (6%)
  local copies, waits for them, and re-layouts  5.35 us (3%)
  matrix products  2.82 us (2%)
    all_to_all x7, waiting for transfers between devices, exchange(): return lax.all_to_all(x, axis, 0, 0, tiled=True)  83.7 us
    all_to_all x7, starting transfers between devices, exchange(): return lax.all_to_all(x, axis, 0, 0, tiled=True)  37.2 us
    all_to_all x1, blocking collectives, exchange(): return lax.all_to_all(x, axis, 0, 0, tiled=True)  15.3 us
    pallas_call x9, Pallas kernels, call(): pl.pallas_call(body, out_shape=outs, in_specs=specs, out_specs=out_specs,...  10.1 us
    unnamed x33, local copies, waits for them, and re-layouts  4.38 us
  transfers between devices with their start and end apart: 8, of which 8 were waited for; matrix products, arithmetic and copies ran while one was open for 3% of the time, Pallas kernels for 0%

profile of v2, /device:TPU:32, one launch (start us, length us, event | category | flops | bytes accessed | tf_op | source)
XLA Modules:
  0.0 157.6 jit_solution(11446649328399084300)
XLA Ops:
  0.7 0.8 copy-done.2
  1.5 0.8 copy-done.5
  2.3 0.7 copy-done.7
  3.0 0.7 copy-done.9
  3.6 1.2 shard_map.184
  4.8 11.3 %all-to-all-start = ((bf16[32,72,128]{2,1,0:T(8,128)(2,1)}), bf16[32,72,128]{2,1,0:T(8,128)(2,1)S(1)}, u32[]{:S(2)}, u32[]{:S(2)}) async-start(bf16[32,72,128]{2,1,0:T(8,128)(2,1)} %shard_map.184), calls=%async_computation | async-start | bytes 1179648 | tf_op jit(solution)/shard_map/all_to_all | solution.py:28
  16.2 0.7 broadcast_in_dim.62
  17.0 0.7 bitcast_convert_fusion
  17.8 17.4 %all-to-all-done.in_ref = bf16[32,72,128]{2,1,0:T(8,128)(2,1)S(1)} async-done(((bf16[32,72,128]{2,1,0:T(8,128)(2,1)}), bf16[32,72,128]{2,1,0:T(8,128)(2,1)S(1)}, u32[]{:S(2)}, u32[]{:S(2)}) %all-to-all-start) | async-done | bytes 589856 | tf_op jit(solution)/shard_map/all_to_all | solution.py:28
  35.2 1.2 copy-done
  36.4 1.8 %shard_map.185 = bf16[32,80,128]{2,1,0:T(8,128)(2,1)} custom-call(s32[1]{0:T(128)} %bitcast.1.me_ref, bf16[32,72,128]{2,1,0:T(8,128)(2,1)S(1)} %all-to-all-done.in_ref, f32[16,128]{1,0:T(8,128)S(1)} %get-tuple-element.20.cos_ref, f32[16,128]{1,0:T(8,128)S(1)} %get-tuple-element.19.sin_ref, s32[128,1]{1,0:T(8,128)S(1)} %broadcast_in_dim_reshape.4.length_ref, ...), custom_call_target="tpu_custom_call" | custom-call | tf_op jit(solution)/shard_map/pallas_call | solution.py:39
  38.2 4.9 %all-to-all-start.1 = ((bf16[32,80,128]{2,1,0:T(8,128)(2,1)}), bf16[32,80,128]{2,1,0:T(8,128)(2,1)S(1)}, u32[]{:S(2)}, u32[]{:S(2)}) async-start(bf16[32,80,128]{2,1,0:T(8,128)(2,1)} %shard_map.185), calls=%async_computation.1 | async-start | bytes 1310720 | tf_op jit(solution)/shard_map/all_to_all | solution.py:28
  43.1 19.5 %all-to-all-done.1.in_ref = bf16[32,80,128]{2,1,0:T(8,128)(2,1)S(1)} async-done(((bf16[32,80,128]{2,1,0:T(8,128)(2,1)}), bf16[32,80,128]{2,1,0:T(8,128)(2,1)S(1)}, u32[]{:S(2)}, u32[]{:S(2)}) %all-to-all-start.1) | async-done | bytes 655392 | tf_op jit(solution)/shard_map/all_to_all | solution.py:28
  62.6 1.5 shard_map.186
  64.1 4.5 %all-to-all-start.2 = ((f32[4,8,128]{2,1,0:T(8,128)}), f32[4,8,128]{2,1,0:T(8,128)S(1)}, u32[]{:S(2)}, u32[]{:S(2)}) async-start(f32[4,8,128]{2,1,0:T(8,128)} %shard_map.186), calls=%async_computation.2 | async-start | bytes 32768 | tf_op jit(solution)/shard_map/all_to_all | solution.py:28
  68.8 5.1 %all-to-all-done.2.in_ref = f32[4,8,128]{2,1,0:T(8,128)S(1)} async-done(((f32[4,8,128]{2,1,0:T(8,128)}), f32[4,8,128]{2,1,0:T(8,128)S(1)}, u32[]{:S(2)}, u32[]{:S(2)}) %all-to-all-start.2) | async-done | bytes 16416 | tf_op jit(solution)/shard_map/all_to_all | solution.py:28
  74.2 15.3 %all_to_all.40.in_ref = bf16[32,24,128]{2,1,0:T(8,128)(2,1)S(1)} all-to-all(bf16[32,24,128]{2,1,0:T(8,128)(2,1)S(1)} %get-tuple-element.11), channel_id=1, replica_groups=mesh['guide'=2,'row'=32,'col'=4] {'row'}, dimensions={0} | all-to-all | bytes 393216 | tf_op jit(solution)/shard_map/all_to_all | solution.py:28
  89.5 0.9 shard_map.188
  90.4 4.3 %all-to-all-start.4 = ((bf16[32,8,128]{2,1,0:T(8,128)(2,1)}), bf16[32,8,128]{2,1,0:T(8,128)(2,1)S(1)}, u32[]{:S(2)}, u32[]{:S(2)}) async-start(bf16[32,8,128]{2,1,0:T(8,128)(2,1)} %shard_map.188), calls=%async_computation.4 | async-start | bytes 131072 | tf_op jit(solution)/shard_map/all_to_all | solution.py:28
  94.9 8.9 %all-to-all-done.4.in_ref = bf16[32,8,128]{2,1,0:T(8,128)(2,1)S(1)} async-done(((bf16[32,8,128]{2,1,0:T(8,128)(2,1)}), bf16[32,8,128]{2,1,0:T(8,128)(2,1)S(1)}, u32[]{:S(2)}, u32[]{:S(2)}) %all-to-all-start.4) | async-done | bytes 65568 | tf_op jit(solution)/shard_map/all_to_all | solution.py:28
  103.9 1.0 shard_map.189
  104.9 3.3 %all-to-all-start.5 = ((f32[4,8,128]{2,1,0:T(8,128)}), f32[4,8,128]{2,1,0:T(8,128)S(1)}, u32[]{:S(2)}, u32[]{:S(2)}) async-start(f32[4,8,128]{2,1,0:T(8,128)} %shard_map.189), calls=%async_computation.5 | async-start | bytes 32768 | tf_op jit(solution)/shard_map/all_to_all | solution.py:28
  108.2 5.2 %all-to-all-done.5 = f32[4,8,128]{2,1,0:T(8,128)S(1)} async-done(((f32[4,8,128]{2,1,0:T(8,128)}), f32[4,8,128]{2,1,0:T(8,128)S(1)}, u32[]{:S(2)}, u32[]{:S(2)}) %all-to-all-start.5) | async-done | bytes 16416 | tf_op jit(solution)/shard_map/all_to_all | solution.py:28
  113.8 1.0 collective-permute-done.other_ref
  114.7 1.0 shard_map.190
  115.7 4.6 %all-to-all-start.6 = ((bf16[32,16,128]{2,1,0:T(8,128)(2,1)}), bf16[32,16,128]{2,1,0:T(8,128)(2,1)S(1)}, u32[]{:S(2)}, u32[]{:S(2)}) async-start(bf16[32,16,128]{2,1,0:T(8,128)(2,1)} %get-tuple-element.12), calls=%async_computation.6 | async-start | bytes 262144 | tf_op jit(solution)/shard_map/all_to_all | solution.py:28
  120.4 2.8 %fusion.7.head_ref = f32[16,32064]{1,0:T(8,128)S(1)} fusion(bf16[16,64]{1,0:T(8,128)(2,1)S(1)} %get-tuple-element.13, bf16[64,32064]{1,0:T(8,128)(2,1)} %param.28), kind=kOutput, calls=%fused_computation.24 | convolution fusion | flops 65667072 | bytes 6158336 | tf_op jit(solution)/shard_map/dot_general | solution.py:534
  123.2 7.7 %all-to-all-done.6.in_ref = bf16[32,16,128]{2,1,0:T(8,128)(2,1)S(1)} async-done(((bf16[32,16,128]{2,1,0:T(8,128)(2,1)}), bf16[32,16,128]{2,1,0:T(8,128)(2,1)S(1)}, u32[]{:S(2)}, u32[]{:S(2)}) %all-to-all-start.6) | async-done | bytes 131104 | tf_op jit(solution)/shard_map/all_to_all | solution.py:28
  130.8 1.7 %shard_map.191 = bf16[32,8,1280]{2,1,0:T(8,128)(2,1)} custom-call(s32[2]{0:T(128)S(1)} %pad_add_fusion.spot_ref, bf16[32,16,128]{2,1,0:T(8,128)(2,1)S(1)} %all-to-all-done.6.in_ref, f32[8,1]{1,0:T(8,128)S(1)} %copy.25.guidance_ref, f32[16,32064]{1,0:T(8,128)S(1)} %fusion.7.head_ref), custom_call_target="tpu_custom_call" | custom-call | tf_op jit(solution)/shard_map/pallas_call | solution.py:39
  132.5 4.3 %all-to-all-start.7 = ((bf16[32,8,1280]{2,1,0:T(8,128)(2,1)}), bf16[32,8,1280]{2,1,0:T(8,128)(2,1)S(1)}, u32[]{:S(2)}, u32[]{:S(2)}) async-start(bf16[32,8,1280]{2,1,0:T(8,128)(2,1)} %shard_map.191), calls=%async_computation.7 | async-start | bytes 1310720 | tf_op jit(solution)/shard_map/all_to_all | solution.py:28
  136.9 19.9 %all-to-all-done.7.in_ref = bf16[32,8,1280]{2,1,0:T(8,128)(2,1)S(1)} async-done(((bf16[32,8,1280]{2,1,0:T(8,128)(2,1)}), bf16[32,8,1280]{2,1,0:T(8,128)(2,1)S(1)}, u32[]{:S(2)}, u32[]{:S(2)}) %all-to-all-start.7) | async-done | bytes 655392 | tf_op jit(solution)/shard_map/all_to_all | solution.py:28
  156.8 0.8 shard_map.192
  (43 shorter events, 1.4 us)
Async XLA Ops:
  0.6 42.4 %copy-start.8 = (bf16[1,16,64]{2,1,0:T(8,128)(2,1)S(1)}, bf16[1,16,64]{2,1,0:T(8,128)(2,1)}, u32[]{:S(2)}) copy-start(bf16[1,16,64]{2,1,0:T(8,128)(2,1)} %param.17) | copy-start | bytes 6148
  0.6 67.9 %copy-start.13 = (bf16[64]{0:T(256)(128)(2,1)S(1)}, bf16[64]{0:T(256)(128)(2,1)}, u32[]{:S(2)}) copy-start(bf16[64]{0:T(256)(128)(2,1)} %param.24) | copy-start | bytes 388
  0.7 0.9 copy-start.2
  1.5 0.8 copy-start.5
  2.3 0.7 copy-start.7
  3.0 0.7 copy-start.9
  3.6 59.0 %copy-start.3 = (bf16[512,64]{0,1:T(8,128)(2,1)S(1)}, bf16[512,64]{0,1:T(8,128)(2,1)}, u32[]{:S(2)}) copy-start(bf16[512,64]{0,1:T(8,128)(2,1)} %param.23) | copy-start | bytes 196612
  3.6 65.0 %copy-start.10 = (bf16[64,2,2048]{2,1,0:T(2,128)(2,1)S(1)}, bf16[64,2,2048]{2,1,0:T(2,128)(2,1)}, u32[]{:S(2)}) copy-start(bf16[64,2,2048]{2,1,0:T(2,128)(2,1)} %param.25) | copy-start | bytes 1572868
  4.8 90.0 %copy-start.11 = (bf16[64]{0:T(256)(128)(2,1)S(1)}, bf16[64]{0:T(256)(128)(2,1)}, u32[]{:S(2)}) copy-start(bf16[64]{0:T(256)(128)(2,1)} %param.27) | copy-start | bytes 388
  4.8 90.0 %copy-start.12 = (bf16[64]{0:T(256)(128)(2,1)S(1)}, bf16[64]{0:T(256)(128)(2,1)}, u32[]{:S(2)}) copy-start(bf16[64]{0:T(256)(128)(2,1)} %param.29) | copy-start | bytes 388
  4.8 90.1 %copy-start.14 = (f32[4]{0:T(128)S(1)}, f32[4]{0:T(128)}, u32[]{:S(2)}) copy-start(f32[4]{0:T(128)} %param.33) | copy-start | bytes 52
  4.8 90.1 %copy-start.15 = (s32[16]{0:T(128)S(1)}, s32[16]{0:T(128)}, u32[]{:S(2)}) copy-start(s32[16]{0:T(128)} %param.32) | copy-start | bytes 196
  4.8 99.1 %copy-start.1 = (bf16[2048,64]{0,1:T(8,128)(2,1)S(1)}, bf16[2048,64]{0,1:T(8,128)(2,1)}, u32[]{:S(2)}) copy-start(bf16[2048,64]{0,1:T(8,128)(2,1)} %param.26) | copy-start | bytes 786436
  4.8 109.9 %copy-start.4 = (bf16[64,512]{1,0:T(8,128)(2,1)S(1)}, bf16[64,512]{1,0:T(8,128)(2,1)}, u32[]{:S(2)}) copy-start(bf16[64,512]{1,0:T(8,128)(2,1)} %query_ref.3) | copy-start | bytes 196612
  4.8 109.9 %copy-start.6 = (bf16[64,2,128]{2,1,0:T(2,128)(2,1)S(1)}, bf16[64,2,128]{2,1,0:T(2,128)(2,1)}, u32[]{:S(2)}) copy-start(bf16[64,2,128]{2,1,0:T(2,128)(2,1)} %param.31) | copy-start | bytes 98308
  4.8 30.3 %all-to-all-start = ((bf16[32,72,128]{2,1,0:T(8,128)(2,1)}), bf16[32,72,128]{2,1,0:T(8,128)(2,1)S(1)}, u32[]{:S(2)}, u32[]{:S(2)}) async-start(bf16[32,72,128]{2,1,0:T(8,128)(2,1)} %shard_map.184), calls=%async_computation | async-start | bytes 1179648 | tf_op jit(solution)/shard_map/all_to_all | solution.py:28
  35.2 1.2 copy-start
  38.2 24.4 %all-to-all-start.1 = ((bf16[32,80,128]{2,1,0:T(8,128)(2,1)}), bf16[32,80,128]{2,1,0:T(8,128)(2,1)S(1)}, u32[]{:S(2)}, u32[]{:S(2)}) async-start(bf16[32,80,128]{2,1,0:T(8,128)(2,1)} %shard_map.185), calls=%async_computation.1 | async-start | bytes 1310720 | tf_op jit(solution)/shard_map/all_to_all | solution.py:28
  64.1 9.8 %all-to-all-start.2 = ((f32[4,8,128]{2,1,0:T(8,128)}), f32[4,8,128]{2,1,0:T(8,128)S(1)}, u32[]{:S(2)}, u32[]{:S(2)}) async-start(f32[4,8,128]{2,1,0:T(8,128)} %shard_map.186), calls=%async_computation.2 | async-start | bytes 32768 | tf_op jit(solution)/shard_map/all_to_all | solution.py:28
  90.4 13.4 %all-to-all-start.4 = ((bf16[32,8,128]{2,1,0:T(8,128)(2,1)}), bf16[32,8,128]{2,1,0:T(8,128)(2,1)S(1)}, u32[]{:S(2)}, u32[]{:S(2)}) async-start(bf16[32,8,128]{2,1,0:T(8,128)(2,1)} %shard_map.188), calls=%async_computation.4 | async-start | bytes 131072 | tf_op jit(solution)/shard_map/all_to_all | solution.py:28
  104.9 8.6 %all-to-all-start.5 = ((f32[4,8,128]{2,1,0:T(8,128)}), f32[4,8,128]{2,1,0:T(8,128)S(1)}, u32[]{:S(2)}, u32[]{:S(2)}) async-start(f32[4,8,128]{2,1,0:T(8,128)} %shard_map.189), calls=%async_computation.5 | async-start | bytes 32768 | tf_op jit(solution)/shard_map/all_to_all | solution.py:28
  113.5 1.2 collective-permute-start
  115.7 15.1 %all-to-all-start.6 = ((bf16[32,16,128]{2,1,0:T(8,128)(2,1)}), bf16[32,16,128]{2,1,0:T(8,128)(2,1)S(1)}, u32[]{:S(2)}, u32[]{:S(2)}) async-start(bf16[32,16,128]{2,1,0:T(8,128)(2,1)} %get-tuple-element.12), calls=%async_computation.6 | async-start | bytes 262144 | tf_op jit(solution)/shard_map/all_to_all | solution.py:28
  132.5 24.2 %all-to-all-start.7 = ((bf16[32,8,1280]{2,1,0:T(8,128)(2,1)}), bf16[32,8,1280]{2,1,0:T(8,128)(2,1)S(1)}, u32[]{:S(2)}, u32[]{:S(2)}) async-start(bf16[32,8,1280]{2,1,0:T(8,128)(2,1)} %shard_map.191), calls=%async_computation.7 | async-start | bytes 1310720 | tf_op jit(solution)/shard_map/all_to_all | solution.py:28

commit v3 on v2

--- a/solution.py
+++ b/solution.py
@@ -14,6 +14,7 @@
 TENANTS = 4
 LANES = 128
 SUBLANES = 8
+LINES = 4
 
 EPSILON = 1e-05
 ROPE_BASE = 500000.0
@@ -30,6 +31,11 @@
 
 def partner_2(x, axis, apart):
     return lax.ppermute(x, axis, [(i, i ^ 1 << apart) for i in range(lax.axis_size(axis))])
+
+
+def from_others(x, axis):
+    n = lax.axis_size(axis)
+    return [lax.ppermute(x, axis, [(i, (i + k) % n) for i in range(n)]) for k in range(1, n)]
 
 
 def call(body, outs, *operands, scratch=(), scalars=0):
@@ -109,24 +115,48 @@
     return [jnp.dot(spread(normed, w), weights, preferred_element_type=F32) for w in range(2)]
 
 
-def start_kernel(x_ref, gain_ref, query_ref, pair_ref, out_ref):
+def start_kernel(
+    x_hbm, gain_hbm, query_hbm, pair_hbm, out_ref, x_ref, gain_ref, query_ref, pair_ref, sems
+):
+    sources = (x_hbm, gain_hbm, query_hbm, pair_hbm)
+    targets = (x_ref, gain_ref, query_ref, pair_ref)
+    copies = [
+        pltpu.make_async_copy(source, target, sems.at[k])
+        for k, (source, target) in enumerate(zip(sources, targets))
+    ]
+    for copy in copies:
+        copy.start()
+    for copy in copies:
+        copy.wait()
     x = x_ref[...].astype(F32)
     requests = x.shape[0]
     normed = (x * gain_ref[...].astype(F32)).astype(BF16)
     query = jnp.dot(normed, query_ref[...], preferred_element_type=F32)
-    tiles = query.shape[1] // LANES
-    rows = jnp.concatenate(
-        [query[:, j * LANES : (j + 1) * LANES] for j in range(tiles)], axis=0
-    ).astype(BF16)
     keys, values = pair_dots(normed, pair_ref)
     low = low_lanes(requests)
     own = (jnp.where(low, keys, turned(values)), jnp.where(low, turned(keys), values))
     high_part, low_part = halves(to_row(jnp.sum(x * x, axis=1, keepdims=True)))
-    depth = rows.shape[0]
+    half = requests // 2
+    upper = index((half, LANES), 0) < half // 2
+    variants = []
+    for parity in range(2):
+        pieces = []
+        for tile in range(query.shape[1] // LANES):
+            first = query[:half, tile * LANES : (tile + 1) * LANES]
+            second = query[half:, tile * LANES : (tile + 1) * LANES]
+            if parity:
+                first = pltpu.roll(first, half // 2, 0)
+                second = pltpu.roll(second, half // 2, 0)
+            pieces.append(jnp.where(upper, first, second))
+        variants.append(jnp.concatenate(pieces, axis=0).astype(BF16))
+    depth = variants[0].shape[0]
+    line = out_ref.shape[0] // LINES
     for peer in range(out_ref.shape[0]):
-        request, head = divmod(peer, 2)
-        side = block_of([own[head][request : request + 1], high_part, low_part])
-        out_ref[peer, 0:depth] = rows
+        column, place = divmod(peer, line)
+        quarter = column % 2 if column < 2 else 3 - column % 2
+        request = quarter * (requests // 4) + place // 2
+        side = block_of([own[place % 2][request : request + 1], high_part, low_part])
+        out_ref[peer, 0:depth] = variants[column % 2]
         out_ref[peer, depth : depth + SUBLANES] = side.astype(BF16)
 
 
@@ -137,34 +167,53 @@
     return x * cosine + other * sine
 
 
-def attention_kernel(me_ref, in_ref, cos_ref, sin_ref, length_ref, cache_ref, out_ref, q_ref, o_ref):
-    me = me_ref[0]
-    requests, _, span, _ = cache_ref.shape
+def attention_kernel(
+    me_ref,
+    in_ref,
+    cos_ref,
+    sin_ref,
+    length_ref,
+    own_a_ref,
+    own_b_ref,
+    other_a_ref,
+    other_b_ref,
+    out_ref,
+    q_ref,
+    o_ref,
+):
+    share, _, span, _ = own_a_ref.shape
     heads = SUBLANES
+    requests = 2 * share
+    line = in_ref.shape[0] // LINES
+    column = me_ref[0] // line
+    place = me_ref[0] % line
+    parity = column % 2
     total = summed(in_ref)
     depth = total.shape[0] - SUBLANES
-    tiles = depth // requests
     scale_row = norm_scale(total[depth + 1 : depth + 2] + total[depth + 2 : depth + 3])
-    scale = to_column(scale_row, requests)
+    lane = index((requests, LANES), 1)
+    row = index((requests, LANES), 0)
+    wanted = jnp.where(row < share, parity * share + row, (2 - parity) * share + row)
+    scale = jnp.sum(jnp.where(lane == wanted, scale_row, 0.0), axis=1, keepdims=True)
     cosine = cos_ref[...]
     sine = sin_ref[...]
     low = low_lanes(requests)
+    tiles = depth // requests
     for j in range(tiles):
         tile = total[j * requests : (j + 1) * requests] * scale
         tile = turn_pairs(tile, cosine, sine).astype(BF16).astype(F32)
+        other = turned(tile)
         if j < tiles // 2:
-            pair = (jnp.where(low, tile, 0.0), jnp.where(low, turned(tile), 0.0))
+            even, odd = jnp.where(low, tile, 0.0), jnp.where(low, other, 0.0)
         else:
-            pair = (jnp.where(low, 0.0, turned(tile)), jnp.where(low, 0.0, tile))
-        q_ref[pl.ds(2 * j, requests, stride=heads), :] = pair[0]
-        q_ref[pl.ds(2 * j + 1, requests, stride=heads), :] = pair[1]
-    own_request = me // 2
-    own_head = me % 2
-    pick = index((requests, LANES), 0) == own_request
+            even, odd = jnp.where(low, 0.0, other), jnp.where(low, 0.0, tile)
+        q_ref[pl.ds(2 * j, requests, stride=heads), :] = even
+        q_ref[pl.ds(2 * j + 1, requests, stride=heads), :] = odd
+    own_request = column // 2 * share + place // 2
+    own_head = place % 2
     one_low = low_lanes(1)
-    own_scale = jnp.sum(
-        jnp.where(index((1, LANES), 1) == own_request, scale_row, 0.0), axis=1, keepdims=True
-    )
+    pick = row == own_request
+    own_scale = jnp.sum(jnp.where(pick[:, :1], scale, 0.0), axis=0, keepdims=True)
     own_pair = total[depth : depth + 1] * own_scale
     own_cos = jnp.sum(jnp.where(pick, cosine, 0.0), axis=0, keepdims=True)
     own_sin = jnp.sum(jnp.where(pick, sine, 0.0), axis=0, keepdims=True)
@@ -174,47 +223,59 @@
     new_value = jnp.where(own_head == 0, turned(new_value), new_value).astype(BF16).astype(F32)
     inv_scale = HD ** (-0.5)
     flat = requests * heads
-    row = index((flat, 1), 0)
-    mine = (row // heads == own_request) & (row % heads // (heads // 2) == own_head)
+    flat_row = index((flat, 1), 0)
+    mine = (flat_row // heads == own_request) & (flat_row % heads // (heads // 2) == own_head)
     own_score = jnp.sum(q_ref[...] * new_key, axis=1, keepdims=True) * inv_scale
     own_score = jnp.where(mine, own_score, NEGATIVE)
-    scores = jnp.concatenate(
-        [
-            lax.dot_general(
-                q_ref[b * heads : (b + 1) * heads, :].astype(BF16),
-                cache_ref[b, 0],
-                LANE_CONTRACT,
-                preferred_element_type=F32,
-            )
-            for b in range(requests)
-        ],
-        axis=0,
-    )
-    usable = me * span + index((flat, span), 1) < length_ref[...]
-    scores = jnp.where(usable, scores * inv_scale, NEGATIVE)
-    best = jnp.maximum(jnp.max(scores, axis=1, keepdims=True), own_score)
-    terms = jnp.where(usable, jnp.exp(scores - best), 0.0)
+    near = column + 1 - 2 * parity
+    far = lax.rem(column + LINES - 1 + 2 * parity, LINES)
+    origins = (
+        jnp.broadcast_to(column, (flat, 1)),
+        jnp.where(flat_row < flat // 2, near, far),
+    )
+    best = own_score
+    scored = []
+    for block, (first, second) in enumerate(((own_a_ref, own_b_ref), (other_a_ref, other_b_ref))):
+        scores = jnp.concatenate(
+            [
+                lax.dot_general(
+                    q_ref[b * heads : (b + 1) * heads, :].astype(BF16),
+                    (first if b < share else second)[b % share, 0],
+                    LANE_CONTRACT,
+                    preferred_element_type=F32,
+                )
+                for b in range(requests)
+            ],
+            axis=0,
+        )
+        position = (origins[block] * line + place) * span + index((flat, span), 1)
+        usable = position < length_ref[...]
+        scores = jnp.where(usable, scores * inv_scale, NEGATIVE)
+        best = jnp.maximum(best, jnp.max(scores, axis=1, keepdims=True))
+        scored.append((scores, usable, first, second))
     own_term = jnp.where(mine, jnp.exp(own_score - best), 0.0)
-    norm = jnp.sum(terms, axis=1, keepdims=True) + own_term
-    weighted = jnp.concatenate(
-        [
-            jnp.dot(
-                terms[b * heads : (b + 1) * heads].astype(BF16),
-                cache_ref[b, 1],
-                preferred_element_type=F32,
-            )
-            for b in range(requests)
-        ],
-        axis=0,
-    )
-    weighted = weighted + own_term.astype(BF16).astype(F32) * new_value
+    norm = own_term
+    weighted = own_term.astype(BF16).astype(F32) * new_value
+    for scores, usable, first, second in scored:
+        terms = jnp.where(usable, jnp.exp(scores - best), 0.0)
+        norm = norm + jnp.sum(terms, axis=1, keepdims=True)
+        weighted = weighted + jnp.concatenate(
+            [
+                jnp.dot(
+                    terms[b * heads : (b + 1) * heads].astype(BF16),
+                    (first if b < share else second)[b % share, 1],
+                    preferred_element_type=F32,
+                )
+                for b in range(requests)
+            ],
+            axis=0,
+        )
     o_ref[...] = weighted / jnp.where(norm > 0.0, norm, 1.0)
-    average = []
+    blocks = []
     for i in range(heads // 2):
         first = o_ref[pl.ds(i, requests, stride=heads), :]
         second = o_ref[pl.ds(i + heads // 2, requests, stride=heads), :]
-        average.append(jnp.where(low, first, second))
-    lane = index((requests, LANES), 1)
+        blocks.append(jnp.where(low, first, second))
     wide = []
     for value in (best, norm):
         o_ref[...] = jnp.broadcast_to(value, (flat, LANES))
@@ -228,7 +289,7 @@
     side = jnp.zeros((requests, LANES), F32)
     for k, piece in enumerate((best_high, best_mid, best_low, norm_high, norm_low)):
         side = jnp.where(lane // heads == k, piece, side)
-    block = jnp.concatenate(average + [side], axis=0).astype(BF16)
+    block = jnp.concatenate(blocks + [side], axis=0).astype(BF16)
     for peer in range(out_ref.shape[0]):
         out_ref[peer] = block
 
@@ -236,38 +297,44 @@
 def combine_kernel(in_ref, weight_ref, out_ref):
     peers, rows, _ = in_ref.shape
     heads = SUBLANES
+    half = SUBLANES
     tiles = heads // 2
-    requests = rows // (tiles + 1)
-    depth = tiles * requests
-    side = in_ref[:, depth:rows, :].astype(F32).reshape(peers * requests, LANES)
+    line = peers // LINES
+    depth = rows - half
+    flat = peers * half
+    side = in_ref[:, depth:rows, :].astype(F32).reshape(flat, LANES)
 
     def piece(k):
         return pltpu.roll(side, LANES - heads * k, 1) if k else side
 
-    best = ((piece(0) + piece(1)) + piece(2)).reshape(peers, requests, LANES)
-    norm = (piece(3) + piece(4)).reshape(peers, requests, LANES)
-    factor = norm * jnp.exp(best - jnp.max(best, axis=0, keepdims=True))
-    factor = factor / jnp.sum(factor, axis=0, keepdims=True)
-    factor = factor.reshape(peers * requests, LANES)
-    factor = jnp.where(index((peers * requests, LANES), 1) < heads, factor, 0.0)
+    def over_peers(reduce, value):
+        return reduce(reduce(value, axis=2, keepdims=True), axis=0, keepdims=True)
+
+    dims = (LINES // 2, 2, line, half, LANES)
+    best = ((piece(0) + piece(1)) + piece(2)).reshape(dims)
+    norm = (piece(3) + piece(4)).reshape(dims)
+    factor = norm * jnp.exp(best - over_peers(jnp.max, best))
+    factor = factor / over_peers(jnp.sum, factor)
+    factor = factor.reshape(flat, LANES)
+    factor = jnp.where(index((flat, LANES), 1) < heads, factor, 0.0)
     dims = (LANES, tiles * LANES)
     column = index(dims, 1)
     owner = column // LANES + tiles * (column % LANES // (LANES // 2))
     pick = (index(dims, 0) == owner).astype(F32).astype(BF16)
-    high, low = halves(factor)
+    high, rest = halves(factor)
     factor = jnp.dot(high.astype(BF16), pick, preferred_element_type=F32) + jnp.dot(
-        low.astype(BF16), pick, preferred_element_type=F32
-    )
-    sums = [jnp.zeros((requests, LANES), F32) for _ in range(tiles)]
-    for peer in range(peers):
-        for i in range(tiles):
-            sums[i] = sums[i] + in_ref[peer, i * requests : (i + 1) * requests, :].astype(
-                F32
-            ) * factor[peer * requests : (peer + 1) * requests, i * LANES : (i + 1) * LANES]
+        rest.astype(BF16), pick, preferred_element_type=F32
+    )
     weights = weight_ref[...].astype(F32)
     take = low_lanes(weights.shape[0])
-    total = jnp.zeros((requests, LANES), F32)
+    result = jnp.zeros((2 * half, LANES), F32)
     for i in range(tiles):
+        averaged = [jnp.zeros((half, LANES), F32) for _ in range(2)]
+        for peer in range(peers):
+            parity = peer // line % 2
+            averaged[parity] = averaged[parity] + in_ref[
+                peer, i * half : (i + 1) * half, :
+            ].astype(F32) * factor[peer * half : (peer + 1) * half, i * LANES : (i + 1) * LANES]
         first = weights[:, i // 2 * LANES : (i // 2 + 1) * LANES]
         second = weights[:, (i // 2 + 2) * LANES : (i // 2 + 3) * LANES]
         if i % 2 == 0:
@@ -275,13 +342,18 @@
         else:
             tile = jnp.where(take, turned(first), second)
         tile = jnp.concatenate([tile, tile], axis=0).astype(BF16)
-        total = total + lax.dot_general(
-            sums[i].astype(BF16), tile, LANE_CONTRACT, preferred_element_type=F32
+        result = result + lax.dot_general(
+            jnp.concatenate(averaged, axis=0).astype(BF16),
+            tile,
+            LANE_CONTRACT,
+            preferred_element_type=F32,
         )
-    half = requests // 2
-    packed = jnp.where(low_lanes(half), total[:half], total[half:])
-    for side_at in range(out_ref.shape[0]):
-        out_ref[side_at] = packed
+    outer = result[:half]
+    inner = pltpu.roll(result[half:], half // 2, 0)
+    upper = index((half, LANES), 0) < half // 2
+    out_ref[...] = jnp.where(
+        low_lanes(half), jnp.where(upper, outer, inner), jnp.where(upper, inner, outer)
+    )
 
 
 def unpacked(packed):
@@ -298,8 +370,9 @@
     return to_row(first, offset) + to_row(second, offset + half)
 
 
-def gate_kernel(in_ref, x_ref, gain_ref, weight_ref, out_ref, one_ref):
-    one = (x_ref[...] + summed(in_ref)).astype(BF16).astype(F32)
+def gate_kernel(own_ref, a_ref, b_ref, c_ref, x_ref, gain_ref, weight_ref, out_ref, one_ref):
+    parts = (own_ref[...] + a_ref[...]) + (b_ref[...] + c_ref[...])
+    one = (x_ref[...] + parts).astype(BF16).astype(F32)
     one_ref[...] = one
     normed = unpacked(one * gain_ref[...]).astype(BF16)
     requests = normed.shape[0]
@@ -344,9 +417,7 @@
         total = total + lax.dot_general(
             units.astype(BF16), tile, LANE_CONTRACT, preferred_element_type=F32
         )
-    packed = jnp.where(low, total[:half], total[half:])
-    for side_at in range(out_ref.shape[0]):
-        out_ref[side_at] = packed
+    out_ref[...] = jnp.where(low, total[:half], total[half:])
 
 
 def next_kernel(
@@ -457,9 +528,7 @@
     cache_block = kv_cache[0]
     requests, local_width = x_rows.shape
     half = requests // 2
-    heads = (HEADS // KVH) * (w_key_value.shape[2] // HD)
     peers = lax.axis_size("row")
-    sides = lax.axis_size("col")
     me = lax.axis_index("row").astype(jnp.int32)
     guide = lax.axis_index("guide").astype(jnp.int32)
 
@@ -468,45 +537,79 @@
         return jnp.concatenate([gain, gain])[None, :]
 
     query_width = w_query.shape[1]
-    depth = query_width // LANES * requests
-    payload = call(
+    line = peers // LINES
+    share = requests // 4
+    column = me // line
+    parity = column % 2
+
+    def quarter_of(source, which):
+        return lax.dynamic_slice_in_dim(source, which * share, share, 0)
+
+    def between(block, partner):
+        pairs = [(i, partner(i // line) % LINES * line + i % line) for i in range(peers)]
+        return lax.ppermute(block, "row", pairs)
+
+    sent = [quarter_of(cache_block, k) for k in (1 - parity, 2 + parity)]
+    x_first, sent, cache_later = lax.optimization_barrier((x_rows, sent, cache_block))
+    caches = [quarter_of(cache_later, k) for k in (parity, 3 - parity)] + [
+        between(sent[0], lambda k: k + 1 - 2 * (k % 2)),
+        between(sent[1], lambda k: k - 1 + 2 * (k % 2)),
+    ]
+    depth = query_width // LANES * half
+    operands = [
+        pltpu.with_memory_space_constraint(operand, pltpu.HBM)
+        for operand in (
+            x_first,
+            attn_gain[None, :],
+            w_query,
+            w_key_value.reshape(2 * local_width, -1),
+        )
+    ]
+    payload = pl.pallas_call(
         start_kernel,
-        shape((peers, depth + SUBLANES, LANES), BF16),
-        x_rows,
-        attn_gain[None, :],
-        w_query,
-        w_key_value.reshape(2 * local_width, -1),
-    )
+        out_shape=shape((peers, depth + SUBLANES, LANES), BF16),
+        in_specs=[pl.BlockSpec(memory_space=pltpu.HBM)] * len(operands),
+        out_specs=pl.BlockSpec(memory_space=pltpu.VMEM),
+        scratch_shapes=[pltpu.VMEM(operand.shape, operand.dtype) for operand in operands]
+        + [pltpu.SemaphoreType.DMA((len(operands),))],
+        compiler_params=pltpu.CompilerParams(vmem_limit_bytes=24 << 20),
+    )(*operands)
     arrived = exchange(payload, "row")
+    my_lengths = jnp.where(
+        parity == 0,
+        jnp.concatenate([length[:share], length[3 * share :]]),
+        length[share : 3 * share],
+    )
     quarter = LANES // 4
     lane = jnp.arange(LANES)
     frequency = ROPE_BASE ** (-2.0 * (lane % quarter).astype(F32) / HD)
-    angles = length.astype(F32)[:, None] * frequency[None, :]
+    angles = my_lengths.astype(F32)[:, None] * frequency[None, :]
     cosine = jnp.cos(angles)
     sine = jnp.where(lane % (2 * quarter) < quarter, -1.0, 1.0)[None, :] * jnp.sin(angles)
-    flat = requests * heads
+    flat = half * SUBLANES
     partial = call(
         attention_kernel,
-        shape((peers, depth + requests, LANES), BF16),
+        shape((peers, depth + SUBLANES, LANES), BF16),
         me[None],
         arrived,
         cosine,
         sine,
-        jnp.repeat(length, heads)[:, None],
-        cache_block,
-        scratch=[pltpu.VMEM((flat, LANES), F32), pltpu.VMEM((flat, LANES), F32)],
+        jnp.repeat(my_lengths, SUBLANES)[:, None],
+        *caches,
+        scratch=[
+            pltpu.VMEM((flat, LANES), F32),
+            pltpu.VMEM((flat, LANES), F32),
+        ],
         scalars=1,
     )
     arrived = exchange(partial, "row")
-    packed_sums = call(
-        combine_kernel, shape((sides, half, LANES), F32), arrived, w_out.T
-    )
-    arrived = exchange(packed_sums, "col")
+    out_part = call(combine_kernel, shape((half, LANES), F32), arrived, w_out.T)
     x_packed = jnp.concatenate([x_rows[:half], x_rows[half:]], axis=1).astype(F32)
     payload, one_packed = call(
         gate_kernel,
         (shape((peers, requests + SUBLANES, LANES), BF16), shape((half, LANES), F32)),
-        arrived,
+        out_part,
+        *from_others(out_part, "col"),
         x_packed,
         doubled(mlp_gain),
         w_gate_up.reshape(local_width, -1),
@@ -514,9 +617,9 @@
     arrived = exchange(payload, "row")
     active = call(activation_kernel, shape((peers, half, LANES), BF16), arrived)
     arrived = exchange(active, "row")
-    packed_sums = call(down_kernel, shape((sides, half, LANES), F32), arrived, w_down.T)
-    arrived = exchange(packed_sums, "col")
-    residual_two = (one_packed + jnp.sum(arrived, axis=0)).astype(BF16)
+    down_part = call(down_kernel, shape((half, LANES), F32), arrived, w_down.T)
+    a, b, c = from_others(down_part, "col")
+    residual_two = (one_packed + ((down_part + a) + (b + c))).astype(BF16)
     other_two = partner_2(residual_two, "guide", 0)
     payload, head_input = call(
         next_kernel,
@@ -542,9 +645,9 @@
     )
     my_guidance = lax.dynamic_slice_in_dim(guidance, guide * half, half, 0)[:, None]
     vocabulary = w_head.shape[1]
-    share = vocabulary // peers
-    window = (share + 2 * LANES - 2) // LANES * LANES
-    starts = [share * k // LANES * LANES for k in range(peers)]
+    part = vocabulary // peers
+    window = (part + 2 * LANES - 2) // LANES * LANES
+    starts = [part * k // LANES * LANES for k in range(peers)]
     payload = call(
         functools.partial(guided_kernel, starts=starts, window=window),
         shape((peers, half, window + LANES), BF16),
@@ -555,11 +658,11 @@
         scalars=1,
     )
     arrived = exchange(payload, "row")
-    shift = (window - share * me % LANES) % window
+    shift = (window - part * me % LANES) % window
     guided, next_query, next_pairs = call(
         functools.partial(finish_kernel, window=window),
         (
-            shape((half, share), F32),
+            shape((half, part), F32),
             shape((requests, query_width), BF16),
             shape((2 * requests, LANES), BF16),
         ),

time: 158 us -> 139 us (0.88)
  waiting for transfers between devices: 84.6 us -> 66.8 us
  local copies, waits for them, and re-layouts: 5.35 us -> 3.55 us
    all_to_all x7 -> x5, waiting for transfers between devices: 83.7 us -> 58.8 us  [exchange(): return lax.all_to_all(x, axis, 0, 0, tiled=True)]
    ppermute x0 -> x8, starting transfers between devices: none -> 11.4 us  [the longest x6 7.78 us: from_others(): lax.ppermute(x, axis, [(i, (i + k) % n) for i in range(n)])]
    all_to_all x7 -> x5, starting transfers between devices: 37.2 us -> 27.2 us  [exchange(): return lax.all_to_all(x, axis, 0, 0, tiled=True)]
    ppermute x0 -> x8, waiting for transfers between devices: none -> 7.05 us  [the longest x6 7.05 us: from_others(): lax.ppermute(x, axis, [(i, (i + k) % n) for i in range(n)])]
    unnamed x33 -> x23, local copies, waits for them, and re-layouts: 4.38 us -> 0.21 us
    pallas_call x9 -> x8, Pallas kernels: 10.1 us -> 7.35 us  [call(): pl.pallas_call(body, out_shape=outs, in_specs=specs, out_specs=out_specs,...]
    dynamic_slice x0 -> x2, local copies, waits for them, and re-layouts: none -> 2.22 us  [quarter_of(): return lax.dynamic_slice_in_dim(source, which * share, share, 0)]
    pallas_call x0 -> x1, Pallas kernels: none -> 1.96 us  [local(): pl.pallas_call(start_kernel, out_shape=shape((peers, depth + SUBLANES, LA...]
  transfers between devices with their start and end apart: 8 -> 14, of which waited for: 8 -> 11; matrix products, arithmetic and copies ran while one was open for 3% -> 5% of each run, Pallas kernels for 0% -> 1%
where the time goes in v3:
time: 139 us; the launch traced here: 138 us
  waiting for transfers between devices  66.8 us (48%)
  starting transfers between devices  38.7 us (28%)
  blocking collectives  14.8 us (11%)
  Pallas kernels  9.31 us (7%)
  local copies, waits for them, and re-layouts  3.55 us (3%)
  matrix products  2.82 us (2%)
    all_to_all x5, waiting for transfers between devices, exchange(): return lax.all_to_all(x, axis, 0, 0, tiled=True)  58.8 us
    all_to_all x5, starting transfers between devices, exchange(): return lax.all_to_all(x, axis, 0, 0, tiled=True)  27.2 us
    all_to_all x1, blocking collectives, exchange(): return lax.all_to_all(x, axis, 0, 0, tiled=True)  14.8 us
    ppermute x6, starting transfers between devices, from_others(): lax.ppermute(x, axis, [(i, (i + k) % n) for i in range(n)])  7.78 us
    pallas_call x8, Pallas kernels, call(): pl.pallas_call(body, out_shape=outs, in_specs=specs, out_specs=out_specs,...  7.35 us
    ppermute x6, waiting for transfers between devices, from_others(): lax.ppermute(x, axis, [(i, (i + k) % n) for i in range(n)])  7.05 us
    ppermute x2, starting transfers between devices, between(): return lax.ppermute(block, 'row', pairs)  3.67 us
    dot_general x1, matrix products, local(): head_part = jnp.dot(head_input, w_head, preferred_element_type=F32)  2.82 us
  transfers between devices with their start and end apart: 14, of which 11 were waited for; matrix products, arithmetic and copies ran while one was open for 5% of the time, Pallas kernels for 1%

profile of v3, /device:TPU:32, one launch (start us, length us, event | category | flops | bytes accessed | tf_op | source)
XLA Modules:
  0.0 138.2 jit_solution(10438479215415816713)
XLA Ops:
  0.8 1.2 dynamic-slice_bitcast_fusion
  1.9 1.6 %collective-permute-start = (bf16[4,2,128,128]{3,2,1,0:T(8,128)(2,1)S(1)}, bf16[4,2,128,128]{3,2,1,0:T(8,128)(2,1)S(1)}, u32[]{:S(2)}, u32[]{:S(2)}) collective-permute-start(bf16[4,2,128,128]{3,2,1,0:T(8,128)(2,1)S(1)} %get-tuple-element.16), channel_id=1, source_target_pairs={{0,32},{4,36},{8,40},{12,44},{16,48},{20,52},{24,56},{28,60},{32,0... | collective-permute-start | bytes 786440 | tf_op jit(solution)/shard_map/ppermute | solution.py:550
  3.5 2.1 %collective-permute-start.1 = (bf16[4,2,128,128]{3,2,1,0:T(8,128)(2,1)S(1)}, bf16[4,2,128,128]{3,2,1,0:T(8,128)(2,1)S(1)}, u32[]{:S(2)}, u32[]{:S(2)}) collective-permute-start(bf16[4,2,128,128]{3,2,1,0:T(8,128)(2,1)S(1)} %get-tuple-element.17), channel_id=1, source_target_pairs={{0,96},{4,100},{8,104},{12,108},{16,112},{20,116},{24,120},{28,124... | collective-permute-start | bytes 786440 | tf_op jit(solution)/shard_map/ppermute | solution.py:550
  5.6 2.0 %shard_map.184 = bf16[32,40,128]{2,1,0:T(8,128)(2,1)} custom-call(bf16[16,64]{1,0:T(8,128)(2,1)} %bitcast.55, bf16[1,64]{1,0:T(2,128)(2,1)} %bitcast.56, bf16[64,512]{1,0:T(8,128)(2,1)} %query_hbm.1, bf16[128,128]{1,0:T(8,128)(2,1)} %bitcast.54), custom_call_target="tpu_custom_call" | custom-call | tf_op jit(solution)/shard_map/pallas_call | solution.py:568
  7.6 9.3 %all-to-all-start = ((bf16[32,40,128]{2,1,0:T(8,128)(2,1)}), bf16[32,40,128]{2,1,0:T(8,128)(2,1)S(1)}, u32[]{:S(2)}, u32[]{:S(2)}) async-start(bf16[32,40,128]{2,1,0:T(8,128)(2,1)} %shard_map.184), calls=%async_computation | async-start | bytes 655360 | tf_op jit(solution)/shard_map/all_to_all | solution.py:29
  16.9 0.8 slice_bitcast_fusion.3
  17.7 1.1 constant_dynamic-slice_fusion
  18.8 0.7 fusion.7
  19.8 10.1 %all-to-all-done.in_ref = bf16[32,40,128]{2,1,0:T(8,128)(2,1)S(1)} async-done(((bf16[32,40,128]{2,1,0:T(8,128)(2,1)}), bf16[32,40,128]{2,1,0:T(8,128)(2,1)S(1)}, u32[]{:S(2)}, u32[]{:S(2)}) %all-to-all-start) | async-done | bytes 327712 | tf_op jit(solution)/shard_map/all_to_all | solution.py:29
  30.0 1.7 %shard_map.185 = bf16[32,40,128]{2,1,0:T(8,128)(2,1)} custom-call(s32[1]{0:T(128)} %bitcast.1.me_ref, bf16[32,40,128]{2,1,0:T(8,128)(2,1)S(1)} %all-to-all-done.in_ref, f32[8,128]{1,0:T(8,128)S(1)} %get-tuple-element.34.cos_ref, f32[8,128]{1,0:T(8,128)S(1)} %get-tuple-element.33.sin_ref, s32[64,1]{1,0:T(8,128)S(1)} %broadcast_in_dim_reshape.4.length_ref, ...), custom_call_target="tpu_custom_call" | custom-call | tf_op jit(solution)/shard_map/pallas_call | solution.py:45
  31.6 4.7 %all-to-all-start.1 = ((bf16[32,40,128]{2,1,0:T(8,128)(2,1)}), bf16[32,40,128]{2,1,0:T(8,128)(2,1)S(1)}, u32[]{:S(2)}, u32[]{:S(2)}) async-start(bf16[32,40,128]{2,1,0:T(8,128)(2,1)} %shard_map.185), calls=%async_computation.1 | async-start | bytes 655360 | tf_op jit(solution)/shard_map/all_to_all | solution.py:29
  36.4 12.2 %all-to-all-done.1.in_ref = bf16[32,40,128]{2,1,0:T(8,128)(2,1)S(1)} async-done(((bf16[32,40,128]{2,1,0:T(8,128)(2,1)}), bf16[32,40,128]{2,1,0:T(8,128)(2,1)S(1)}, u32[]{:S(2)}, u32[]{:S(2)}) %all-to-all-start.1) | async-done | bytes 327712 | tf_op jit(solution)/shard_map/all_to_all | solution.py:29
  49.2 3.0 %collective-permute-start.4 = (f32[8,128]{1,0:T(8,128)S(1)}, f32[8,128]{1,0:T(8,128)S(1)}, u32[]{:S(2)}, u32[]{:S(2)}) collective-permute-start(f32[8,128]{1,0:T(8,128)S(1)} %shard_map.186.own_ref), channel_id=1, source_target_pairs={{0,3},{1,0},{2,1},{3,2},{4,7},{5,4},{6,5},{7,6},{8,11},{9,8},{10,9... | collective-permute-start | bytes 12296 | tf_op jit(solution)/shard_map/ppermute | solution.py:38
  52.9 1.0 collective-permute-start.2
  54.1 3.3 %collective-permute-done.3.b_ref = f32[8,128]{1,0:T(8,128)S(1)} collective-permute-done((f32[8,128]{1,0:T(8,128)S(1)}, f32[8,128]{1,0:T(8,128)S(1)}, u32[]{:S(2)}, u32[]{:S(2)}) %collective-permute-start.3) | collective-permute-done | bytes 4128 | tf_op jit(solution)/shard_map/ppermute | solution.py:38
  58.0 14.8 %all_to_all.30.in_ref = bf16[32,24,128]{2,1,0:T(8,128)(2,1)S(1)} all-to-all(bf16[32,24,128]{2,1,0:T(8,128)(2,1)S(1)} %get-tuple-element.19), channel_id=1, replica_groups=mesh['guide'=2,'row'=32,'col'=4] {'row'}, dimensions={0} | all-to-all | bytes 393216 | tf_op jit(solution)/shard_map/all_to_all | solution.py:29
  72.8 0.9 shard_map.188
  73.7 4.3 %all-to-all-start.3 = ((bf16[32,8,128]{2,1,0:T(8,128)(2,1)}), bf16[32,8,128]{2,1,0:T(8,128)(2,1)S(1)}, u32[]{:S(2)}, u32[]{:S(2)}) async-start(bf16[32,8,128]{2,1,0:T(8,128)(2,1)} %shard_map.188), calls=%async_computation.3 | async-start | bytes 131072 | tf_op jit(solution)/shard_map/all_to_all | solution.py:29
  78.2 8.9 %all-to-all-done.3.in_ref = bf16[32,8,128]{2,1,0:T(8,128)(2,1)S(1)} async-done(((bf16[32,8,128]{2,1,0:T(8,128)(2,1)}), bf16[32,8,128]{2,1,0:T(8,128)(2,1)S(1)}, u32[]{:S(2)}, u32[]{:S(2)}) %all-to-all-start.3) | async-done | bytes 65568 | tf_op jit(solution)/shard_map/all_to_all | solution.py:29
  87.9 1.4 %collective-permute-start.6 = (f32[8,128]{1,0:T(8,128)S(1)}, f32[8,128]{1,0:T(8,128)S(1)}, u32[]{:S(2)}, u32[]{:S(2)}) collective-permute-start(f32[8,128]{1,0:T(8,128)S(1)} %shard_map.189), channel_id=1, source_target_pairs={{0,2},{1,3},{2,0},{3,1},{4,6},{5,7},{6,4},{7,5},{8,10},{9,11},{10,... | collective-permute-start | bytes 12296 | tf_op jit(solution)/shard_map/ppermute | solution.py:38
  89.3 1.3 collective-permute-start.5
  91.1 1.9 %collective-permute-done.6 = f32[8,128]{1,0:T(8,128)S(1)} collective-permute-done((f32[8,128]{1,0:T(8,128)S(1)}, f32[8,128]{1,0:T(8,128)S(1)}, u32[]{:S(2)}, u32[]{:S(2)}) %collective-permute-start.6) | collective-permute-done | bytes 4128 | tf_op jit(solution)/shard_map/ppermute | solution.py:38
  93.0 1.1 collective-permute-done.5
  94.3 1.0 collective-permute-done.8.other_ref
  95.3 1.0 shard_map.190
  96.3 4.6 %all-to-all-start.4 = ((bf16[32,16,128]{2,1,0:T(8,128)(2,1)}), bf16[32,16,128]{2,1,0:T(8,128)(2,1)S(1)}, u32[]{:S(2)}, u32[]{:S(2)}) async-start(bf16[32,16,128]{2,1,0:T(8,128)(2,1)} %get-tuple-element.20), calls=%async_computation.4 | async-start | bytes 262144 | tf_op jit(solution)/shard_map/all_to_all | solution.py:29
  100.9 2.8 %fusion.8.head_ref = f32[16,32064]{1,0:T(8,128)S(1)} fusion(bf16[16,64]{1,0:T(8,128)(2,1)S(1)} %get-tuple-element.21, bf16[64,32064]{1,0:T(8,128)(2,1)} %param.28), kind=kOutput, calls=%fused_computation.31 | convolution fusion | flops 65667072 | bytes 6158336 | tf_op jit(solution)/shard_map/dot_general | solution.py:637
  103.8 7.7 %all-to-all-done.4.in_ref = bf16[32,16,128]{2,1,0:T(8,128)(2,1)S(1)} async-done(((bf16[32,16,128]{2,1,0:T(8,128)(2,1)}), bf16[32,16,128]{2,1,0:T(8,128)(2,1)S(1)}, u32[]{:S(2)}, u32[]{:S(2)}) %all-to-all-start.4) | async-done | bytes 131104 | tf_op jit(solution)/shard_map/all_to_all | solution.py:29
  111.4 1.7 %shard_map.191 = bf16[32,8,1280]{2,1,0:T(8,128)(2,1)} custom-call(s32[2]{0:T(128)S(1)} %pad_add_fusion.spot_ref, bf16[32,16,128]{2,1,0:T(8,128)(2,1)S(1)} %all-to-all-done.4.in_ref, f32[8,1]{1,0:T(8,128)S(1)} %copy.23.guidance_ref, f32[16,32064]{1,0:T(8,128)S(1)} %fusion.8.head_ref), custom_call_target="tpu_custom_call" | custom-call | tf_op jit(solution)/shard_map/pallas_call | solution.py:45
  113.1 4.3 %all-to-all-start.5 = ((bf16[32,8,1280]{2,1,0:T(8,128)(2,1)}), bf16[32,8,1280]{2,1,0:T(8,128)(2,1)S(1)}, u32[]{:S(2)}, u32[]{:S(2)}) async-start(bf16[32,8,1280]{2,1,0:T(8,128)(2,1)} %shard_map.191), calls=%async_computation.5 | async-start | bytes 1310720 | tf_op jit(solution)/shard_map/all_to_all | solution.py:29
  117.5 19.9 %all-to-all-done.5.in_ref = bf16[32,8,1280]{2,1,0:T(8,128)(2,1)S(1)} async-done(((bf16[32,8,1280]{2,1,0:T(8,128)(2,1)}), bf16[32,8,1280]{2,1,0:T(8,128)(2,1)S(1)}, u32[]{:S(2)}, u32[]{:S(2)}) %all-to-all-start.5) | async-done | bytes 655392 | tf_op jit(solution)/shard_map/all_to_all | solution.py:29
  137.4 0.8 shard_map.192
  (47 shorter events, 4.2 us)
Async XLA Ops:
  0.6 35.7 %copy-start.5 = (bf16[1,16,64]{2,1,0:T(8,128)(2,1)S(1)}, bf16[1,16,64]{2,1,0:T(8,128)(2,1)}, u32[]{:S(2)}) copy-start(bf16[1,16,64]{2,1,0:T(8,128)(2,1)} %param.17) | copy-start | bytes 6148
  0.6 48.0 %copy-start.1 = (bf16[512,64]{0,1:T(8,128)(2,1)S(1)}, bf16[512,64]{0,1:T(8,128)(2,1)}, u32[]{:S(2)}) copy-start(bf16[512,64]{0,1:T(8,128)(2,1)} %param.23) | copy-start | bytes 196612
  0.7 53.2 %copy-start.8 = (bf16[64]{0:T(256)(128)(2,1)S(1)}, bf16[64]{0:T(256)(128)(2,1)}, u32[]{:S(2)}) copy-start(bf16[64]{0:T(256)(128)(2,1)} %param.24) | copy-start | bytes 388
  0.7 53.3 %copy-start.4 = (bf16[64,2,2048]{2,1,0:T(2,128)(2,1)S(1)}, bf16[64,2,2048]{2,1,0:T(2,128)(2,1)}, u32[]{:S(2)}) copy-start(bf16[64,2,2048]{2,1,0:T(2,128)(2,1)} %param.25) | copy-start | bytes 1572868
  0.7 77.3 %copy-start.6 = (bf16[64]{0:T(256)(128)(2,1)S(1)}, bf16[64]{0:T(256)(128)(2,1)}, u32[]{:S(2)}) copy-start(bf16[64]{0:T(256)(128)(2,1)} %param.27) | copy-start | bytes 388
  0.7 77.3 %copy-start.7 = (bf16[64]{0:T(256)(128)(2,1)S(1)}, bf16[64]{0:T(256)(128)(2,1)}, u32[]{:S(2)}) copy-start(bf16[64]{0:T(256)(128)(2,1)} %param.29) | copy-start | bytes 388
  0.7 77.3 %copy-start.9 = (f32[4]{0:T(128)S(1)}, f32[4]{0:T(128)}, u32[]{:S(2)}) copy-start(f32[4]{0:T(128)} %param.33) | copy-start | bytes 52
  0.7 77.3 %copy-start.10 = (s32[16]{0:T(128)S(1)}, s32[16]{0:T(128)}, u32[]{:S(2)}) copy-start(s32[16]{0:T(128)} %param.32) | copy-start | bytes 196
  0.8 86.3 %copy-start = (bf16[2048,64]{0,1:T(8,128)(2,1)S(1)}, bf16[2048,64]{0,1:T(8,128)(2,1)}, u32[]{:S(2)}) copy-start(bf16[2048,64]{0,1:T(8,128)(2,1)} %param.26) | copy-start | bytes 786436
  1.9 93.4 %copy-start.2 = (bf16[64,512]{1,0:T(8,128)(2,1)S(1)}, bf16[64,512]{1,0:T(8,128)(2,1)}, u32[]{:S(2)}) copy-start(bf16[64,512]{1,0:T(8,128)(2,1)} %query_ref.1) | copy-start | bytes 196612
  1.9 93.4 %copy-start.3 = (bf16[64,2,128]{2,1,0:T(2,128)(2,1)S(1)}, bf16[64,2,128]{2,1,0:T(2,128)(2,1)}, u32[]{:S(2)}) copy-start(bf16[64,2,128]{2,1,0:T(2,128)(2,1)} %param.31) | copy-start | bytes 98308
  1.9 17.9 %collective-permute-start = (bf16[4,2,128,128]{3,2,1,0:T(8,128)(2,1)S(1)}, bf16[4,2,128,128]{3,2,1,0:T(8,128)(2,1)S(1)}, u32[]{:S(2)}, u32[]{:S(2)}) collective-permute-start(bf16[4,2,128,128]{3,2,1,0:T(8,128)(2,1)S(1)} %get-tuple-element.16), channel_id=1, source_target_pairs={{0,32},{4,36},{8,40},{12,44},{16,48},{20,52},{24,56},{28,60},{32,0... | collective-permute-start | bytes 786440 | tf_op jit(solution)/shard_map/ppermute | solution.py:550
  3.5 16.3 %collective-permute-start.1 = (bf16[4,2,128,128]{3,2,1,0:T(8,128)(2,1)S(1)}, bf16[4,2,128,128]{3,2,1,0:T(8,128)(2,1)S(1)}, u32[]{:S(2)}, u32[]{:S(2)}) collective-permute-start(bf16[4,2,128,128]{3,2,1,0:T(8,128)(2,1)S(1)} %get-tuple-element.17), channel_id=1, source_target_pairs={{0,96},{4,100},{8,104},{12,108},{16,112},{20,116},{24,120},{28,124... | collective-permute-start | bytes 786440 | tf_op jit(solution)/shard_map/ppermute | solution.py:550
  7.6 22.4 %all-to-all-start = ((bf16[32,40,128]{2,1,0:T(8,128)(2,1)}), bf16[32,40,128]{2,1,0:T(8,128)(2,1)S(1)}, u32[]{:S(2)}, u32[]{:S(2)}) async-start(bf16[32,40,128]{2,1,0:T(8,128)(2,1)} %shard_map.184), calls=%async_computation | async-start | bytes 655360 | tf_op jit(solution)/shard_map/all_to_all | solution.py:29
  31.6 17.0 %all-to-all-start.1 = ((bf16[32,40,128]{2,1,0:T(8,128)(2,1)}), bf16[32,40,128]{2,1,0:T(8,128)(2,1)S(1)}, u32[]{:S(2)}, u32[]{:S(2)}) async-start(bf16[32,40,128]{2,1,0:T(8,128)(2,1)} %shard_map.185), calls=%async_computation.1 | async-start | bytes 655360 | tf_op jit(solution)/shard_map/all_to_all | solution.py:29
  49.2 4.9 %collective-permute-start.4 = (f32[8,128]{1,0:T(8,128)S(1)}, f32[8,128]{1,0:T(8,128)S(1)}, u32[]{:S(2)}, u32[]{:S(2)}) collective-permute-start(f32[8,128]{1,0:T(8,128)S(1)} %shard_map.186.own_ref), channel_id=1, source_target_pairs={{0,3},{1,0},{2,1},{3,2},{4,7},{5,4},{6,5},{7,6},{8,11},{9,8},{10,9... | collective-permute-start | bytes 12296 | tf_op jit(solution)/shard_map/ppermute | solution.py:38
  52.2 5.1 %collective-permute-start.3 = (f32[8,128]{1,0:T(8,128)S(1)}, f32[8,128]{1,0:T(8,128)S(1)}, u32[]{:S(2)}, u32[]{:S(2)}) collective-permute-start(f32[8,128]{1,0:T(8,128)S(1)} %shard_map.186.own_ref), channel_id=1, source_target_pairs={{0,2},{1,3},{2,0},{3,1},{4,6},{5,7},{6,4},{7,5},{8,10},{9,11},{10,... | collective-permute-start | bytes 12296 | tf_op jit(solution)/shard_map/ppermute | solution.py:38
  52.9 4.8 %collective-permute-start.2 = (f32[8,128]{1,0:T(8,128)S(1)}, f32[8,128]{1,0:T(8,128)S(1)}, u32[]{:S(2)}, u32[]{:S(2)}) collective-permute-start(f32[8,128]{1,0:T(8,128)S(1)} %shard_map.186.own_ref), channel_id=1, source_target_pairs={{0,1},{1,2},{2,3},{3,0},{4,5},{5,6},{6,7},{7,4},{8,9},{9,10},{10,1... | collective-permute-start | bytes 12296 | tf_op jit(solution)/shard_map/ppermute | solution.py:38
  73.7 13.4 %all-to-all-start.3 = ((bf16[32,8,128]{2,1,0:T(8,128)(2,1)}), bf16[32,8,128]{2,1,0:T(8,128)(2,1)S(1)}, u32[]{:S(2)}, u32[]{:S(2)}) async-start(bf16[32,8,128]{2,1,0:T(8,128)(2,1)} %shard_map.188), calls=%async_computation.3 | async-start | bytes 131072 | tf_op jit(solution)/shard_map/all_to_all | solution.py:29
  87.5 3.6 %collective-permute-start.7 = (f32[8,128]{1,0:T(8,128)S(1)}, f32[8,128]{1,0:T(8,128)S(1)}, u32[]{:S(2)}, u32[]{:S(2)}) collective-permute-start(f32[8,128]{1,0:T(8,128)S(1)} %shard_map.189), channel_id=1, source_target_pairs={{0,3},{1,0},{2,1},{3,2},{4,7},{5,4},{6,5},{7,6},{8,11},{9,8},{10,9... | collective-permute-start | bytes 12296 | tf_op jit(solution)/shard_map/ppermute | solution.py:38
  87.9 5.1 %collective-permute-start.6 = (f32[8,128]{1,0:T(8,128)S(1)}, f32[8,128]{1,0:T(8,128)S(1)}, u32[]{:S(2)}, u32[]{:S(2)}) collective-permute-start(f32[8,128]{1,0:T(8,128)S(1)} %shard_map.189), channel_id=1, source_target_pairs={{0,2},{1,3},{2,0},{3,1},{4,6},{5,7},{6,4},{7,5},{8,10},{9,11},{10,... | collective-permute-start | bytes 12296 | tf_op jit(solution)/shard_map/ppermute | solution.py:38
  89.3 4.8 %collective-permute-start.5 = (f32[8,128]{1,0:T(8,128)S(1)}, f32[8,128]{1,0:T(8,128)S(1)}, u32[]{:S(2)}, u32[]{:S(2)}) collective-permute-start(f32[8,128]{1,0:T(8,128)S(1)} %shard_map.189), channel_id=1, source_target_pairs={{0,1},{1,2},{2,3},{3,0},{4,5},{5,6},{6,7},{7,4},{8,9},{9,10},{10,1... | collective-permute-start | bytes 12296 | tf_op jit(solution)/shard_map/ppermute | solution.py:38
  94.2 1.2 collective-permute-start.8
  96.3 15.1 %all-to-all-start.4 = ((bf16[32,16,128]{2,1,0:T(8,128)(2,1)}), bf16[32,16,128]{2,1,0:T(8,128)(2,1)S(1)}, u32[]{:S(2)}, u32[]{:S(2)}) async-start(bf16[32,16,128]{2,1,0:T(8,128)(2,1)} %get-tuple-element.20), calls=%async_computation.4 | async-start | bytes 262144 | tf_op jit(solution)/shard_map/all_to_all | solution.py:29
  113.1 24.2 %all-to-all-start.5 = ((bf16[32,8,1280]{2,1,0:T(8,128)(2,1)}), bf16[32,8,1280]{2,1,0:T(8,128)(2,1)S(1)}, u32[]{:S(2)}, u32[]{:S(2)}) async-start(bf16[32,8,1280]{2,1,0:T(8,128)(2,1)} %shard_map.191), calls=%async_computation.5 | async-start | bytes 1310720 | tf_op jit(solution)/shard_map/all_to_all | solution.py:29

commit v4 on v3

--- a/solution.py
+++ b/solution.py
@@ -444,8 +444,9 @@
     high_part, low_part = halves(packed_squares(first) + packed_squares(second, 2 * half))
     side = block_of([high_part, low_part])
     zero = jnp.zeros((half, LANES), F32)
+    line = out_ref.shape[0] // LINES
     for peer in range(out_ref.shape[0]):
-        j, part = divmod(peer, 2)
+        j, part = divmod(peer // line // 2 * line + peer % line, 2)
         piece = tiles[j][part * half : (part + 1) * half] if j < len(tiles) else zero
         out_ref[peer] = jnp.concatenate([piece, side], axis=0).astype(BF16)
     width = LANES // 2
@@ -456,9 +457,44 @@
     head_ref[...] = jnp.concatenate(both, axis=0).astype(BF16)
 
 
-def guided_kernel(spot_ref, in_ref, guidance_ref, head_ref, out_ref, *, starts, window):
+def windows_of(parity, starts):
+    line = len(starts) // LINES
+    return [start for peer, start in enumerate(starts) if peer // line % 2 == parity]
+
+
+def window_rows(ref, wide_ref, rows, start, width):
+    origin = start // LANES * LANES
+    wide = wide_ref.shape[1]
+    stop = min(origin + wide, ref.shape[1])
+    value = ref[rows, origin:stop]
+    if stop - origin < wide:
+        wide_ref[...] = jnp.zeros(wide_ref.shape, F32)
+        wide_ref[:, 0 : stop - origin] = value
+        value = wide_ref[...]
+    return pltpu.roll(value, (wide - start + origin) % wide, 1)[:, :width]
+
+
+def share_kernel(spot_ref, head_ref, cond_ref, plain_ref, wide_ref, *, starts):
+    parity = spot_ref[0]
+    half = head_ref.shape[0] // 2
+    width = cond_ref.shape[2]
+
+    def write(sent):
+        for slot, start in enumerate(windows_of(sent, starts)):
+            for k, ref in enumerate((cond_ref, plain_ref)):
+                rows = slice(k * half, (k + 1) * half)
+                ref[slot] = window_rows(head_ref, wide_ref, rows, start, width).astype(BF16)
+
+    pl.when(parity == 0)(lambda: write(1))
+    pl.when(parity != 0)(lambda: write(0))
+
+
+def guided_kernel(
+    spot_ref, in_ref, guidance_ref, head_ref, cond_ref, plain_ref, out_ref, wide_ref, *, starts
+):
     me = spot_ref[0]
     guide = spot_ref[1]
+    parity = spot_ref[2]
     total = summed(in_ref)
     half = SUBLANES
     scale_row = norm_scale(total[half : half + 1] + total[half + 1 : half + 2])
@@ -471,22 +507,26 @@
     first = guidance * scales(guide * half)
     second = (1.0 - guidance) * scales(2 * half + guide * half)
     piece = (total[:half] * scales(2 * half * guide + me % 2 * half)).astype(BF16)
-    vocabulary = head_ref.shape[1]
-    for peer, start in enumerate(starts):
-        stop = min(start + window, vocabulary)
-        part = first * head_ref[0:half, start:stop] + second * head_ref[half : 2 * half, start:stop]
-        if stop - start < window:
-            out_ref[peer, :, window - LANES : window] = jnp.zeros((half, LANES), BF16)
-        out_ref[peer, :, 0 : stop - start] = part.astype(BF16)
-        out_ref[peer, :, window : window + LANES] = piece
-
-
-def finish_kernel(spot_ref, in_ref, guided_ref, query_ref, pair_ref, total_ref, pairs_ref, *, window):
-    shift = spot_ref[0]
+    width = cond_ref.shape[2]
+
+    def write(kept):
+        for slot, start in enumerate(windows_of(kept, starts)):
+            cond = window_rows(head_ref, wide_ref, slice(0, half), start, width)
+            plain = window_rows(head_ref, wide_ref, slice(half, 2 * half), start, width)
+            cond = cond + cond_ref[slot].astype(F32)
+            plain = plain + plain_ref[slot].astype(F32)
+            out_ref[slot, :, 0:width] = (first * cond + second * plain).astype(BF16)
+            out_ref[slot, :, width : width + LANES] = piece
+
+    pl.when(parity == 0)(lambda: write(0))
+    pl.when(parity != 0)(lambda: write(1))
+
+
+def finish_kernel(in_ref, guided_ref, query_ref, pair_ref, pairs_ref):
+    window = in_ref.shape[2] - LANES
     total = in_ref[0, :, 0:window].astype(F32)
     for peer in range(1, in_ref.shape[0]):
         total = total + in_ref[peer, :, 0:window].astype(F32)
-    total = pltpu.roll(total, shift, 1)
     guided_ref[...] = total[:, : guided_ref.shape[1]]
     tiles = query_ref.shape[1] // LANES
     half = in_ref.shape[1]
@@ -545,6 +585,12 @@
     def quarter_of(source, which):
         return lax.dynamic_slice_in_dim(source, which * share, share, 0)
 
+    def nearer(k):
+        return k + 1 - 2 * (k % 2)
+
+    def farther(k):
+        return k - 1 + 2 * (k % 2)
+
     def between(block, partner):
         pairs = [(i, partner(i // line) % LINES * line + i % line) for i in range(peers)]
         return lax.ppermute(block, "row", pairs)
@@ -552,8 +598,8 @@
     sent = [quarter_of(cache_block, k) for k in (1 - parity, 2 + parity)]
     x_first, sent, cache_later = lax.optimization_barrier((x_rows, sent, cache_block))
     caches = [quarter_of(cache_later, k) for k in (parity, 3 - parity)] + [
-        between(sent[0], lambda k: k + 1 - 2 * (k % 2)),
-        between(sent[1], lambda k: k - 1 + 2 * (k % 2)),
+        between(sent[0], nearer),
+        between(sent[1], farther),
     ]
     depth = query_width // LANES * half
     operands = [
@@ -646,30 +692,41 @@
     my_guidance = lax.dynamic_slice_in_dim(guidance, guide * half, half, 0)[:, None]
     vocabulary = w_head.shape[1]
     part = vocabulary // peers
-    window = (part + 2 * LANES - 2) // LANES * LANES
-    starts = [part * k // LANES * LANES for k in range(peers)]
+    width = (part + LANES - 1) // LANES * LANES
+    starts = [part * k for k in range(peers)]
+    wide = pltpu.VMEM((half, width + LANES), F32)
+    members = peers // 2
+    cond_sent, plain_sent = call(
+        functools.partial(share_kernel, starts=starts),
+        (shape((members, half, width), BF16), shape((members, half, width), BF16)),
+        parity[None],
+        head_part,
+        scratch=[wide],
+        scalars=1,
+    )
     payload = call(
-        functools.partial(guided_kernel, starts=starts, window=window),
-        shape((peers, half, window + LANES), BF16),
-        jnp.stack([me, guide]),
+        functools.partial(guided_kernel, starts=starts),
+        shape((members, half, width + LANES), BF16),
+        jnp.stack([me, guide, parity]),
         arrived,
         my_guidance,
         head_part,
+        between(cond_sent, nearer),
+        between(plain_sent, farther),
+        scratch=[wide],
         scalars=1,
     )
-    arrived = exchange(payload, "row")
-    shift = (window - part * me % LANES) % window
+    groups = [[i for i in range(peers) if i // line % 2 == k] for k in range(2)]
+    arrived = lax.all_to_all(payload, "row", 0, 0, axis_index_groups=groups, tiled=True)
     guided, next_query, next_pairs = call(
-        functools.partial(finish_kernel, window=window),
+        finish_kernel,
         (
             shape((half, part), F32),
             shape((requests, query_width), BF16),
             shape((2 * requests, LANES), BF16),
         ),
-        shift[None],
         arrived,
-        scratch=[pltpu.VMEM((half, window), F32), pltpu.VMEM((2 * requests, LANES), F32)],
-        scalars=1,
+        scratch=[pltpu.VMEM((2 * requests, LANES), F32)],
     )
     return (guided, next_query[None], next_pairs.reshape(1, requests, 2, LANES))
 

time: 139 us -> 135 us (0.971)
  blocking collectives: 14.8 us -> 46.9 us
  waiting for transfers between devices: 66.8 us -> 37.5 us
  starting transfers between devices: 38.7 us -> 33.8 us
    all_to_all x5 -> x3, waiting for transfers between devices: 58.8 us -> 25.7 us  [exchange(): return lax.all_to_all(x, axis, 0, 0, tiled=True)]
    all_to_all x0 -> x1, blocking collectives: none -> 18.9 us  [local(): lax.all_to_all(payload, 'row', 0, 0, axis_index_groups=groups, tiled=True)]
    all_to_all x1 -> x2, blocking collectives: 14.8 us -> 28 us  [exchange(): return lax.all_to_all(x, axis, 0, 0, tiled=True)]
    all_to_all x5 -> x3, starting transfers between devices: 27.2 us -> 18.6 us  [exchange(): return lax.all_to_all(x, axis, 0, 0, tiled=True)]
    ppermute x2 -> x4, starting transfers between devices: 3.67 us -> 7.4 us  [between(): return lax.ppermute(block, 'row', pairs)]
    ppermute x2 -> x4, waiting for transfers between devices: 0.01 us -> 3.59 us  [between(): return lax.ppermute(block, 'row', pairs)]
    pallas_call x8 -> x9, Pallas kernels: 7.35 us -> 6.12 us  [call(): pl.pallas_call(body, out_shape=outs, in_specs=specs, out_specs=out_specs,...]
  transfers between devices with their start and end apart: 14 -> 14, of which waited for: 11 -> 11; matrix products, arithmetic and copies ran while one was open for 5% -> 5% of each run, Pallas kernels for 1% -> 2%
where the time goes in v4:
time: 135 us
  blocking collectives  46.9 us (35%)
  waiting for transfers between devices  37.5 us (28%)
  starting transfers between devices  33.8 us (25%)
  Pallas kernels  8.08 us (6%)
  local copies, waits for them, and re-layouts  3.54 us (3%)
  matrix products  2.83 us (2%)
    all_to_all x2, blocking collectives, exchange(): return lax.all_to_all(x, axis, 0, 0, tiled=True)  28 us
    all_to_all x3, waiting for transfers between devices, exchange(): return lax.all_to_all(x, axis, 0, 0, tiled=True)  25.7 us
    all_to_all x1, blocking collectives, local(): lax.all_to_all(payload, 'row', 0, 0, axis_index_groups=groups, tiled=True)  18.9 us
    all_to_all x3, starting transfers between devices, exchange(): return lax.all_to_all(x, axis, 0, 0, tiled=True)  18.6 us
    ppermute x6, starting transfers between devices, from_others(): lax.ppermute(x, axis, [(i, (i + k) % n) for i in range(n)])  7.78 us
    ppermute x4, starting transfers between devices, between(): return lax.ppermute(block, 'row', pairs)  7.4 us
    ppermute x6, waiting for transfers between devices, from_others(): lax.ppermute(x, axis, [(i, (i + k) % n) for i in range(n)])  7.12 us
    pallas_call x9, Pallas kernels, call(): pl.pallas_call(body, out_shape=outs, in_specs=specs, out_specs=out_specs,...  6.12 us
  transfers between devices with their start and end apart: 14, of which 11 were waited for; matrix products, arithmetic and copies ran while one was open for 5% of the time, Pallas kernels for 2%

profile of v4, /device:TPU:32, one launch (start us, length us, event | category | flops | bytes accessed | tf_op | source)
XLA Modules:
  0.0 134.8 jit_solution(6288587681620725385)
XLA Ops:
  0.7 1.1 dynamic-slice_bitcast_fusion
  1.9 1.6 %collective-permute-start = (bf16[4,2,128,128]{3,2,1,0:T(8,128)(2,1)S(1)}, bf16[4,2,128,128]{3,2,1,0:T(8,128)(2,1)S(1)}, u32[]{:S(2)}, u32[]{:S(2)}) collective-permute-start(bf16[4,2,128,128]{3,2,1,0:T(8,128)(2,1)S(1)} %get-tuple-element.18), channel_id=1, source_target_pairs={{0,32},{4,36},{8,40},{12,44},{16,48},{20,52},{24,56},{28,60},{32,0... | collective-permute-start | bytes 786440 | tf_op jit(solution)/shard_map/ppermute | solution.py:596
  3.5 2.1 %collective-permute-start.1 = (bf16[4,2,128,128]{3,2,1,0:T(8,128)(2,1)S(1)}, bf16[4,2,128,128]{3,2,1,0:T(8,128)(2,1)S(1)}, u32[]{:S(2)}, u32[]{:S(2)}) collective-permute-start(bf16[4,2,128,128]{3,2,1,0:T(8,128)(2,1)S(1)} %get-tuple-element.19), channel_id=1, source_target_pairs={{0,96},{4,100},{8,104},{12,108},{16,112},{20,116},{24,120},{28,124... | collective-permute-start | bytes 786440 | tf_op jit(solution)/shard_map/ppermute | solution.py:596
  5.6 2.0 %shard_map.184 = bf16[32,40,128]{2,1,0:T(8,128)(2,1)} custom-call(bf16[16,64]{1,0:T(8,128)(2,1)} %bitcast.55, bf16[1,64]{1,0:T(2,128)(2,1)} %bitcast.56, bf16[64,512]{1,0:T(8,128)(2,1)} %query_hbm.1, bf16[128,128]{1,0:T(8,128)(2,1)} %bitcast.54), custom_call_target="tpu_custom_call" | custom-call | tf_op jit(solution)/shard_map/pallas_call | solution.py:614
  7.6 9.3 %all-to-all-start = ((bf16[32,40,128]{2,1,0:T(8,128)(2,1)}), bf16[32,40,128]{2,1,0:T(8,128)(2,1)S(1)}, u32[]{:S(2)}, u32[]{:S(2)}) async-start(bf16[32,40,128]{2,1,0:T(8,128)(2,1)} %shard_map.184), calls=%async_computation | async-start | bytes 655360 | tf_op jit(solution)/shard_map/all_to_all | solution.py:29
  16.9 0.8 slice_bitcast_fusion.3
  17.7 1.1 constant_dynamic-slice_fusion
  18.8 0.7 fusion.7
  19.8 10.1 %all-to-all-done.in_ref = bf16[32,40,128]{2,1,0:T(8,128)(2,1)S(1)} async-done(((bf16[32,40,128]{2,1,0:T(8,128)(2,1)}), bf16[32,40,128]{2,1,0:T(8,128)(2,1)S(1)}, u32[]{:S(2)}, u32[]{:S(2)}) %all-to-all-start) | async-done | bytes 327712 | tf_op jit(solution)/shard_map/all_to_all | solution.py:29
  29.9 1.7 %shard_map.185 = bf16[32,40,128]{2,1,0:T(8,128)(2,1)} custom-call(s32[1]{0:T(128)} %bitcast.me_ref, bf16[32,40,128]{2,1,0:T(8,128)(2,1)S(1)} %all-to-all-done.in_ref, f32[8,128]{1,0:T(8,128)S(1)} %get-tuple-element.38.cos_ref, f32[8,128]{1,0:T(8,128)S(1)} %get-tuple-element.37.sin_ref, s32[64,1]{1,0:T(8,128)S(1)} %broadcast_in_dim_reshape.4.length_ref, ...), custom_call_target="tpu_custom_call" | custom-call | tf_op jit(solution)/shard_map/pallas_call | solution.py:45
  31.6 4.7 %all-to-all-start.1 = ((bf16[32,40,128]{2,1,0:T(8,128)(2,1)}), bf16[32,40,128]{2,1,0:T(8,128)(2,1)S(1)}, u32[]{:S(2)}, u32[]{:S(2)}) async-start(bf16[32,40,128]{2,1,0:T(8,128)(2,1)} %shard_map.185), calls=%async_computation.1 | async-start | bytes 655360 | tf_op jit(solution)/shard_map/all_to_all | solution.py:29
  36.4 12.2 %all-to-all-done.1.in_ref = bf16[32,40,128]{2,1,0:T(8,128)(2,1)S(1)} async-done(((bf16[32,40,128]{2,1,0:T(8,128)(2,1)}), bf16[32,40,128]{2,1,0:T(8,128)(2,1)S(1)}, u32[]{:S(2)}, u32[]{:S(2)}) %all-to-all-start.1) | async-done | bytes 327712 | tf_op jit(solution)/shard_map/all_to_all | solution.py:29
  49.2 3.0 %collective-permute-start.4 = (f32[8,128]{1,0:T(8,128)S(1)}, f32[8,128]{1,0:T(8,128)S(1)}, u32[]{:S(2)}, u32[]{:S(2)}) collective-permute-start(f32[8,128]{1,0:T(8,128)S(1)} %shard_map.186.own_ref), channel_id=1, source_target_pairs={{0,3},{1,0},{2,1},{3,2},{4,7},{5,4},{6,5},{7,6},{8,11},{9,8},{10,9... | collective-permute-start | bytes 12296 | tf_op jit(solution)/shard_map/ppermute | solution.py:38
  52.8 1.0 collective-permute-start.2
  54.1 3.3 %collective-permute-done.3.b_ref = f32[8,128]{1,0:T(8,128)S(1)} collective-permute-done((f32[8,128]{1,0:T(8,128)S(1)}, f32[8,128]{1,0:T(8,128)S(1)}, u32[]{:S(2)}, u32[]{:S(2)}) %collective-permute-start.3) | collective-permute-done | bytes 4128 | tf_op jit(solution)/shard_map/ppermute | solution.py:38
  58.0 14.8 %all_to_all.30.in_ref = bf16[32,24,128]{2,1,0:T(8,128)(2,1)S(1)} all-to-all(bf16[32,24,128]{2,1,0:T(8,128)(2,1)S(1)} %get-tuple-element.21), channel_id=1, replica_groups=mesh['guide'=2,'row'=32,'col'=4] {'row'}, dimensions={0} | all-to-all | bytes 393216 | tf_op jit(solution)/shard_map/all_to_all | solution.py:29
  73.0 13.2 %all_to_all.31.in_ref = bf16[32,8,128]{2,1,0:T(8,128)(2,1)S(1)} all-to-all(bf16[32,8,128]{2,1,0:T(8,128)(2,1)S(1)} %shard_map.188), channel_id=1, replica_groups=mesh['guide'=2,'row'=32,'col'=4] {'row'}, dimensions={0} | all-to-all | bytes 131072 | tf_op jit(solution)/shard_map/all_to_all | solution.py:29
  87.1 1.4 %collective-permute-start.6 = (f32[8,128]{1,0:T(8,128)S(1)}, f32[8,128]{1,0:T(8,128)S(1)}, u32[]{:S(2)}, u32[]{:S(2)}) collective-permute-start(f32[8,128]{1,0:T(8,128)S(1)} %shard_map.189), channel_id=1, source_target_pairs={{0,2},{1,3},{2,0},{3,1},{4,6},{5,7},{6,4},{7,5},{8,10},{9,11},{10,... | collective-permute-start | bytes 12296 | tf_op jit(solution)/shard_map/ppermute | solution.py:38
  88.5 1.3 collective-permute-start.5
  90.2 1.9 %collective-permute-done.6 = f32[8,128]{1,0:T(8,128)S(1)} collective-permute-done((f32[8,128]{1,0:T(8,128)S(1)}, f32[8,128]{1,0:T(8,128)S(1)}, u32[]{:S(2)}, u32[]{:S(2)}) %collective-permute-start.6) | collective-permute-done | bytes 4128 | tf_op jit(solution)/shard_map/ppermute | solution.py:38
  92.2 1.1 collective-permute-done.5
  93.4 1.1 collective-permute-done.8.other_ref
  94.5 1.0 shard_map.190
  95.4 4.6 %all-to-all-start.4 = ((bf16[32,16,128]{2,1,0:T(8,128)(2,1)}), bf16[32,16,128]{2,1,0:T(8,128)(2,1)S(1)}, u32[]{:S(2)}, u32[]{:S(2)}) async-start(bf16[32,16,128]{2,1,0:T(8,128)(2,1)} %get-tuple-element.22), calls=%async_computation.4 | async-start | bytes 262144 | tf_op jit(solution)/shard_map/all_to_all | solution.py:29
  100.1 2.8 %fusion.8.head_ref = f32[16,32064]{1,0:T(8,128)S(1)} fusion(bf16[16,64]{1,0:T(8,128)(2,1)S(1)} %get-tuple-element.23, bf16[64,32064]{1,0:T(8,128)(2,1)} %param.28), kind=kOutput, calls=%fused_computation.31 | convolution fusion | flops 65667072 | bytes 6158336 | tf_op jit(solution)/shard_map/dot_general | solution.py:683
  103.2 1.6 %collective-permute-start.9 = (bf16[16,8,1024]{2,1,0:T(8,128)(2,1)S(1)}, bf16[16,8,1024]{2,1,0:T(8,128)(2,1)S(1)}, u32[]{:S(2)}, u32[]{:S(2)}) collective-permute-start(bf16[16,8,1024]{2,1,0:T(8,128)(2,1)S(1)} %get-tuple-element.24), channel_id=1, source_target_pairs={{0,32},{4,36},{8,40},{12,44},{16,48},{20,52},{24,56},{28,60},{32,0... | collective-permute-start | bytes 786440 | tf_op jit(solution)/shard_map/ppermute | solution.py:596
  104.7 2.1 %collective-permute-start.10 = (bf16[16,8,1024]{2,1,0:T(8,128)(2,1)S(1)}, bf16[16,8,1024]{2,1,0:T(8,128)(2,1)S(1)}, u32[]{:S(2)}, u32[]{:S(2)}) collective-permute-start(bf16[16,8,1024]{2,1,0:T(8,128)(2,1)S(1)} %get-tuple-element.25), channel_id=1, source_target_pairs={{0,96},{4,100},{8,104},{12,108},{16,112},{20,116},{24,120},{28,124... | collective-permute-start | bytes 786440 | tf_op jit(solution)/shard_map/ppermute | solution.py:596
  107.2 3.3 %all-to-all-done.4.in_ref = bf16[32,16,128]{2,1,0:T(8,128)(2,1)S(1)} async-done(((bf16[32,16,128]{2,1,0:T(8,128)(2,1)}), bf16[32,16,128]{2,1,0:T(8,128)(2,1)S(1)}, u32[]{:S(2)}, u32[]{:S(2)}) %all-to-all-start.4) | async-done | bytes 131104 | tf_op jit(solution)/shard_map/all_to_all | solution.py:29
  110.5 1.3 collective-permute-done.9.cond_ref
  111.9 2.3 %collective-permute-done.10.plain_ref = bf16[16,8,1024]{2,1,0:T(8,128)(2,1)S(1)} collective-permute-done((bf16[16,8,1024]{2,1,0:T(8,128)(2,1)S(1)}, bf16[16,8,1024]{2,1,0:T(8,128)(2,1)S(1)}, u32[]{:S(2)}, u32[]{:S(2)}) %collective-permute-start.10) | collective-permute-done | bytes 262176 | tf_op jit(solution)/shard_map/ppermute | solution.py:596
  114.1 1.0 shard_map.192
  115.2 18.9 %all_to_all.32.in_ref = bf16[16,8,1152]{2,1,0:T(8,128)(2,1)S(1)} all-to-all(bf16[16,8,1152]{2,1,0:T(8,128)(2,1)S(1)} %shard_map.192), channel_id=1, replica_groups={{0,4,8,12,16,20,24,28,64,68,72,76,80,84,88,92},{32,36,40,44,48,52,56,60..., dimensions={0} | all-to-all | bytes 589824 | tf_op jit(solution)/shard_map/all_to_all | solution.py:720
  (50 shorter events, 5.4 us)
Async XLA Ops:
  0.6 35.6 %copy-start.5 = (bf16[1,16,64]{2,1,0:T(8,128)(2,1)S(1)}, bf16[1,16,64]{2,1,0:T(8,128)(2,1)}, u32[]{:S(2)}) copy-start(bf16[1,16,64]{2,1,0:T(8,128)(2,1)} %param.17) | copy-start | bytes 6148
  0.6 47.9 %copy-start.1 = (bf16[512,64]{0,1:T(8,128)(2,1)S(1)}, bf16[512,64]{0,1:T(8,128)(2,1)}, u32[]{:S(2)}) copy-start(bf16[512,64]{0,1:T(8,128)(2,1)} %param.23) | copy-start | bytes 196612
  0.7 53.2 %copy-start.8 = (bf16[64]{0:T(256)(128)(2,1)S(1)}, bf16[64]{0:T(256)(128)(2,1)}, u32[]{:S(2)}) copy-start(bf16[64]{0:T(256)(128)(2,1)} %param.24) | copy-start | bytes 388
  0.7 53.2 %copy-start.4 = (bf16[64,2,2048]{2,1,0:T(2,128)(2,1)S(1)}, bf16[64,2,2048]{2,1,0:T(2,128)(2,1)}, u32[]{:S(2)}) copy-start(bf16[64,2,2048]{2,1,0:T(2,128)(2,1)} %param.25) | copy-start | bytes 1572868
  0.7 85.5 %copy-start = (bf16[2048,64]{0,1:T(8,128)(2,1)S(1)}, bf16[2048,64]{0,1:T(8,128)(2,1)}, u32[]{:S(2)}) copy-start(bf16[2048,64]{0,1:T(8,128)(2,1)} %param.26) | copy-start | bytes 786436
  1.9 91.4 %copy-start.6 = (bf16[64]{0:T(256)(128)(2,1)S(1)}, bf16[64]{0:T(256)(128)(2,1)}, u32[]{:S(2)}) copy-start(bf16[64]{0:T(256)(128)(2,1)} %param.27) | copy-start | bytes 388
  1.9 91.4 %copy-start.7 = (bf16[64]{0:T(256)(128)(2,1)S(1)}, bf16[64]{0:T(256)(128)(2,1)}, u32[]{:S(2)}) copy-start(bf16[64]{0:T(256)(128)(2,1)} %param.29) | copy-start | bytes 388
  1.9 92.6 %copy-start.2 = (bf16[64,512]{1,0:T(8,128)(2,1)S(1)}, bf16[64,512]{1,0:T(8,128)(2,1)}, u32[]{:S(2)}) copy-start(bf16[64,512]{1,0:T(8,128)(2,1)} %query_ref.1) | copy-start | bytes 196612
  1.9 92.6 %copy-start.3 = (bf16[64,2,128]{2,1,0:T(2,128)(2,1)S(1)}, bf16[64,2,128]{2,1,0:T(2,128)(2,1)}, u32[]{:S(2)}) copy-start(bf16[64,2,128]{2,1,0:T(2,128)(2,1)} %param.31) | copy-start | bytes 98308
  1.9 17.9 %collective-permute-start = (bf16[4,2,128,128]{3,2,1,0:T(8,128)(2,1)S(1)}, bf16[4,2,128,128]{3,2,1,0:T(8,128)(2,1)S(1)}, u32[]{:S(2)}, u32[]{:S(2)}) collective-permute-start(bf16[4,2,128,128]{3,2,1,0:T(8,128)(2,1)S(1)} %get-tuple-element.18), channel_id=1, source_target_pairs={{0,32},{4,36},{8,40},{12,44},{16,48},{20,52},{24,56},{28,60},{32,0... | collective-permute-start | bytes 786440 | tf_op jit(solution)/shard_map/ppermute | solution.py:596
  3.5 16.3 %collective-permute-start.1 = (bf16[4,2,128,128]{3,2,1,0:T(8,128)(2,1)S(1)}, bf16[4,2,128,128]{3,2,1,0:T(8,128)(2,1)S(1)}, u32[]{:S(2)}, u32[]{:S(2)}) collective-permute-start(bf16[4,2,128,128]{3,2,1,0:T(8,128)(2,1)S(1)} %get-tuple-element.19), channel_id=1, source_target_pairs={{0,96},{4,100},{8,104},{12,108},{16,112},{20,116},{24,120},{28,124... | collective-permute-start | bytes 786440 | tf_op jit(solution)/shard_map/ppermute | solution.py:596
  7.6 22.4 %all-to-all-start = ((bf16[32,40,128]{2,1,0:T(8,128)(2,1)}), bf16[32,40,128]{2,1,0:T(8,128)(2,1)S(1)}, u32[]{:S(2)}, u32[]{:S(2)}) async-start(bf16[32,40,128]{2,1,0:T(8,128)(2,1)} %shard_map.184), calls=%async_computation | async-start | bytes 655360 | tf_op jit(solution)/shard_map/all_to_all | solution.py:29
  31.6 17.0 %all-to-all-start.1 = ((bf16[32,40,128]{2,1,0:T(8,128)(2,1)}), bf16[32,40,128]{2,1,0:T(8,128)(2,1)S(1)}, u32[]{:S(2)}, u32[]{:S(2)}) async-start(bf16[32,40,128]{2,1,0:T(8,128)(2,1)} %shard_map.185), calls=%async_computation.1 | async-start | bytes 655360 | tf_op jit(solution)/shard_map/all_to_all | solution.py:29
  49.2 4.9 %collective-permute-start.4 = (f32[8,128]{1,0:T(8,128)S(1)}, f32[8,128]{1,0:T(8,128)S(1)}, u32[]{:S(2)}, u32[]{:S(2)}) collective-permute-start(f32[8,128]{1,0:T(8,128)S(1)} %shard_map.186.own_ref), channel_id=1, source_target_pairs={{0,3},{1,0},{2,1},{3,2},{4,7},{5,4},{6,5},{7,6},{8,11},{9,8},{10,9... | collective-permute-start | bytes 12296 | tf_op jit(solution)/shard_map/ppermute | solution.py:38
  52.2 5.1 %collective-permute-start.3 = (f32[8,128]{1,0:T(8,128)S(1)}, f32[8,128]{1,0:T(8,128)S(1)}, u32[]{:S(2)}, u32[]{:S(2)}) collective-permute-start(f32[8,128]{1,0:T(8,128)S(1)} %shard_map.186.own_ref), channel_id=1, source_target_pairs={{0,2},{1,3},{2,0},{3,1},{4,6},{5,7},{6,4},{7,5},{8,10},{9,11},{10,... | collective-permute-start | bytes 12296 | tf_op jit(solution)/shard_map/ppermute | solution.py:38
  52.8 4.8 %collective-permute-start.2 = (f32[8,128]{1,0:T(8,128)S(1)}, f32[8,128]{1,0:T(8,128)S(1)}, u32[]{:S(2)}, u32[]{:S(2)}) collective-permute-start(f32[8,128]{1,0:T(8,128)S(1)} %shard_map.186.own_ref), channel_id=1, source_target_pairs={{0,1},{1,2},{2,3},{3,0},{4,5},{5,6},{6,7},{7,4},{8,9},{9,10},{10,1... | collective-permute-start | bytes 12296 | tf_op jit(solution)/shard_map/ppermute | solution.py:38
  86.6 3.6 %collective-permute-start.7 = (f32[8,128]{1,0:T(8,128)S(1)}, f32[8,128]{1,0:T(8,128)S(1)}, u32[]{:S(2)}, u32[]{:S(2)}) collective-permute-start(f32[8,128]{1,0:T(8,128)S(1)} %shard_map.189), channel_id=1, source_target_pairs={{0,3},{1,0},{2,1},{3,2},{4,7},{5,4},{6,5},{7,6},{8,11},{9,8},{10,9... | collective-permute-start | bytes 12296 | tf_op jit(solution)/shard_map/ppermute | solution.py:38
  87.1 5.1 %collective-permute-start.6 = (f32[8,128]{1,0:T(8,128)S(1)}, f32[8,128]{1,0:T(8,128)S(1)}, u32[]{:S(2)}, u32[]{:S(2)}) collective-permute-start(f32[8,128]{1,0:T(8,128)S(1)} %shard_map.189), channel_id=1, source_target_pairs={{0,2},{1,3},{2,0},{3,1},{4,6},{5,7},{6,4},{7,5},{8,10},{9,11},{10,... | collective-permute-start | bytes 12296 | tf_op jit(solution)/shard_map/ppermute | solution.py:38
  88.5 4.8 %collective-permute-start.5 = (f32[8,128]{1,0:T(8,128)S(1)}, f32[8,128]{1,0:T(8,128)S(1)}, u32[]{:S(2)}, u32[]{:S(2)}) collective-permute-start(f32[8,128]{1,0:T(8,128)S(1)} %shard_map.189), channel_id=1, source_target_pairs={{0,1},{1,2},{2,3},{3,0},{4,5},{5,6},{6,7},{7,4},{8,9},{9,10},{10,1... | collective-permute-start | bytes 12296 | tf_op jit(solution)/shard_map/ppermute | solution.py:38
  93.3 1.2 collective-permute-start.8
  95.4 15.1 %all-to-all-start.4 = ((bf16[32,16,128]{2,1,0:T(8,128)(2,1)}), bf16[32,16,128]{2,1,0:T(8,128)(2,1)S(1)}, u32[]{:S(2)}, u32[]{:S(2)}) async-start(bf16[32,16,128]{2,1,0:T(8,128)(2,1)} %get-tuple-element.22), calls=%async_computation.4 | async-start | bytes 262144 | tf_op jit(solution)/shard_map/all_to_all | solution.py:29
  100.1 6.8 %copy-start.9 = (f32[4]{0:T(128)S(1)}, f32[4]{0:T(128)}, u32[]{:S(2)}) copy-start(f32[4]{0:T(128)} %param.33) | copy-start | bytes 52
  100.1 6.8 %copy-start.10 = (s32[16]{0:T(128)S(1)}, s32[16]{0:T(128)}, u32[]{:S(2)}) copy-start(s32[16]{0:T(128)} %param.32) | copy-start | bytes 196
  103.2 8.7 %collective-permute-start.9 = (bf16[16,8,1024]{2,1,0:T(8,128)(2,1)S(1)}, bf16[16,8,1024]{2,1,0:T(8,128)(2,1)S(1)}, u32[]{:S(2)}, u32[]{:S(2)}) collective-permute-start(bf16[16,8,1024]{2,1,0:T(8,128)(2,1)S(1)} %get-tuple-element.24), channel_id=1, source_target_pairs={{0,32},{4,36},{8,40},{12,44},{16,48},{20,52},{24,56},{28,60},{32,0... | collective-permute-start | bytes 786440 | tf_op jit(solution)/shard_map/ppermute | solution.py:596
  104.7 9.4 %collective-permute-start.10 = (bf16[16,8,1024]{2,1,0:T(8,128)(2,1)S(1)}, bf16[16,8,1024]{2,1,0:T(8,128)(2,1)S(1)}, u32[]{:S(2)}, u32[]{:S(2)}) collective-permute-start(bf16[16,8,1024]{2,1,0:T(8,128)(2,1)S(1)} %get-tuple-element.25), channel_id=1, source_target_pairs={{0,96},{4,100},{8,104},{12,108},{16,112},{20,116},{24,120},{28,124... | collective-permute-start | bytes 786440 | tf_op jit(solution)/shard_map/ppermute | solution.py:596

commit v5 on v4

--- a/solution.py
+++ b/solution.py
@@ -38,9 +38,10 @@
     return [lax.ppermute(x, axis, [(i, (i + k) % n) for i in range(n)]) for k in range(1, n)]
 
 
-def call(body, outs, *operands, scratch=(), scalars=0):
+def call(body, outs, *operands, scratch=(), scalars=0, in_hbm=0, limit=8 << 20):
     specs = [pl.BlockSpec(memory_space=pltpu.SMEM)] * scalars
-    specs += [pl.BlockSpec(memory_space=pltpu.VMEM)] * (len(operands) - scalars)
+    specs += [pl.BlockSpec(memory_space=pltpu.VMEM)] * (len(operands) - scalars - in_hbm)
+    specs += [pl.BlockSpec(memory_space=pltpu.HBM)] * in_hbm
     out_specs = jax.tree.map(lambda _: pl.BlockSpec(memory_space=pltpu.VMEM), outs)
     return pl.pallas_call(
         body,
@@ -48,7 +49,7 @@
         in_specs=specs,
         out_specs=out_specs,
         scratch_shapes=list(scratch),
-        compiler_params=pltpu.CompilerParams(vmem_limit_bytes=24 << 20),
+        compiler_params=pltpu.CompilerParams(vmem_limit_bytes=limit),
     )(*operands)
 
 
@@ -474,8 +475,29 @@
     return pltpu.roll(value, (wide - start + origin) % wide, 1)[:, :width]
 
 
-def share_kernel(spot_ref, head_ref, cond_ref, plain_ref, wide_ref, *, starts):
+def share_kernel(
+    spot_ref, x_ref, weight_hbm, head_ref, cond_ref, plain_ref, wide_ref, weight_ref, sems, *, starts
+):
     parity = spot_ref[0]
+    vocabulary = weight_ref.shape[1]
+    step = vocabulary // sems.shape[0] // LANES * LANES + LANES
+    cuts = [(start, min(start + step, vocabulary)) for start in range(0, vocabulary, step)]
+    copies = [
+        pltpu.make_async_copy(
+            weight_hbm.at[:, pl.ds(start, stop - start)],
+            weight_ref.at[:, pl.ds(start, stop - start)],
+            sems.at[k],
+        )
+        for k, (start, stop) in enumerate(cuts)
+    ]
+    for copy in copies:
+        copy.start()
+    x = x_ref[...]
+    for copy, (start, stop) in zip(copies, cuts):
+        copy.wait()
+        head_ref[:, start:stop] = jnp.dot(
+            x, weight_ref[:, start:stop], preferred_element_type=F32
+        )
     half = head_ref.shape[0] // 2
     width = cond_ref.shape[2]
 
@@ -618,7 +640,7 @@
         out_specs=pl.BlockSpec(memory_space=pltpu.VMEM),
         scratch_shapes=[pltpu.VMEM(operand.shape, operand.dtype) for operand in operands]
         + [pltpu.SemaphoreType.DMA((len(operands),))],
-        compiler_params=pltpu.CompilerParams(vmem_limit_bytes=24 << 20),
+        compiler_params=pltpu.CompilerParams(vmem_limit_bytes=8 << 20),
     )(*operands)
     arrived = exchange(payload, "row")
     my_lengths = jnp.where(
@@ -680,7 +702,6 @@
         scalars=1,
     )
     arrived = exchange(payload, "row")
-    head_part = jnp.dot(head_input, w_head, preferred_element_type=F32)
     guidance = jnp.sum(
         jnp.where(
             tenant[:, None] == jnp.arange(TENANTS, dtype=jnp.int32)[None, :],
@@ -696,13 +717,20 @@
     starts = [part * k for k in range(peers)]
     wide = pltpu.VMEM((half, width + LANES), F32)
     members = peers // 2
-    cond_sent, plain_sent = call(
+    head_part, cond_sent, plain_sent = call(
         functools.partial(share_kernel, starts=starts),
-        (shape((members, half, width), BF16), shape((members, half, width), BF16)),
+        (
+            shape((requests, vocabulary), F32),
+            shape((members, half, width), BF16),
+            shape((members, half, width), BF16),
+        ),
         parity[None],
-        head_part,
-        scratch=[wide],
+        head_input,
+        pltpu.with_memory_space_constraint(w_head, pltpu.HBM),
+        scratch=[wide, pltpu.VMEM(w_head.shape, BF16), pltpu.SemaphoreType.DMA((4,))],
         scalars=1,
+        in_hbm=1,
+        limit=12 << 20,
     )
     payload = call(
         functools.partial(guided_kernel, starts=starts),

time: 135 us -> 135 us (level)
  matrix products: 2.83 us -> 0 us
  Pallas kernels: 8.08 us -> 10.5 us
    dot_general x1 -> x0, matrix products: 2.83 us -> none  [local(): head_part = jnp.dot(head_input, w_head, preferred_element_type=F32)]
    pallas_call x9, Pallas kernels: 6.12 us -> 8.53 us  [call(): pl.pallas_call(body, out_shape=outs, in_specs=specs, out_specs=out_specs,...]
  transfers between devices with their start and end apart: 14 -> 14, of which waited for: 11 -> 11; matrix products, arithmetic and copies ran while one was open for 5% -> 3% of each run, Pallas kernels for 2% -> 3%
where the time goes in v5:
time: 135 us; the launch traced here: 134 us
  blocking collectives  46.8 us (35%)
  waiting for transfers between devices  37.6 us (28%)
  starting transfers between devices  33.9 us (25%)
  Pallas kernels  10.5 us (8%)
  local copies, waits for them, and re-layouts  3.53 us (3%)
    all_to_all x2, blocking collectives, exchange(): return lax.all_to_all(x, axis, 0, 0, tiled=True)  28 us
    all_to_all x3, waiting for transfers between devices, exchange(): return lax.all_to_all(x, axis, 0, 0, tiled=True)  26.1 us
    all_to_all x1, blocking collectives, local(): lax.all_to_all(payload, 'row', 0, 0, axis_index_groups=groups, tiled=True)  18.8 us
    all_to_all x3, starting transfers between devices, exchange(): return lax.all_to_all(x, axis, 0, 0, tiled=True)  18.7 us
    pallas_call x9, Pallas kernels, call(): pl.pallas_call(body, out_shape=outs, in_specs=specs, out_specs=out_specs,...  8.53 us
    ppermute x6, starting transfers between devices, from_others(): lax.ppermute(x, axis, [(i, (i + k) % n) for i in range(n)])  7.78 us
    ppermute x4, starting transfers between devices, between(): return lax.ppermute(block, 'row', pairs)  7.4 us
    ppermute x6, waiting for transfers between devices, from_others(): lax.ppermute(x, axis, [(i, (i + k) % n) for i in range(n)])  7.12 us
  transfers between devices with their start and end apart: 14, of which 11 were waited for; matrix products, arithmetic and copies ran while one was open for 3% of the time, Pallas kernels for 3%

profile of v5, /device:TPU:32, one launch (start us, length us, event | category | flops | bytes accessed | tf_op | source)
XLA Modules:
  0.0 134.5 jit_solution(11185447968069732111)
XLA Ops:
  0.7 1.1 dynamic-slice_bitcast_fusion
  1.9 1.6 %collective-permute-start = (bf16[4,2,128,128]{3,2,1,0:T(8,128)(2,1)S(1)}, bf16[4,2,128,128]{3,2,1,0:T(8,128)(2,1)S(1)}, u32[]{:S(2)}, u32[]{:S(2)}) collective-permute-start(bf16[4,2,128,128]{3,2,1,0:T(8,128)(2,1)S(1)} %get-tuple-element.19), channel_id=1, source_target_pairs={{0,32},{4,36},{8,40},{12,44},{16,48},{20,52},{24,56},{28,60},{32,0... | collective-permute-start | bytes 786440 | tf_op jit(solution)/shard_map/ppermute | solution.py:618
  3.5 2.1 %collective-permute-start.1 = (bf16[4,2,128,128]{3,2,1,0:T(8,128)(2,1)S(1)}, bf16[4,2,128,128]{3,2,1,0:T(8,128)(2,1)S(1)}, u32[]{:S(2)}, u32[]{:S(2)}) collective-permute-start(bf16[4,2,128,128]{3,2,1,0:T(8,128)(2,1)S(1)} %get-tuple-element.20), channel_id=1, source_target_pairs={{0,96},{4,100},{8,104},{12,108},{16,112},{20,116},{24,120},{28,124... | collective-permute-start | bytes 786440 | tf_op jit(solution)/shard_map/ppermute | solution.py:618
  5.6 2.0 %shard_map.184 = bf16[32,40,128]{2,1,0:T(8,128)(2,1)} custom-call(bf16[16,64]{1,0:T(8,128)(2,1)} %bitcast.53, bf16[1,64]{1,0:T(2,128)(2,1)} %bitcast.54, bf16[64,512]{1,0:T(8,128)(2,1)} %query_hbm.1, bf16[128,128]{1,0:T(8,128)(2,1)} %bitcast.52), custom_call_target="tpu_custom_call" | custom-call | tf_op jit(solution)/shard_map/pallas_call | solution.py:636
  7.6 9.3 %all-to-all-start = ((bf16[32,40,128]{2,1,0:T(8,128)(2,1)}), bf16[32,40,128]{2,1,0:T(8,128)(2,1)S(1)}, u32[]{:S(2)}, u32[]{:S(2)}) async-start(bf16[32,40,128]{2,1,0:T(8,128)(2,1)} %shard_map.184), calls=%async_computation | async-start | bytes 655360 | tf_op jit(solution)/shard_map/all_to_all | solution.py:29
  16.9 0.8 slice_bitcast_fusion.3
  17.7 1.1 constant_dynamic-slice_fusion
  18.8 0.7 fusion.7
  19.8 10.1 %all-to-all-done.in_ref = bf16[32,40,128]{2,1,0:T(8,128)(2,1)S(1)} async-done(((bf16[32,40,128]{2,1,0:T(8,128)(2,1)}), bf16[32,40,128]{2,1,0:T(8,128)(2,1)S(1)}, u32[]{:S(2)}, u32[]{:S(2)}) %all-to-all-start) | async-done | bytes 327712 | tf_op jit(solution)/shard_map/all_to_all | solution.py:29
  29.9 1.7 %shard_map.185 = bf16[32,40,128]{2,1,0:T(8,128)(2,1)} custom-call(s32[1]{0:T(128)} %bitcast.me_ref, bf16[32,40,128]{2,1,0:T(8,128)(2,1)S(1)} %all-to-all-done.in_ref, f32[8,128]{1,0:T(8,128)S(1)} %get-tuple-element.40.cos_ref, f32[8,128]{1,0:T(8,128)S(1)} %get-tuple-element.39.sin_ref, s32[64,1]{1,0:T(8,128)S(1)} %broadcast_in_dim_reshape.4.length_ref, ...), custom_call_target="tpu_custom_call" | custom-call | tf_op jit(solution)/shard_map/pallas_call | solution.py:46
  31.6 4.8 %all-to-all-start.1 = ((bf16[32,40,128]{2,1,0:T(8,128)(2,1)}), bf16[32,40,128]{2,1,0:T(8,128)(2,1)S(1)}, u32[]{:S(2)}, u32[]{:S(2)}) async-start(bf16[32,40,128]{2,1,0:T(8,128)(2,1)} %shard_map.185), calls=%async_computation.1 | async-start | bytes 655360 | tf_op jit(solution)/shard_map/all_to_all | solution.py:29
  36.5 12.2 %all-to-all-done.1.in_ref = bf16[32,40,128]{2,1,0:T(8,128)(2,1)S(1)} async-done(((bf16[32,40,128]{2,1,0:T(8,128)(2,1)}), bf16[32,40,128]{2,1,0:T(8,128)(2,1)S(1)}, u32[]{:S(2)}, u32[]{:S(2)}) %all-to-all-start.1) | async-done | bytes 327712 | tf_op jit(solution)/shard_map/all_to_all | solution.py:29
  49.3 3.0 %collective-permute-start.4 = (f32[8,128]{1,0:T(8,128)S(1)}, f32[8,128]{1,0:T(8,128)S(1)}, u32[]{:S(2)}, u32[]{:S(2)}) collective-permute-start(f32[8,128]{1,0:T(8,128)S(1)} %shard_map.186.own_ref), channel_id=1, source_target_pairs={{0,3},{1,0},{2,1},{3,2},{4,7},{5,4},{6,5},{7,6},{8,11},{9,8},{10,9... | collective-permute-start | bytes 12296 | tf_op jit(solution)/shard_map/ppermute | solution.py:38
  53.0 1.0 collective-permute-start.2
  54.2 3.3 %collective-permute-done.3.b_ref = f32[8,128]{1,0:T(8,128)S(1)} collective-permute-done((f32[8,128]{1,0:T(8,128)S(1)}, f32[8,128]{1,0:T(8,128)S(1)}, u32[]{:S(2)}, u32[]{:S(2)}) %collective-permute-start.3) | collective-permute-done | bytes 4128 | tf_op jit(solution)/shard_map/ppermute | solution.py:38
  58.1 14.8 %all_to_all.30.in_ref = bf16[32,24,128]{2,1,0:T(8,128)(2,1)S(1)} all-to-all(bf16[32,24,128]{2,1,0:T(8,128)(2,1)S(1)} %get-tuple-element.22), channel_id=1, replica_groups=mesh['guide'=2,'row'=32,'col'=4] {'row'}, dimensions={0} | all-to-all | bytes 393216 | tf_op jit(solution)/shard_map/all_to_all | solution.py:29
  73.2 13.2 %all_to_all.31.in_ref = bf16[32,8,128]{2,1,0:T(8,128)(2,1)S(1)} all-to-all(bf16[32,8,128]{2,1,0:T(8,128)(2,1)S(1)} %shard_map.188), channel_id=1, replica_groups=mesh['guide'=2,'row'=32,'col'=4] {'row'}, dimensions={0} | all-to-all | bytes 131072 | tf_op jit(solution)/shard_map/all_to_all | solution.py:29
  87.2 1.4 %collective-permute-start.6 = (f32[8,128]{1,0:T(8,128)S(1)}, f32[8,128]{1,0:T(8,128)S(1)}, u32[]{:S(2)}, u32[]{:S(2)}) collective-permute-start(f32[8,128]{1,0:T(8,128)S(1)} %shard_map.189), channel_id=1, source_target_pairs={{0,2},{1,3},{2,0},{3,1},{4,6},{5,7},{6,4},{7,5},{8,10},{9,11},{10,... | collective-permute-start | bytes 12296 | tf_op jit(solution)/shard_map/ppermute | solution.py:38
  88.6 1.3 collective-permute-start.5
  90.4 1.9 %collective-permute-done.6 = f32[8,128]{1,0:T(8,128)S(1)} collective-permute-done((f32[8,128]{1,0:T(8,128)S(1)}, f32[8,128]{1,0:T(8,128)S(1)}, u32[]{:S(2)}, u32[]{:S(2)}) %collective-permute-start.6) | collective-permute-done | bytes 4128 | tf_op jit(solution)/shard_map/ppermute | solution.py:38
  92.3 1.1 collective-permute-done.5
  93.5 1.1 collective-permute-done.8.other_ref
  94.6 1.0 shard_map.190
  95.6 4.6 %all-to-all-start.4 = ((bf16[32,16,128]{2,1,0:T(8,128)(2,1)}), bf16[32,16,128]{2,1,0:T(8,128)(2,1)S(1)}, u32[]{:S(2)}, u32[]{:S(2)}) async-start(bf16[32,16,128]{2,1,0:T(8,128)(2,1)} %get-tuple-element.23), calls=%async_computation.4 | async-start | bytes 262144 | tf_op jit(solution)/shard_map/all_to_all | solution.py:29
  100.2 2.6 %shard_map.191 = (f32[16,32064]{1,0:T(8,128)S(1)}, bf16[16,8,1024]{2,1,0:T(8,128)(2,1)S(1)}, bf16[16,8,1024]{2,1,0:T(8,128)(2,1)S(1)}) custom-call(s32[1]{0:T(128)} %bitcast.2.spot_ref, bf16[16,64]{1,0:T(8,128)(2,1)S(1)} %get-tuple-element.24.x_ref, bf16[64,32064]{1,0:T(8,128)(2,1)} %weight_hbm.1), custom_call_target="tpu_custom_call" | custom-call | tf_op jit(solution)/shard_map/pallas_call | solution.py:46
  102.8 1.6 %collective-permute-start.9 = (bf16[16,8,1024]{2,1,0:T(8,128)(2,1)S(1)}, bf16[16,8,1024]{2,1,0:T(8,128)(2,1)S(1)}, u32[]{:S(2)}, u32[]{:S(2)}) collective-permute-start(bf16[16,8,1024]{2,1,0:T(8,128)(2,1)S(1)} %get-tuple-element.26), channel_id=1, source_target_pairs={{0,32},{4,36},{8,40},{12,44},{16,48},{20,52},{24,56},{28,60},{32,0... | collective-permute-start | bytes 786440 | tf_op jit(solution)/shard_map/ppermute | solution.py:618
  104.5 2.1 %collective-permute-start.10 = (bf16[16,8,1024]{2,1,0:T(8,128)(2,1)S(1)}, bf16[16,8,1024]{2,1,0:T(8,128)(2,1)S(1)}, u32[]{:S(2)}, u32[]{:S(2)}) collective-permute-start(bf16[16,8,1024]{2,1,0:T(8,128)(2,1)S(1)} %get-tuple-element.27), channel_id=1, source_target_pairs={{0,96},{4,100},{8,104},{12,108},{16,112},{20,116},{24,120},{28,124... | collective-permute-start | bytes 786440 | tf_op jit(solution)/shard_map/ppermute | solution.py:618
  106.9 3.8 %all-to-all-done.4.in_ref = bf16[32,16,128]{2,1,0:T(8,128)(2,1)S(1)} async-done(((bf16[32,16,128]{2,1,0:T(8,128)(2,1)}), bf16[32,16,128]{2,1,0:T(8,128)(2,1)S(1)}, u32[]{:S(2)}, u32[]{:S(2)}) %all-to-all-start.4) | async-done | bytes 131104 | tf_op jit(solution)/shard_map/all_to_all | solution.py:29
  110.7 1.0 collective-permute-done.9.cond_ref
  111.7 2.3 %collective-permute-done.10.plain_ref = bf16[16,8,1024]{2,1,0:T(8,128)(2,1)S(1)} collective-permute-done((bf16[16,8,1024]{2,1,0:T(8,128)(2,1)S(1)}, bf16[16,8,1024]{2,1,0:T(8,128)(2,1)S(1)}, u32[]{:S(2)}, u32[]{:S(2)}) %collective-permute-start.10) | collective-permute-done | bytes 262176 | tf_op jit(solution)/shard_map/ppermute | solution.py:618
  114.0 1.0 shard_map.192
  115.0 18.8 %all_to_all.32.in_ref = bf16[16,8,1152]{2,1,0:T(8,128)(2,1)S(1)} all-to-all(bf16[16,8,1152]{2,1,0:T(8,128)(2,1)S(1)} %shard_map.192), channel_id=1, replica_groups={{0,4,8,12,16,20,24,28,64,68,72,76,80,84,88,92},{32,36,40,44,48,52,56,60..., dimensions={0} | all-to-all | bytes 589824 | tf_op jit(solution)/shard_map/all_to_all | solution.py:748
  (49 shorter events, 5.2 us)
Async XLA Ops:
  0.6 35.8 %copy-start.5 = (bf16[1,16,64]{2,1,0:T(8,128)(2,1)S(1)}, bf16[1,16,64]{2,1,0:T(8,128)(2,1)}, u32[]{:S(2)}) copy-start(bf16[1,16,64]{2,1,0:T(8,128)(2,1)} %param.17) | copy-start | bytes 6148
  0.6 48.1 %copy-start.1 = (bf16[512,64]{0,1:T(8,128)(2,1)S(1)}, bf16[512,64]{0,1:T(8,128)(2,1)}, u32[]{:S(2)}) copy-start(bf16[512,64]{0,1:T(8,128)(2,1)} %param.23) | copy-start | bytes 196612
  0.7 53.3 %copy-start.8 = (bf16[64]{0:T(256)(128)(2,1)S(1)}, bf16[64]{0:T(256)(128)(2,1)}, u32[]{:S(2)}) copy-start(bf16[64]{0:T(256)(128)(2,1)} %param.24) | copy-start | bytes 388
  0.7 53.4 %copy-start.4 = (bf16[64,2,2048]{2,1,0:T(2,128)(2,1)S(1)}, bf16[64,2,2048]{2,1,0:T(2,128)(2,1)}, u32[]{:S(2)}) copy-start(bf16[64,2,2048]{2,1,0:T(2,128)(2,1)} %param.25) | copy-start | bytes 1572868
  0.7 85.6 %copy-start = (bf16[2048,64]{0,1:T(8,128)(2,1)S(1)}, bf16[2048,64]{0,1:T(8,128)(2,1)}, u32[]{:S(2)}) copy-start(bf16[2048,64]{0,1:T(8,128)(2,1)} %param.26) | copy-start | bytes 786436
  1.9 91.6 %copy-start.6 = (bf16[64]{0:T(256)(128)(2,1)S(1)}, bf16[64]{0:T(256)(128)(2,1)}, u32[]{:S(2)}) copy-start(bf16[64]{0:T(256)(128)(2,1)} %param.27) | copy-start | bytes 388
  1.9 91.6 %copy-start.7 = (bf16[64]{0:T(256)(128)(2,1)S(1)}, bf16[64]{0:T(256)(128)(2,1)}, u32[]{:S(2)}) copy-start(bf16[64]{0:T(256)(128)(2,1)} %param.29) | copy-start | bytes 388
  1.9 92.7 %copy-start.2 = (bf16[64,512]{1,0:T(8,128)(2,1)S(1)}, bf16[64,512]{1,0:T(8,128)(2,1)}, u32[]{:S(2)}) copy-start(bf16[64,512]{1,0:T(8,128)(2,1)} %query_ref.1) | copy-start | bytes 196612
  1.9 92.7 %copy-start.3 = (bf16[64,2,128]{2,1,0:T(2,128)(2,1)S(1)}, bf16[64,2,128]{2,1,0:T(2,128)(2,1)}, u32[]{:S(2)}) copy-start(bf16[64,2,128]{2,1,0:T(2,128)(2,1)} %param.31) | copy-start | bytes 98308
  1.9 17.9 %collective-permute-start = (bf16[4,2,128,128]{3,2,1,0:T(8,128)(2,1)S(1)}, bf16[4,2,128,128]{3,2,1,0:T(8,128)(2,1)S(1)}, u32[]{:S(2)}, u32[]{:S(2)}) collective-permute-start(bf16[4,2,128,128]{3,2,1,0:T(8,128)(2,1)S(1)} %get-tuple-element.19), channel_id=1, source_target_pairs={{0,32},{4,36},{8,40},{12,44},{16,48},{20,52},{24,56},{28,60},{32,0... | collective-permute-start | bytes 786440 | tf_op jit(solution)/shard_map/ppermute | solution.py:618
  3.5 16.3 %collective-permute-start.1 = (bf16[4,2,128,128]{3,2,1,0:T(8,128)(2,1)S(1)}, bf16[4,2,128,128]{3,2,1,0:T(8,128)(2,1)S(1)}, u32[]{:S(2)}, u32[]{:S(2)}) collective-permute-start(bf16[4,2,128,128]{3,2,1,0:T(8,128)(2,1)S(1)} %get-tuple-element.20), channel_id=1, source_target_pairs={{0,96},{4,100},{8,104},{12,108},{16,112},{20,116},{24,120},{28,124... | collective-permute-start | bytes 786440 | tf_op jit(solution)/shard_map/ppermute | solution.py:618
  7.6 22.4 %all-to-all-start = ((bf16[32,40,128]{2,1,0:T(8,128)(2,1)}), bf16[32,40,128]{2,1,0:T(8,128)(2,1)S(1)}, u32[]{:S(2)}, u32[]{:S(2)}) async-start(bf16[32,40,128]{2,1,0:T(8,128)(2,1)} %shard_map.184), calls=%async_computation | async-start | bytes 655360 | tf_op jit(solution)/shard_map/all_to_all | solution.py:29
  31.6 75.0 %copy-start.9 = (f32[4]{0:T(128)S(1)}, f32[4]{0:T(128)}, u32[]{:S(2)}) copy-start(f32[4]{0:T(128)} %param.33) | copy-start | bytes 52
  31.6 75.0 %copy-start.10 = (s32[16]{0:T(128)S(1)}, s32[16]{0:T(128)}, u32[]{:S(2)}) copy-start(s32[16]{0:T(128)} %param.32) | copy-start | bytes 196
  31.6 17.1 %all-to-all-start.1 = ((bf16[32,40,128]{2,1,0:T(8,128)(2,1)}), bf16[32,40,128]{2,1,0:T(8,128)(2,1)S(1)}, u32[]{:S(2)}, u32[]{:S(2)}) async-start(bf16[32,40,128]{2,1,0:T(8,128)(2,1)} %shard_map.185), calls=%async_computation.1 | async-start | bytes 655360 | tf_op jit(solution)/shard_map/all_to_all | solution.py:29
  49.3 4.9 %collective-permute-start.4 = (f32[8,128]{1,0:T(8,128)S(1)}, f32[8,128]{1,0:T(8,128)S(1)}, u32[]{:S(2)}, u32[]{:S(2)}) collective-permute-start(f32[8,128]{1,0:T(8,128)S(1)} %shard_map.186.own_ref), channel_id=1, source_target_pairs={{0,3},{1,0},{2,1},{3,2},{4,7},{5,4},{6,5},{7,6},{8,11},{9,8},{10,9... | collective-permute-start | bytes 12296 | tf_op jit(solution)/shard_map/ppermute | solution.py:38
  52.3 5.1 %collective-permute-start.3 = (f32[8,128]{1,0:T(8,128)S(1)}, f32[8,128]{1,0:T(8,128)S(1)}, u32[]{:S(2)}, u32[]{:S(2)}) collective-permute-start(f32[8,128]{1,0:T(8,128)S(1)} %shard_map.186.own_ref), channel_id=1, source_target_pairs={{0,2},{1,3},{2,0},{3,1},{4,6},{5,7},{6,4},{7,5},{8,10},{9,11},{10,... | collective-permute-start | bytes 12296 | tf_op jit(solution)/shard_map/ppermute | solution.py:38
  53.0 4.8 %collective-permute-start.2 = (f32[8,128]{1,0:T(8,128)S(1)}, f32[8,128]{1,0:T(8,128)S(1)}, u32[]{:S(2)}, u32[]{:S(2)}) collective-permute-start(f32[8,128]{1,0:T(8,128)S(1)} %shard_map.186.own_ref), channel_id=1, source_target_pairs={{0,1},{1,2},{2,3},{3,0},{4,5},{5,6},{6,7},{7,4},{8,9},{9,10},{10,1... | collective-permute-start | bytes 12296 | tf_op jit(solution)/shard_map/ppermute | solution.py:38
  86.8 3.6 %collective-permute-start.7 = (f32[8,128]{1,0:T(8,128)S(1)}, f32[8,128]{1,0:T(8,128)S(1)}, u32[]{:S(2)}, u32[]{:S(2)}) collective-permute-start(f32[8,128]{1,0:T(8,128)S(1)} %shard_map.189), channel_id=1, source_target_pairs={{0,3},{1,0},{2,1},{3,2},{4,7},{5,4},{6,5},{7,6},{8,11},{9,8},{10,9... | collective-permute-start | bytes 12296 | tf_op jit(solution)/shard_map/ppermute | solution.py:38
  87.2 5.1 %collective-permute-start.6 = (f32[8,128]{1,0:T(8,128)S(1)}, f32[8,128]{1,0:T(8,128)S(1)}, u32[]{:S(2)}, u32[]{:S(2)}) collective-permute-start(f32[8,128]{1,0:T(8,128)S(1)} %shard_map.189), channel_id=1, source_target_pairs={{0,2},{1,3},{2,0},{3,1},{4,6},{5,7},{6,4},{7,5},{8,10},{9,11},{10,... | collective-permute-start | bytes 12296 | tf_op jit(solution)/shard_map/ppermute | solution.py:38
  88.6 4.8 %collective-permute-start.5 = (f32[8,128]{1,0:T(8,128)S(1)}, f32[8,128]{1,0:T(8,128)S(1)}, u32[]{:S(2)}, u32[]{:S(2)}) collective-permute-start(f32[8,128]{1,0:T(8,128)S(1)} %shard_map.189), channel_id=1, source_target_pairs={{0,1},{1,2},{2,3},{3,0},{4,5},{5,6},{6,7},{7,4},{8,9},{9,10},{10,1... | collective-permute-start | bytes 12296 | tf_op jit(solution)/shard_map/ppermute | solution.py:38
  93.4 1.2 collective-permute-start.8
  95.6 15.1 %all-to-all-start.4 = ((bf16[32,16,128]{2,1,0:T(8,128)(2,1)}), bf16[32,16,128]{2,1,0:T(8,128)(2,1)S(1)}, u32[]{:S(2)}, u32[]{:S(2)}) async-start(bf16[32,16,128]{2,1,0:T(8,128)(2,1)} %get-tuple-element.23), calls=%async_computation.4 | async-start | bytes 262144 | tf_op jit(solution)/shard_map/all_to_all | solution.py:29
  102.8 8.8 %collective-permute-start.9 = (bf16[16,8,1024]{2,1,0:T(8,128)(2,1)S(1)}, bf16[16,8,1024]{2,1,0:T(8,128)(2,1)S(1)}, u32[]{:S(2)}, u32[]{:S(2)}) collective-permute-start(bf16[16,8,1024]{2,1,0:T(8,128)(2,1)S(1)} %get-tuple-element.26), channel_id=1, source_target_pairs={{0,32},{4,36},{8,40},{12,44},{16,48},{20,52},{24,56},{28,60},{32,0... | collective-permute-start | bytes 786440 | tf_op jit(solution)/shard_map/ppermute | solution.py:618
  104.5 9.5 %collective-permute-start.10 = (bf16[16,8,1024]{2,1,0:T(8,128)(2,1)S(1)}, bf16[16,8,1024]{2,1,0:T(8,128)(2,1)S(1)}, u32[]{:S(2)}, u32[]{:S(2)}) collective-permute-start(bf16[16,8,1024]{2,1,0:T(8,128)(2,1)S(1)} %get-tuple-element.27), channel_id=1, source_target_pairs={{0,96},{4,100},{8,104},{12,108},{16,112},{20,116},{24,120},{28,124... | collective-permute-start | bytes 786440 | tf_op jit(solution)/shard_map/ppermute | solution.py:618

commit v6 on v5

--- a/solution.py
+++ b/solution.py
@@ -727,7 +727,7 @@
         parity[None],
         head_input,
         pltpu.with_memory_space_constraint(w_head, pltpu.HBM),
-        scratch=[wide, pltpu.VMEM(w_head.shape, BF16), pltpu.SemaphoreType.DMA((4,))],
+        scratch=[wide, pltpu.VMEM(w_head.shape, BF16), pltpu.SemaphoreType.DMA((8,))],
         scalars=1,
         in_hbm=1,
         limit=12 << 20,

time: 135 us -> 135 us (level)
  transfers between devices with their start and end apart: 14 -> 14, of which waited for: 11 -> 11; matrix products, arithmetic and copies ran while one was open for 3% -> 3% of each run, Pallas kernels for 3% -> 4%
where the time goes in v6:
time: 135 us
  blocking collectives  46.9 us (35%)
  waiting for transfers between devices  37.5 us (28%)
  starting transfers between devices  33.9 us (25%)
  Pallas kernels  10.7 us (8%)
  local copies, waits for them, and re-layouts  3.53 us (3%)
    all_to_all x2, blocking collectives, exchange(): return lax.all_to_all(x, axis, 0, 0, tiled=True)  28 us
    all_to_all x3, waiting for transfers between devices, exchange(): return lax.all_to_all(x, axis, 0, 0, tiled=True)  25.9 us
    all_to_all x1, blocking collectives, local(): lax.all_to_all(payload, 'row', 0, 0, axis_index_groups=groups, tiled=True)  18.9 us
    all_to_all x3, starting transfers between devices, exchange(): return lax.all_to_all(x, axis, 0, 0, tiled=True)  18.7 us
    pallas_call x9, Pallas kernels, call(): pl.pallas_call(body, out_shape=outs, in_specs=specs, out_specs=out_specs,...  8.73 us
    ppermute x6, starting transfers between devices, from_others(): lax.ppermute(x, axis, [(i, (i + k) % n) for i in range(n)])  7.78 us
    ppermute x4, starting transfers between devices, between(): return lax.ppermute(block, 'row', pairs)  7.4 us
    ppermute x6, waiting for transfers between devices, from_others(): lax.ppermute(x, axis, [(i, (i + k) % n) for i in range(n)])  7.12 us
  transfers between devices with their start and end apart: 14, of which 11 were waited for; matrix products, arithmetic and copies ran while one was open for 3% of the time, Pallas kernels for 4%

profile of v6, /device:TPU:32, one launch (start us, length us, event | category | flops | bytes accessed | tf_op | source)
XLA Modules:
  0.0 134.7 jit_solution(14237297926791599190)
XLA Ops:
  0.7 1.1 dynamic-slice_bitcast_fusion
  1.9 1.6 %collective-permute-start = (bf16[4,2,128,128]{3,2,1,0:T(8,128)(2,1)S(1)}, bf16[4,2,128,128]{3,2,1,0:T(8,128)(2,1)S(1)}, u32[]{:S(2)}, u32[]{:S(2)}) collective-permute-start(bf16[4,2,128,128]{3,2,1,0:T(8,128)(2,1)S(1)} %get-tuple-element.19), channel_id=1, source_target_pairs={{0,32},{4,36},{8,40},{12,44},{16,48},{20,52},{24,56},{28,60},{32,0... | collective-permute-start | bytes 786440 | tf_op jit(solution)/shard_map/ppermute | solution.py:618
  3.5 2.1 %collective-permute-start.1 = (bf16[4,2,128,128]{3,2,1,0:T(8,128)(2,1)S(1)}, bf16[4,2,128,128]{3,2,1,0:T(8,128)(2,1)S(1)}, u32[]{:S(2)}, u32[]{:S(2)}) collective-permute-start(bf16[4,2,128,128]{3,2,1,0:T(8,128)(2,1)S(1)} %get-tuple-element.20), channel_id=1, source_target_pairs={{0,96},{4,100},{8,104},{12,108},{16,112},{20,116},{24,120},{28,124... | collective-permute-start | bytes 786440 | tf_op jit(solution)/shard_map/ppermute | solution.py:618
  5.6 2.0 %shard_map.184 = bf16[32,40,128]{2,1,0:T(8,128)(2,1)} custom-call(bf16[16,64]{1,0:T(8,128)(2,1)} %bitcast.53, bf16[1,64]{1,0:T(2,128)(2,1)} %bitcast.54, bf16[64,512]{1,0:T(8,128)(2,1)} %query_hbm.1, bf16[128,128]{1,0:T(8,128)(2,1)} %bitcast.52), custom_call_target="tpu_custom_call" | custom-call | tf_op jit(solution)/shard_map/pallas_call | solution.py:636
  7.6 9.3 %all-to-all-start = ((bf16[32,40,128]{2,1,0:T(8,128)(2,1)}), bf16[32,40,128]{2,1,0:T(8,128)(2,1)S(1)}, u32[]{:S(2)}, u32[]{:S(2)}) async-start(bf16[32,40,128]{2,1,0:T(8,128)(2,1)} %shard_map.184), calls=%async_computation | async-start | bytes 655360 | tf_op jit(solution)/shard_map/all_to_all | solution.py:29
  16.9 0.8 slice_bitcast_fusion.3
  17.7 1.1 constant_dynamic-slice_fusion
  18.8 0.7 fusion.7
  19.8 10.1 %all-to-all-done.in_ref = bf16[32,40,128]{2,1,0:T(8,128)(2,1)S(1)} async-done(((bf16[32,40,128]{2,1,0:T(8,128)(2,1)}), bf16[32,40,128]{2,1,0:T(8,128)(2,1)S(1)}, u32[]{:S(2)}, u32[]{:S(2)}) %all-to-all-start) | async-done | bytes 327712 | tf_op jit(solution)/shard_map/all_to_all | solution.py:29
  29.9 1.7 %shard_map.185 = bf16[32,40,128]{2,1,0:T(8,128)(2,1)} custom-call(s32[1]{0:T(128)} %bitcast.me_ref, bf16[32,40,128]{2,1,0:T(8,128)(2,1)S(1)} %all-to-all-done.in_ref, f32[8,128]{1,0:T(8,128)S(1)} %get-tuple-element.40.cos_ref, f32[8,128]{1,0:T(8,128)S(1)} %get-tuple-element.39.sin_ref, s32[64,1]{1,0:T(8,128)S(1)} %broadcast_in_dim_reshape.4.length_ref, ...), custom_call_target="tpu_custom_call" | custom-call | tf_op jit(solution)/shard_map/pallas_call | solution.py:46
  31.6 4.8 %all-to-all-start.1 = ((bf16[32,40,128]{2,1,0:T(8,128)(2,1)}), bf16[32,40,128]{2,1,0:T(8,128)(2,1)S(1)}, u32[]{:S(2)}, u32[]{:S(2)}) async-start(bf16[32,40,128]{2,1,0:T(8,128)(2,1)} %shard_map.185), calls=%async_computation.1 | async-start | bytes 655360 | tf_op jit(solution)/shard_map/all_to_all | solution.py:29
  36.5 12.2 %all-to-all-done.1.in_ref = bf16[32,40,128]{2,1,0:T(8,128)(2,1)S(1)} async-done(((bf16[32,40,128]{2,1,0:T(8,128)(2,1)}), bf16[32,40,128]{2,1,0:T(8,128)(2,1)S(1)}, u32[]{:S(2)}, u32[]{:S(2)}) %all-to-all-start.1) | async-done | bytes 327712 | tf_op jit(solution)/shard_map/all_to_all | solution.py:29
  49.3 3.0 %collective-permute-start.4 = (f32[8,128]{1,0:T(8,128)S(1)}, f32[8,128]{1,0:T(8,128)S(1)}, u32[]{:S(2)}, u32[]{:S(2)}) collective-permute-start(f32[8,128]{1,0:T(8,128)S(1)} %shard_map.186.own_ref), channel_id=1, source_target_pairs={{0,3},{1,0},{2,1},{3,2},{4,7},{5,4},{6,5},{7,6},{8,11},{9,8},{10,9... | collective-permute-start | bytes 12296 | tf_op jit(solution)/shard_map/ppermute | solution.py:38
  53.0 1.0 collective-permute-start.2
  54.2 3.3 %collective-permute-done.3.b_ref = f32[8,128]{1,0:T(8,128)S(1)} collective-permute-done((f32[8,128]{1,0:T(8,128)S(1)}, f32[8,128]{1,0:T(8,128)S(1)}, u32[]{:S(2)}, u32[]{:S(2)}) %collective-permute-start.3) | collective-permute-done | bytes 4128 | tf_op jit(solution)/shard_map/ppermute | solution.py:38
  58.1 14.8 %all_to_all.30.in_ref = bf16[32,24,128]{2,1,0:T(8,128)(2,1)S(1)} all-to-all(bf16[32,24,128]{2,1,0:T(8,128)(2,1)S(1)} %get-tuple-element.22), channel_id=1, replica_groups=mesh['guide'=2,'row'=32,'col'=4] {'row'}, dimensions={0} | all-to-all | bytes 393216 | tf_op jit(solution)/shard_map/all_to_all | solution.py:29
  73.2 13.2 %all_to_all.31.in_ref = bf16[32,8,128]{2,1,0:T(8,128)(2,1)S(1)} all-to-all(bf16[32,8,128]{2,1,0:T(8,128)(2,1)S(1)} %shard_map.188), channel_id=1, replica_groups=mesh['guide'=2,'row'=32,'col'=4] {'row'}, dimensions={0} | all-to-all | bytes 131072 | tf_op jit(solution)/shard_map/all_to_all | solution.py:29
  87.2 1.4 %collective-permute-start.6 = (f32[8,128]{1,0:T(8,128)S(1)}, f32[8,128]{1,0:T(8,128)S(1)}, u32[]{:S(2)}, u32[]{:S(2)}) collective-permute-start(f32[8,128]{1,0:T(8,128)S(1)} %shard_map.189), channel_id=1, source_target_pairs={{0,2},{1,3},{2,0},{3,1},{4,6},{5,7},{6,4},{7,5},{8,10},{9,11},{10,... | collective-permute-start | bytes 12296 | tf_op jit(solution)/shard_map/ppermute | solution.py:38
  88.6 1.3 collective-permute-start.5
  90.4 1.9 %collective-permute-done.6 = f32[8,128]{1,0:T(8,128)S(1)} collective-permute-done((f32[8,128]{1,0:T(8,128)S(1)}, f32[8,128]{1,0:T(8,128)S(1)}, u32[]{:S(2)}, u32[]{:S(2)}) %collective-permute-start.6) | collective-permute-done | bytes 4128 | tf_op jit(solution)/shard_map/ppermute | solution.py:38
  92.3 1.1 collective-permute-done.5
  93.5 1.1 collective-permute-done.8.other_ref
  94.6 1.0 shard_map.190
  95.6 4.6 %all-to-all-start.4 = ((bf16[32,16,128]{2,1,0:T(8,128)(2,1)}), bf16[32,16,128]{2,1,0:T(8,128)(2,1)S(1)}, u32[]{:S(2)}, u32[]{:S(2)}) async-start(bf16[32,16,128]{2,1,0:T(8,128)(2,1)} %get-tuple-element.23), calls=%async_computation.4 | async-start | bytes 262144 | tf_op jit(solution)/shard_map/all_to_all | solution.py:29
  100.2 2.8 %shard_map.191 = (f32[16,32064]{1,0:T(8,128)S(1)}, bf16[16,8,1024]{2,1,0:T(8,128)(2,1)S(1)}, bf16[16,8,1024]{2,1,0:T(8,128)(2,1)S(1)}) custom-call(s32[1]{0:T(128)} %bitcast.2.spot_ref, bf16[16,64]{1,0:T(8,128)(2,1)S(1)} %get-tuple-element.24.x_ref, bf16[64,32064]{1,0:T(8,128)(2,1)} %weight_hbm.1), custom_call_target="tpu_custom_call" | custom-call | tf_op jit(solution)/shard_map/pallas_call | solution.py:46
  103.1 1.6 %collective-permute-start.9 = (bf16[16,8,1024]{2,1,0:T(8,128)(2,1)S(1)}, bf16[16,8,1024]{2,1,0:T(8,128)(2,1)S(1)}, u32[]{:S(2)}, u32[]{:S(2)}) collective-permute-start(bf16[16,8,1024]{2,1,0:T(8,128)(2,1)S(1)} %get-tuple-element.26), channel_id=1, source_target_pairs={{0,32},{4,36},{8,40},{12,44},{16,48},{20,52},{24,56},{28,60},{32,0... | collective-permute-start | bytes 786440 | tf_op jit(solution)/shard_map/ppermute | solution.py:618
  104.7 2.1 %collective-permute-start.10 = (bf16[16,8,1024]{2,1,0:T(8,128)(2,1)S(1)}, bf16[16,8,1024]{2,1,0:T(8,128)(2,1)S(1)}, u32[]{:S(2)}, u32[]{:S(2)}) collective-permute-start(bf16[16,8,1024]{2,1,0:T(8,128)(2,1)S(1)} %get-tuple-element.27), channel_id=1, source_target_pairs={{0,96},{4,100},{8,104},{12,108},{16,112},{20,116},{24,120},{28,124... | collective-permute-start | bytes 786440 | tf_op jit(solution)/shard_map/ppermute | solution.py:618
  107.1 3.6 %all-to-all-done.4.in_ref = bf16[32,16,128]{2,1,0:T(8,128)(2,1)S(1)} async-done(((bf16[32,16,128]{2,1,0:T(8,128)(2,1)}), bf16[32,16,128]{2,1,0:T(8,128)(2,1)S(1)}, u32[]{:S(2)}, u32[]{:S(2)}) %all-to-all-start.4) | async-done | bytes 131104 | tf_op jit(solution)/shard_map/all_to_all | solution.py:29
  110.7 1.2 collective-permute-done.9.cond_ref
  111.8 2.3 %collective-permute-done.10.plain_ref = bf16[16,8,1024]{2,1,0:T(8,128)(2,1)S(1)} collective-permute-done((bf16[16,8,1024]{2,1,0:T(8,128)(2,1)S(1)}, bf16[16,8,1024]{2,1,0:T(8,128)(2,1)S(1)}, u32[]{:S(2)}, u32[]{:S(2)}) %collective-permute-start.10) | collective-permute-done | bytes 262176 | tf_op jit(solution)/shard_map/ppermute | solution.py:618
  114.1 1.0 shard_map.192
  115.1 18.9 %all_to_all.32.in_ref = bf16[16,8,1152]{2,1,0:T(8,128)(2,1)S(1)} all-to-all(bf16[16,8,1152]{2,1,0:T(8,128)(2,1)S(1)} %shard_map.192), channel_id=1, replica_groups={{0,4,8,12,16,20,24,28,64,68,72,76,80,84,88,92},{32,36,40,44,48,52,56,60..., dimensions={0} | all-to-all | bytes 589824 | tf_op jit(solution)/shard_map/all_to_all | solution.py:748
  (49 shorter events, 5.2 us)
Async XLA Ops:
  0.6 35.8 %copy-start.5 = (bf16[1,16,64]{2,1,0:T(8,128)(2,1)S(1)}, bf16[1,16,64]{2,1,0:T(8,128)(2,1)}, u32[]{:S(2)}) copy-start(bf16[1,16,64]{2,1,0:T(8,128)(2,1)} %param.17) | copy-start | bytes 6148
  0.6 48.1 %copy-start.1 = (bf16[512,64]{0,1:T(8,128)(2,1)S(1)}, bf16[512,64]{0,1:T(8,128)(2,1)}, u32[]{:S(2)}) copy-start(bf16[512,64]{0,1:T(8,128)(2,1)} %param.23) | copy-start | bytes 196612
  0.7 53.3 %copy-start.8 = (bf16[64]{0:T(256)(128)(2,1)S(1)}, bf16[64]{0:T(256)(128)(2,1)}, u32[]{:S(2)}) copy-start(bf16[64]{0:T(256)(128)(2,1)} %param.24) | copy-start | bytes 388
  0.7 53.4 %copy-start.4 = (bf16[64,2,2048]{2,1,0:T(2,128)(2,1)S(1)}, bf16[64,2,2048]{2,1,0:T(2,128)(2,1)}, u32[]{:S(2)}) copy-start(bf16[64,2,2048]{2,1,0:T(2,128)(2,1)} %param.25) | copy-start | bytes 1572868
  0.7 85.6 %copy-start = (bf16[2048,64]{0,1:T(8,128)(2,1)S(1)}, bf16[2048,64]{0,1:T(8,128)(2,1)}, u32[]{:S(2)}) copy-start(bf16[2048,64]{0,1:T(8,128)(2,1)} %param.26) | copy-start | bytes 786436
  1.9 91.6 %copy-start.6 = (bf16[64]{0:T(256)(128)(2,1)S(1)}, bf16[64]{0:T(256)(128)(2,1)}, u32[]{:S(2)}) copy-start(bf16[64]{0:T(256)(128)(2,1)} %param.27) | copy-start | bytes 388
  1.9 91.6 %copy-start.7 = (bf16[64]{0:T(256)(128)(2,1)S(1)}, bf16[64]{0:T(256)(128)(2,1)}, u32[]{:S(2)}) copy-start(bf16[64]{0:T(256)(128)(2,1)} %param.29) | copy-start | bytes 388
  1.9 92.7 %copy-start.2 = (bf16[64,512]{1,0:T(8,128)(2,1)S(1)}, bf16[64,512]{1,0:T(8,128)(2,1)}, u32[]{:S(2)}) copy-start(bf16[64,512]{1,0:T(8,128)(2,1)} %query_ref.1) | copy-start | bytes 196612
  1.9 92.7 %copy-start.3 = (bf16[64,2,128]{2,1,0:T(2,128)(2,1)S(1)}, bf16[64,2,128]{2,1,0:T(2,128)(2,1)}, u32[]{:S(2)}) copy-start(bf16[64,2,128]{2,1,0:T(2,128)(2,1)} %param.31) | copy-start | bytes 98308
  1.9 17.9 %collective-permute-start = (bf16[4,2,128,128]{3,2,1,0:T(8,128)(2,1)S(1)}, bf16[4,2,128,128]{3,2,1,0:T(8,128)(2,1)S(1)}, u32[]{:S(2)}, u32[]{:S(2)}) collective-permute-start(bf16[4,2,128,128]{3,2,1,0:T(8,128)(2,1)S(1)} %get-tuple-element.19), channel_id=1, source_target_pairs={{0,32},{4,36},{8,40},{12,44},{16,48},{20,52},{24,56},{28,60},{32,0... | collective-permute-start | bytes 786440 | tf_op jit(solution)/shard_map/ppermute | solution.py:618
  3.5 16.3 %collective-permute-start.1 = (bf16[4,2,128,128]{3,2,1,0:T(8,128)(2,1)S(1)}, bf16[4,2,128,128]{3,2,1,0:T(8,128)(2,1)S(1)}, u32[]{:S(2)}, u32[]{:S(2)}) collective-permute-start(bf16[4,2,128,128]{3,2,1,0:T(8,128)(2,1)S(1)} %get-tuple-element.20), channel_id=1, source_target_pairs={{0,96},{4,100},{8,104},{12,108},{16,112},{20,116},{24,120},{28,124... | collective-permute-start | bytes 786440 | tf_op jit(solution)/shard_map/ppermute | solution.py:618
  7.6 22.4 %all-to-all-start = ((bf16[32,40,128]{2,1,0:T(8,128)(2,1)}), bf16[32,40,128]{2,1,0:T(8,128)(2,1)S(1)}, u32[]{:S(2)}, u32[]{:S(2)}) async-start(bf16[32,40,128]{2,1,0:T(8,128)(2,1)} %shard_map.184), calls=%async_computation | async-start | bytes 655360 | tf_op jit(solution)/shard_map/all_to_all | solution.py:29
  31.6 75.2 %copy-start.9 = (f32[4]{0:T(128)S(1)}, f32[4]{0:T(128)}, u32[]{:S(2)}) copy-start(f32[4]{0:T(128)} %param.33) | copy-start | bytes 52
  31.6 75.2 %copy-start.10 = (s32[16]{0:T(128)S(1)}, s32[16]{0:T(128)}, u32[]{:S(2)}) copy-start(s32[16]{0:T(128)} %param.32) | copy-start | bytes 196
  31.6 17.1 %all-to-all-start.1 = ((bf16[32,40,128]{2,1,0:T(8,128)(2,1)}), bf16[32,40,128]{2,1,0:T(8,128)(2,1)S(1)}, u32[]{:S(2)}, u32[]{:S(2)}) async-start(bf16[32,40,128]{2,1,0:T(8,128)(2,1)} %shard_map.185), calls=%async_computation.1 | async-start | bytes 655360 | tf_op jit(solution)/shard_map/all_to_all | solution.py:29
  49.3 4.9 %collective-permute-start.4 = (f32[8,128]{1,0:T(8,128)S(1)}, f32[8,128]{1,0:T(8,128)S(1)}, u32[]{:S(2)}, u32[]{:S(2)}) collective-permute-start(f32[8,128]{1,0:T(8,128)S(1)} %shard_map.186.own_ref), channel_id=1, source_target_pairs={{0,3},{1,0},{2,1},{3,2},{4,7},{5,4},{6,5},{7,6},{8,11},{9,8},{10,9... | collective-permute-start | bytes 12296 | tf_op jit(solution)/shard_map/ppermute | solution.py:38
  52.3 5.1 %collective-permute-start.3 = (f32[8,128]{1,0:T(8,128)S(1)}, f32[8,128]{1,0:T(8,128)S(1)}, u32[]{:S(2)}, u32[]{:S(2)}) collective-permute-start(f32[8,128]{1,0:T(8,128)S(1)} %shard_map.186.own_ref), channel_id=1, source_target_pairs={{0,2},{1,3},{2,0},{3,1},{4,6},{5,7},{6,4},{7,5},{8,10},{9,11},{10,... | collective-permute-start | bytes 12296 | tf_op jit(solution)/shard_map/ppermute | solution.py:38
  53.0 4.8 %collective-permute-start.2 = (f32[8,128]{1,0:T(8,128)S(1)}, f32[8,128]{1,0:T(8,128)S(1)}, u32[]{:S(2)}, u32[]{:S(2)}) collective-permute-start(f32[8,128]{1,0:T(8,128)S(1)} %shard_map.186.own_ref), channel_id=1, source_target_pairs={{0,1},{1,2},{2,3},{3,0},{4,5},{5,6},{6,7},{7,4},{8,9},{9,10},{10,1... | collective-permute-start | bytes 12296 | tf_op jit(solution)/shard_map/ppermute | solution.py:38
  86.8 3.6 %collective-permute-start.7 = (f32[8,128]{1,0:T(8,128)S(1)}, f32[8,128]{1,0:T(8,128)S(1)}, u32[]{:S(2)}, u32[]{:S(2)}) collective-permute-start(f32[8,128]{1,0:T(8,128)S(1)} %shard_map.189), channel_id=1, source_target_pairs={{0,3},{1,0},{2,1},{3,2},{4,7},{5,4},{6,5},{7,6},{8,11},{9,8},{10,9... | collective-permute-start | bytes 12296 | tf_op jit(solution)/shard_map/ppermute | solution.py:38
  87.2 5.1 %collective-permute-start.6 = (f32[8,128]{1,0:T(8,128)S(1)}, f32[8,128]{1,0:T(8,128)S(1)}, u32[]{:S(2)}, u32[]{:S(2)}) collective-permute-start(f32[8,128]{1,0:T(8,128)S(1)} %shard_map.189), channel_id=1, source_target_pairs={{0,2},{1,3},{2,0},{3,1},{4,6},{5,7},{6,4},{7,5},{8,10},{9,11},{10,... | collective-permute-start | bytes 12296 | tf_op jit(solution)/shard_map/ppermute | solution.py:38
  88.6 4.8 %collective-permute-start.5 = (f32[8,128]{1,0:T(8,128)S(1)}, f32[8,128]{1,0:T(8,128)S(1)}, u32[]{:S(2)}, u32[]{:S(2)}) collective-permute-start(f32[8,128]{1,0:T(8,128)S(1)} %shard_map.189), channel_id=1, source_target_pairs={{0,1},{1,2},{2,3},{3,0},{4,5},{5,6},{6,7},{7,4},{8,9},{9,10},{10,1... | collective-permute-start | bytes 12296 | tf_op jit(solution)/shard_map/ppermute | solution.py:38
  93.4 1.2 collective-permute-start.8
  95.6 15.1 %all-to-all-start.4 = ((bf16[32,16,128]{2,1,0:T(8,128)(2,1)}), bf16[32,16,128]{2,1,0:T(8,128)(2,1)S(1)}, u32[]{:S(2)}, u32[]{:S(2)}) async-start(bf16[32,16,128]{2,1,0:T(8,128)(2,1)} %get-tuple-element.23), calls=%async_computation.4 | async-start | bytes 262144 | tf_op jit(solution)/shard_map/all_to_all | solution.py:29
  103.1 8.8 %collective-permute-start.9 = (bf16[16,8,1024]{2,1,0:T(8,128)(2,1)S(1)}, bf16[16,8,1024]{2,1,0:T(8,128)(2,1)S(1)}, u32[]{:S(2)}, u32[]{:S(2)}) collective-permute-start(bf16[16,8,1024]{2,1,0:T(8,128)(2,1)S(1)} %get-tuple-element.26), channel_id=1, source_target_pairs={{0,32},{4,36},{8,40},{12,44},{16,48},{20,52},{24,56},{28,60},{32,0... | collective-permute-start | bytes 786440 | tf_op jit(solution)/shard_map/ppermute | solution.py:618
  104.7 9.4 %collective-permute-start.10 = (bf16[16,8,1024]{2,1,0:T(8,128)(2,1)S(1)}, bf16[16,8,1024]{2,1,0:T(8,128)(2,1)S(1)}, u32[]{:S(2)}, u32[]{:S(2)}) collective-permute-start(bf16[16,8,1024]{2,1,0:T(8,128)(2,1)S(1)} %get-tuple-element.27), channel_id=1, source_target_pairs={{0,96},{4,100},{8,104},{12,108},{16,112},{20,116},{24,120},{28,124... | collective-permute-start | bytes 786440 | tf_op jit(solution)/shard_map/ppermute | solution.py:618
